TPU v7x, 32 devices: a whole 2x2x4 slice. The times are simulated.
32 devices in a mesh: focus: 2 (over y), tx: 4 (over z), ty: 2 (over core), dose: 2 (over x).
Axes of the slice: x: 2, y: 2, z: 4, core: 2. Of those that a mesh axis runs over, the one named last changes fastest.
Arguments:
- aerial_image: float32 [64, 32, 256], P('focus', 'tx', 'ty'), parts along dimension 0, may hold values from 0.2 to 2
- quencher: float32 [32, 32, 256], P(None, 'tx', 'ty'), may hold values from 0.1 to 0.8
- cotangent: float32 [8, 32, 32, 256], P(('focus', 'dose'), None, 'tx', 'ty'), parts along dimension 0, may hold values from -6 to 6
- dose_levels: float32 [16], replicated, may hold values from 0.5 to 2
- dose_index: int32 [8], P(('focus', 'dose')), parts along dimension 0, may hold values from 0 to 15
Outputs:
- image_grad: float32 [64, 32, 256], P(('focus', 'dose'), 'tx', 'ty'), parts along dimension 0
There are 2 independent parts, one for each index of `focus`. A program takes and returns all parts, laid end to end along the dimension named above; an argument that names none is the same for every part. Nothing has to cross between parts.
All inputs are finite; a program needn't handle non-finite values.
Results may differ from a plain program's by a relative error of at most 0.00002.
Values sent between devices are 32-bit elements; how exact they have to be, the bound alone decides.
No kernel may reach another device: no remote copies, remote signals or barrier semaphores. Data moves between devices by JAX's collectives and lax.ppermute only.
A program may use at most 64 MiB of HBM per device.

v0:
```python
import jax
import jax.numpy as jnp
from jax import lax
from jax.sharding import PartitionSpec as P

STEPS = 4


exposure_rate = 1.0
neutral_rate = 0.8
deprotect_rate = 0.5
acid_lateral = 0.23
acid_depth = 0.02
base_lateral = 0.2
base_depth = 0.02


def with_halo(value, sides, width):
    for axis, dim in sides:
        devices, length = (lax.axis_size(axis), value.shape[dim])
        up = [(i, (i + 1) % devices) for i in range(devices)]
        down = [(j, i) for i, j in up]
        last = lax.slice_in_dim(value, length - width, length, axis=dim)
        leading = lax.slice_in_dim(value, 0, width, axis=dim)
        before = lax.ppermute(last, axis, up)
        after = lax.ppermute(leading, axis, down)
        value = jnp.concatenate([before, value, after], axis=dim)
    return value


def shrink(field):
    return field[..., 1:-1, 1:-1]


def diffuse(padded):
    center = shrink(padded)
    lateral = (
        padded[..., 2:, 1:-1]
        + padded[..., :-2, 1:-1]
        + padded[..., 1:-1, 2:]
        + padded[..., 1:-1, :-2]
        - 4.0 * center
    )
    upward = jnp.concatenate((center[..., 1:, :, :], center[..., -1:, :, :]), axis=-3)
    downward = jnp.concatenate((center[..., :1, :, :], center[..., :-1, :, :]), axis=-3)
    return (lateral, upward + downward - 2.0 * center)


def advance(padded, protect):
    center = shrink(padded)
    acid_now = center[:, 0]
    quench_now = center[:, 1]
    reaction = neutral_rate * acid_now * quench_now
    lateral, vertical = diffuse(padded)
    next_acid = acid_now + acid_lateral * lateral[:, 0] + acid_depth * vertical[:, 0] - reaction
    next_quench = quench_now + base_lateral * lateral[:, 1] + base_depth * vertical[:, 1] - reaction
    snapshot = jnp.concatenate((center, protect[:, None]), axis=1)
    next_protect = protect * (1.0 - deprotect_rate * acid_now)
    return (jnp.stack((next_acid, next_quench), axis=1), next_protect, snapshot)


def retreat(padded, adj_protect, snapshot):
    center = shrink(padded)
    adj_acid = center[:, 0]
    adj_quench = center[:, 1]
    acid_old = snapshot[:, 0]
    quench_old = snapshot[:, 1]
    protect_old = snapshot[:, 2]
    lateral, vertical = diffuse(padded)
    adj_sum = adj_acid + adj_quench
    next_acid = (
        adj_acid
        + acid_lateral * lateral[:, 0]
        + acid_depth * vertical[:, 0]
        - neutral_rate * quench_old * adj_sum
        - deprotect_rate * protect_old * adj_protect
    )
    next_quench = (
        adj_quench
        + base_lateral * lateral[:, 1]
        + base_depth * vertical[:, 1]
        - neutral_rate * acid_old * adj_sum
    )
    next_protect = adj_protect * (1.0 - deprotect_rate * acid_old)
    return (jnp.stack((next_acid, next_quench), axis=1), next_protect)


def on_device(aerial_image, quencher, cotangent, dose_levels, dose_index):
    levels = jnp.arange(dose_levels.shape[0], dtype=jnp.int32)
    choose_mask = (dose_index[:, None] == levels[None, :]).astype(jnp.float32)
    dose_value = jnp.sum(choose_mask * dose_levels[None, :], axis=1)
    dose_col = dose_value[:, None, None, None]
    absorbed = jnp.exp(-exposure_rate * dose_col * aerial_image[None])
    acid_now = 1.0 - absorbed
    quench_now = jnp.broadcast_to(quencher[None], acid_now.shape)
    fields = jnp.stack((acid_now, quench_now), axis=1)
    protect = jnp.ones_like(acid_now)
    history = []
    for bake_step in range(STEPS):
        padded = with_halo(fields, (("tx", 3), ("ty", 4)), 1)
        fields, protect, snapshot = advance(padded, protect)
        history.append(snapshot)
    adjoint = jnp.zeros_like(fields)
    adj_protect = cotangent
    for bake_step in reversed(range(STEPS)):
        padded = with_halo(adjoint, (("tx", 3), ("ty", 4)), 1)
        adjoint, adj_protect = retreat(padded, adj_protect, history[bake_step])
    partial_value = jnp.sum(adjoint[:, 0] * exposure_rate * dose_col * absorbed, axis=0)
    return lax.psum_scatter(partial_value, "dose", scatter_dimension=0, tiled=True)


def solution(mesh):
    placed = (
        P("focus", "tx", "ty"),
        P(None, "tx", "ty"),
        P(("focus", "dose"), None, "tx", "ty"),
        P(),
        P(("focus", "dose")),
    )
    return jax.shard_map(
        on_device,
        mesh=mesh,
        in_specs=placed,
        out_specs=P(("focus", "dose"), "tx", "ty"),
        check_vma=False,
    )
```

profile of v0, /device:TPU:0, one launch (start us, length us, event | category | flops | bytes accessed | tf_op | source)
XLA Modules:
  0.0 161.7 jit_solution(10039179641620063067)
XLA Ops:
  7.3 5.1 %collective-permute-start = (f32[2,2,32,1,128]{2,1,4,3,0:T(2,128)}, f32[2,2,32,1,128]{2,1,4,3,0:T(2,128)S(1)}, u32[]{:S(2)}, u32[]{:S(2)}) collective-permute-start(f32[2,2,32,1,128]{2,1,4,3,0:T(2,128)} %broadcast.202), channel_id=1, source_target_pairs={{4,0},{8,4},{12,8},{0,12},{5,1},{9,5},{13,9},{1,13},{6,2},{10,6},{... | collective-permute-start | bytes 196616 | tf_op jit(solution)/shard_map/ppermute | solution.py:26
  12.4 1.1 copy.411
  13.5 1.2 copy.412
  14.8 0.9 fusion.129
  16.0 0.8 fusion.118
  16.9 3.8 %collective-permute-start.4 = (f32[2,2,32,1,128]{2,4,3,0,1:T(8,128)}, f32[2,2,32,1,128]{2,4,3,0,1:T(8,128)}, u32[]{:S(2)}, u32[]{:S(2)}) collective-permute-start(f32[2,2,32,1,128]{2,4,3,0,1:T(8,128)} %get-tuple-element.69), channel_id=1, source_target_pairs={{4,0},{8,4},{12,8},{0,12},{5,1},{9,5},{13,9},{1,13},{6,2},{10,6},{... | collective-permute-start | bytes 196616 | tf_op jit(solution)/shard_map/ppermute | solution.py:26
  20.7 2.8 %fusion.29 = (f32[2,2,1,8,128]{2,4,3,0,1:T(8,128)}, f32[2,2,1,8,128]{2,4,3,0,1:T(8,128)}) fusion(f32[2,1,32,8,128]{2,4,3,0,1:T(8,128)S(1)} %exponential_subtract_fusion, f32[2,1,32,8,128]{2,4,3,0,1:T(8,128)S(1)} %stack_broadcast_in_dim.2), kind=kLoop, calls=%fused_computation.110 | loop fusion | flops 8192 | bytes 557056 | tf_op jit(solution)/shard_map/stack | solution.py:96
  23.5 2.8 %fusion.30 = (f32[2,2,31,8,128]{2,4,3,0,1:T(8,128)}, f32[2,2,31,8,128]{2,4,3,0,1:T(8,128)}) fusion(f32[2,1,32,8,128]{2,4,3,0,1:T(8,128)S(1)} %exponential_subtract_fusion, f32[2,1,32,8,128]{2,4,3,0,1:T(8,128)S(1)} %stack_broadcast_in_dim.2), kind=kLoop, calls=%fused_computation.111 | loop fusion | flops 253952 | bytes 1540096 | tf_op jit(solution)/shard_map/stack | solution.py:96
  26.3 1.0 copy.419
  27.3 1.3 copy.429
  28.6 4.6 %fusion.2 = f32[2,2,32,8,128]{2,4,3,0,1:T(8,128)S(1)} fusion(f32[2,1,32,8,128]{2,4,3,0,1:T(8,128)S(1)} %stack_broadcast_in_dim.2, f32[2,1,32,8,128]{2,4,3,0,1:T(8,128)S(1)} %exponential_subtract_fusion, f32[2,2,1,8,128]{2,4,3,0,1:T(8,128)} %get-tuple-element.65, f32[2,2,31,8,128]{2,4,3,0,1:T(8,128)} %get-tuple-element.67, ...), kind=kLoop, calls=%fused_computation.83 | loop fusion | flops 786432 | bytes 2097152 | tf_op jit(solution)/shard_map/sub | solution.py:46
  33.3 2.8 %collective-permute-done.5 = f32[2,2,32,1,128]{2,4,3,0,1:T(8,128)} collective-permute-done((f32[2,2,32,1,128]{2,4,3,0,1:T(8,128)}, f32[2,2,32,1,128]{2,4,3,0,1:T(8,128)}, u32[]{:S(2)}, u32[]{:S(2)}) %collective-permute-start.5) | collective-permute-done | bytes 65568 | tf_op jit(solution)/shard_map/ppermute | solution.py:25
  36.1 0.8 pad_maximum_fusion.105
  39.7 2.4 %fusion.3 = f32[2,2,32,8,128]{2,4,3,0,1:T(8,128)S(1)} fusion(f32[2,1,32,8,128]{2,4,3,0,1:T(8,128)S(1)} %stack_broadcast_in_dim.2, f32[2,1,32,8,128]{2,4,3,0,1:T(8,128)S(1)} %exponential_subtract_fusion, f32[2,2,32,10,1]{2,4,3,0,1:T(1,128)S(1)} %copy.417, f32[2,2,32,1,128]{2,4,3,0,1:T(8,128)} %collective-permute-done.4, ...), kind=kLoop, calls=%fused_computation.84 | loop fusion | flops 2359296 | bytes 1189888 | tf_op jit(solution)/shard_map/sub | solution.py:38
  42.9 0.8 fusion.25
  43.7 1.8 %collective-permute-start.8 = (f32[2,2,32,1,128]{2,4,3,0,1:T(8,128)S(1)}, f32[2,2,32,1,128]{2,4,3,0,1:T(8,128)S(1)}, u32[]{:S(2)}, u32[]{:S(2)}) collective-permute-start(f32[2,2,32,1,128]{2,4,3,0,1:T(8,128)S(1)} %get-tuple-element.63), channel_id=1, source_target_pairs={{4,0},{8,4},{12,8},{0,12},{5,1},{9,5},{13,9},{1,13},{6,2},{10,6},{... | collective-permute-start | bytes 196616 | tf_op jit(solution)/shard_map/ppermute | solution.py:26
  45.8 4.5 %fusion.6 = f32[2,2,32,8,128]{2,1,4,3,0:T(2,128)S(1)} fusion(f32[2,2,32,1,128]{2,1,4,3,0:T(2,128)S(1)} %collective-permute-done, f32[2,2,32,1,128]{2,1,4,3,0:T(2,128)} %collective-permute-done.1, f32[2,2,32,10,1]{2,1,4,3,0:T(2,128)S(1)} %collective-permute-done.3, f32[2,2,32,8,128]{2,1,4,3,0:T(2,128)S(1)} %broadcast_in_dim.2, ...), kind=kLoop, calls=%fused_computation.87 | loop fusion | flops 1179648 | bytes 1189888 | tf_op jit(solution)/shard_map/add | solution.py:38
  50.4 2.2 %slice_multiply_fusion.10 = (f32[2,1,32,8,128]{2,1,4,3,0:T(1,128)S(1)}, f32[2,1,32,8,128]{2,1,4,3,0:T(1,128)S(1)}) fusion(f32[2,1,32,8,128]{2,1,4,3,0:T(1,128)S(1)} %bitcast.187, f32[2,2,32,8,128]{2,1,4,3,0:T(2,128)S(1)} %fusion.6), kind=kLoop, calls=%fused_computation.274 | loop fusion | flops 65536 | bytes 1310720 | tf_op jit(solution)/shard_map/mul | solution.py:80
  53.4 4.5 %collective-permute-done.9 = f32[2,2,32,1,128]{2,4,3,0,1:T(8,128)S(1)} collective-permute-done((f32[2,2,32,1,128]{2,4,3,0,1:T(8,128)S(1)}, f32[2,2,32,1,128]{2,4,3,0,1:T(8,128)S(1)}, u32[]{:S(2)}, u32[]{:S(2)}) %collective-permute-start.9) | collective-permute-done | bytes 65568 | tf_op jit(solution)/shard_map/ppermute | solution.py:25
  58.6 1.1 fusion.50
  59.9 1.3 fusion.44
  62.7 2.4 %collective-permute-start.12 = (f32[2,2,32,1,128]{2,4,3,0,1:T(8,128)S(1)}, f32[2,2,32,1,128]{2,4,3,0,1:T(8,128)S(1)}, u32[]{:S(2)}, u32[]{:S(2)}) collective-permute-start(f32[2,2,32,1,128]{2,4,3,0,1:T(8,128)S(1)} %get-tuple-element.53), channel_id=1, source_target_pairs={{4,0},{8,4},{12,8},{0,12},{5,1},{9,5},{13,9},{1,13},{6,2},{10,6},{... | collective-permute-start | bytes 196616 | tf_op jit(solution)/shard_map/ppermute | solution.py:26
  65.0 0.8 fusion.22
  65.9 5.9 %collective-permute-done.12 = f32[2,2,32,1,128]{2,4,3,0,1:T(8,128)S(1)} collective-permute-done((f32[2,2,32,1,128]{2,4,3,0,1:T(8,128)S(1)}, f32[2,2,32,1,128]{2,4,3,0,1:T(8,128)S(1)}, u32[]{:S(2)}, u32[]{:S(2)}) %collective-permute-start.12) | collective-permute-done | bytes 65568 | tf_op jit(solution)/shard_map/ppermute | solution.py:26
  71.8 6.6 %collective-permute-done.13 = f32[2,2,32,1,128]{2,4,3,0,1:T(8,128)S(1)} collective-permute-done((f32[2,2,32,1,128]{2,4,3,0,1:T(8,128)S(1)}, f32[2,2,32,1,128]{2,4,3,0,1:T(8,128)S(1)}, u32[]{:S(2)}, u32[]{:S(2)}) %collective-permute-start.13) | collective-permute-done | bytes 65568 | tf_op jit(solution)/shard_map/ppermute | solution.py:25
  79.1 1.1 fusion.51
  80.4 1.3 fusion.40
  82.2 2.0 %fusion.104 = (f32[2,32,8,128]{1,3,2,0:T(8,128)S(1)}, f32[2,32,8,128]{1,3,2,0:T(8,128)S(1)}, f32[2,32,8,128]{1,3,2,0:T(8,128)S(1)}, f32[2,32,8,128]{1,3,2,0:T(8,128)S(1)}, f32[2,32,8,128]{1,3,2,0:T(8,128)S(1)}) fusion(f32[2,2,32,8,128]{2,4,3,0,1:T(8,128)S(1)} %fusion.51, f32[2,2,32,8,128]{2,4,3,0,1:T(8,128)S(1)} %fusion.40, ...), kind=kLoop, calls=%fused_computation.281 | loop fusion | flops 3080192 | bytes 4849800 | tf_op jit(solution)/shard_map/sub | solution.py:72
  84.2 0.8 fusion.17
  85.0 1.8 %collective-permute-start.16 = (f32[2,2,32,1,128]{2,4,3,0,1:T(8,128)S(1)}, f32[2,2,32,1,128]{2,4,3,0,1:T(8,128)S(1)}, u32[]{:S(2)}, u32[]{:S(2)}) collective-permute-start(f32[2,2,32,1,128]{2,4,3,0,1:T(8,128)S(1)} %get-tuple-element.45), channel_id=1, source_target_pairs={{4,0},{8,4},{12,8},{0,12},{5,1},{9,5},{13,9},{1,13},{6,2},{10,6},{... | collective-permute-start | bytes 196616 | tf_op jit(solution)/shard_map/ppermute | solution.py:26
  87.9 6.0 %collective-permute-done.16 = f32[2,2,32,1,128]{2,4,3,0,1:T(8,128)S(1)} collective-permute-done((f32[2,2,32,1,128]{2,4,3,0,1:T(8,128)S(1)}, f32[2,2,32,1,128]{2,4,3,0,1:T(8,128)S(1)}, u32[]{:S(2)}, u32[]{:S(2)}) %collective-permute-start.16) | collective-permute-done | bytes 65568 | tf_op jit(solution)/shard_map/ppermute | solution.py:26
  93.9 5.3 %collective-permute-done.17 = f32[2,2,32,1,128]{2,4,3,0,1:T(8,128)S(1)} collective-permute-done((f32[2,2,32,1,128]{2,4,3,0,1:T(8,128)S(1)}, f32[2,2,32,1,128]{2,4,3,0,1:T(8,128)S(1)}, u32[]{:S(2)}, u32[]{:S(2)}) %collective-permute-start.17) | collective-permute-done | bytes 65568 | tf_op jit(solution)/shard_map/ppermute | solution.py:25
  100.0 1.1 fusion.52
  101.2 1.3 fusion.36
  102.5 0.9 fusion.90
  103.5 1.1 fusion.96
  105.4 1.8 %collective-permute-start.20 = (f32[2,2,32,1,128]{2,4,3,0,1:T(8,128)S(1)}, f32[2,2,32,1,128]{2,4,3,0,1:T(8,128)S(1)}, u32[]{:S(2)}, u32[]{:S(2)}) collective-permute-start(f32[2,2,32,1,128]{2,4,3,0,1:T(8,128)S(1)} %get-tuple-element.39), channel_id=1, source_target_pairs={{4,0},{8,4},{12,8},{0,12},{5,1},{9,5},{13,9},{1,13},{6,2},{10,6},{... | collective-permute-start | bytes 196616 | tf_op jit(solution)/shard_map/ppermute | solution.py:26
  108.3 5.7 %collective-permute-done.20 = f32[2,2,32,1,128]{2,4,3,0,1:T(8,128)S(1)} collective-permute-done((f32[2,2,32,1,128]{2,4,3,0,1:T(8,128)S(1)}, f32[2,2,32,1,128]{2,4,3,0,1:T(8,128)S(1)}, u32[]{:S(2)}, u32[]{:S(2)}) %collective-permute-start.20) | collective-permute-done | bytes 65568 | tf_op jit(solution)/shard_map/ppermute | solution.py:26
  114.0 6.3 %collective-permute-done.21 = f32[2,2,32,1,128]{2,4,3,0,1:T(8,128)S(1)} collective-permute-done((f32[2,2,32,1,128]{2,4,3,0,1:T(8,128)S(1)}, f32[2,2,32,1,128]{2,4,3,0,1:T(8,128)S(1)}, u32[]{:S(2)}, u32[]{:S(2)}) %collective-permute-start.21) | collective-permute-done | bytes 65568 | tf_op jit(solution)/shard_map/ppermute | solution.py:25
  120.9 1.1 fusion.53
  122.2 1.3 fusion.32
  123.5 1.5 fusion.79
  125.1 1.7 %collective-permute-start.24 = (f32[2,2,32,1,128]{2,4,3,0,1:T(8,128)S(1)}, f32[2,2,32,1,128]{2,4,3,0,1:T(8,128)S(1)}, u32[]{:S(2)}, u32[]{:S(2)}) collective-permute-start(f32[2,2,32,1,128]{2,4,3,0,1:T(8,128)S(1)} %get-tuple-element.33), channel_id=1, source_target_pairs={{4,0},{8,4},{12,8},{0,12},{5,1},{9,5},{13,9},{1,13},{6,2},{10,6},{... | collective-permute-start | bytes 196616 | tf_op jit(solution)/shard_map/ppermute | solution.py:26
  128.0 5.6 %collective-permute-done.24 = f32[2,2,32,1,128]{2,4,3,0,1:T(8,128)S(1)} collective-permute-done((f32[2,2,32,1,128]{2,4,3,0,1:T(8,128)S(1)}, f32[2,2,32,1,128]{2,4,3,0,1:T(8,128)S(1)}, u32[]{:S(2)}, u32[]{:S(2)}) %collective-permute-start.24) | collective-permute-done | bytes 65568 | tf_op jit(solution)/shard_map/ppermute | solution.py:26
  133.6 6.6 %collective-permute-done.25 = f32[2,2,32,1,128]{2,4,3,0,1:T(8,128)S(1)} collective-permute-done((f32[2,2,32,1,128]{2,4,3,0,1:T(8,128)S(1)}, f32[2,2,32,1,128]{2,4,3,0,1:T(8,128)S(1)}, u32[]{:S(2)}, u32[]{:S(2)}) %collective-permute-start.25) | collective-permute-done | bytes 65568 | tf_op jit(solution)/shard_map/ppermute | solution.py:25
  141.8 2.3 %fusion.115 = f32[32,8,128]{0,2,1:T(8,128)S(1)} fusion(f32[2,32,8,128]{1,3,2,0:T(8,128)S(1)} %get-tuple-element.13, f32[2,32,8,128]{1,3,2,0:T(8,128)S(1)} %get-tuple-element.12, f32[2,1,32,8,128]{2,4,3,0,1:T(8,128)S(1)} %bitcast.177, f32[2,1,32,8,128]{2,4,3,0,1:T(8,128)S(1)} %bitcast.182, f32[2,2,31,8,128]{2,4,3,0,1:T(8,128)S(1)} %get-tuple-element.35, ...), kind=kLoop, calls=%fused_computation.325 | loop fusion | flops 2981888 | bytes 3680272 | tf_op jit(solution)/shard_map/reduce_sum | solution.py:108
  144.1 0.8 copy.445
  144.9 9.9 %reduce-scatter.2.cloned.1.call-done = f32[16,8,128]{2,1,0:T(8,128)} async-done(((f32[32,8,128]{2,1,0:T(8,128)}), f32[16,8,128]{2,1,0:T(8,128)}) %reduce-scatter.2.cloned.1.call-update) | async-done | bytes 65552 | tf_op jit(solution)/shard_map/reduce_scatter | solution.py:109
  (107 shorter events, 16.5 us)
Async XLA Ops:
  6.5 148.3 %reduce-scatter.2.cloned.1.call-start = ((), (), s32[]{:S(2)}) async-start(), calls=%async_computation.1 | async-start | bytes 196608 | tf_op jit(solution)/shard_map/reduce_scatter | solution.py:109
  7.3 30.2 %collective-permute-start = (f32[2,2,32,1,128]{2,1,4,3,0:T(2,128)}, f32[2,2,32,1,128]{2,1,4,3,0:T(2,128)S(1)}, u32[]{:S(2)}, u32[]{:S(2)}) collective-permute-start(f32[2,2,32,1,128]{2,1,4,3,0:T(2,128)} %broadcast.202), channel_id=1, source_target_pairs={{4,0},{8,4},{12,8},{0,12},{5,1},{9,5},{13,9},{1,13},{6,2},{10,6},{... | collective-permute-start | bytes 196616 | tf_op jit(solution)/shard_map/ppermute | solution.py:26
  12.4 25.2 %collective-permute-start.1 = (f32[2,2,32,1,128]{2,1,4,3,0:T(2,128)}, f32[2,2,32,1,128]{2,1,4,3,0:T(2,128)}, u32[]{:S(2)}, u32[]{:S(2)}) collective-permute-start(f32[2,2,32,1,128]{2,1,4,3,0:T(2,128)} %broadcast.202), channel_id=1, source_target_pairs={{0,4},{4,8},{8,12},{12,0},{1,5},{5,9},{9,13},{13,1},{2,6},{6,10},{... | collective-permute-start | bytes 196616 | tf_op jit(solution)/shard_map/ppermute | solution.py:25
  13.5 3.4 %copy-start.3 = (f32[32,8,128]{0,2,1:T(8,128)}, f32[32,8,128]{0,2,1:T(8,128)S(1)}, u32[]{:S(2)}) copy-start(f32[32,8,128]{0,2,1:T(8,128)S(1)} %copy.411) | copy-start | bytes 393220
  14.8 0.9 copy-start
  16.9 16.4 %collective-permute-start.4 = (f32[2,2,32,1,128]{2,4,3,0,1:T(8,128)}, f32[2,2,32,1,128]{2,4,3,0,1:T(8,128)}, u32[]{:S(2)}, u32[]{:S(2)}) collective-permute-start(f32[2,2,32,1,128]{2,4,3,0,1:T(8,128)} %get-tuple-element.69), channel_id=1, source_target_pairs={{4,0},{8,4},{12,8},{0,12},{5,1},{9,5},{13,9},{1,13},{6,2},{10,6},{... | collective-permute-start | bytes 196616 | tf_op jit(solution)/shard_map/ppermute | solution.py:26
  20.7 15.4 %collective-permute-start.5 = (f32[2,2,32,1,128]{2,4,3,0,1:T(8,128)}, f32[2,2,32,1,128]{2,4,3,0,1:T(8,128)}, u32[]{:S(2)}, u32[]{:S(2)}) collective-permute-start(f32[2,2,32,1,128]{2,4,3,0,1:T(8,128)} %get-tuple-element.68), channel_id=1, source_target_pairs={{0,4},{4,8},{8,12},{12,0},{1,5},{5,9},{9,13},{13,1},{2,6},{6,10},{... | collective-permute-start | bytes 196616 | tf_op jit(solution)/shard_map/ppermute | solution.py:25
  23.5 2.8 %copy-start.5 = (f32[32,8,128]{2,1,0:T(8,128)S(1)}, f32[32,8,128]{2,1,0:T(8,128)}, u32[]{:S(2)}) copy-start(f32[32,8,128]{2,1,0:T(8,128)} %param.6) | copy-start | bytes 393220
  36.9 2.7 %collective-permute-start.7 = (f32[2,2,32,10,1]{2,1,4,3,0:T(2,128)S(1)}, f32[2,2,32,10,1]{2,1,4,3,0:T(2,128)S(1)}, u32[]{:S(2)}, u32[]{:S(2)}) collective-permute-start(f32[2,2,32,10,1]{2,1,4,3,0:T(2,128)S(1)} %copy.416), channel_id=1, source_target_pairs={{0,2},{2,0},{1,3},{3,1},{4,6},{6,4},{5,7},{7,5},{8,10},{10,8},{9,1... | collective-permute-start | bytes 15368 | tf_op jit(solution)/shard_map/ppermute | solution.py:25
  37.0 2.7 %collective-permute-start.6 = (f32[2,2,32,10,1]{2,1,4,3,0:T(2,128)S(1)}, f32[2,2,32,10,1]{2,1,4,3,0:T(2,128)S(1)}, u32[]{:S(2)}, u32[]{:S(2)}) collective-permute-start(f32[2,2,32,10,1]{2,1,4,3,0:T(2,128)S(1)} %copy.414), channel_id=1, source_target_pairs={{2,0},{0,2},{3,1},{1,3},{6,4},{4,6},{7,5},{5,7},{10,8},{8,10},{11,... | collective-permute-start | bytes 15368 | tf_op jit(solution)/shard_map/ppermute | solution.py:26
  39.1 6.8 %collective-permute-start.3 = (f32[2,2,32,10,1]{2,1,4,3,0:T(2,128)S(1)}, f32[2,2,32,10,1]{2,1,4,3,0:T(2,128)S(1)}, u32[]{:S(2)}, u32[]{:S(2)}) collective-permute-start(f32[2,2,32,10,1]{2,1,4,3,0:T(2,128)S(1)} %get-tuple-element.25), channel_id=1, source_target_pairs={{0,2},{2,0},{1,3},{3,1},{4,6},{6,4},{5,7},{7,5},{8,10},{10,8},{9,1... | collective-permute-start | bytes 15368 | tf_op jit(solution)/shard_map/ppermute | solution.py:25
  39.2 6.7 %collective-permute-start.2 = (f32[2,2,32,10,1]{2,1,4,3,0:T(2,128)S(1)}, f32[2,2,32,10,1]{2,1,4,3,0:T(2,128)S(1)}, u32[]{:S(2)}, u32[]{:S(2)}) collective-permute-start(f32[2,2,32,10,1]{2,1,4,3,0:T(2,128)S(1)} %get-tuple-element.24), channel_id=1, source_target_pairs={{2,0},{0,2},{3,1},{1,3},{6,4},{4,6},{7,5},{5,7},{10,8},{8,10},{11,... | collective-permute-start | bytes 15368 | tf_op jit(solution)/shard_map/ppermute | solution.py:26
  39.7 2.5 %copy-start.1 = (f32[32,8,128]{0,2,1:T(8,128)S(1)}, f32[32,8,128]{0,2,1:T(8,128)}, u32[]{:S(2)}) copy-start(f32[32,8,128]{0,2,1:T(8,128)} %copy-done) | copy-start | bytes 393220
  39.7 2.5 %copy-start.2 = (f32[32,8,128]{0,2,1:T(8,128)S(1)}, f32[32,8,128]{0,2,1:T(8,128)}, u32[]{:S(2)}) copy-start(f32[32,8,128]{0,2,1:T(8,128)} %copy.419) | copy-start | bytes 393220
  39.7 2.5 %copy-start.4 = (f32[32,8,128]{0,2,1:T(8,128)S(1)}, f32[32,8,128]{0,2,1:T(8,128)}, u32[]{:S(2)}) copy-start(f32[32,8,128]{0,2,1:T(8,128)} %copy-done.3) | copy-start | bytes 393220
  43.7 9.7 %collective-permute-start.8 = (f32[2,2,32,1,128]{2,4,3,0,1:T(8,128)S(1)}, f32[2,2,32,1,128]{2,4,3,0,1:T(8,128)S(1)}, u32[]{:S(2)}, u32[]{:S(2)}) collective-permute-start(f32[2,2,32,1,128]{2,4,3,0,1:T(8,128)S(1)} %get-tuple-element.63), channel_id=1, source_target_pairs={{4,0},{8,4},{12,8},{0,12},{5,1},{9,5},{13,9},{1,13},{6,2},{10,6},{... | collective-permute-start | bytes 196616 | tf_op jit(solution)/shard_map/ppermute | solution.py:26
  45.5 12.4 %collective-permute-start.9 = (f32[2,2,32,1,128]{2,4,3,0,1:T(8,128)S(1)}, f32[2,2,32,1,128]{2,4,3,0,1:T(8,128)S(1)}, u32[]{:S(2)}, u32[]{:S(2)}) collective-permute-start(f32[2,2,32,1,128]{2,4,3,0,1:T(8,128)S(1)} %get-tuple-element.62), channel_id=1, source_target_pairs={{0,4},{4,8},{8,12},{12,0},{1,5},{5,9},{9,13},{13,1},{2,6},{6,10},{... | collective-permute-start | bytes 196616 | tf_op jit(solution)/shard_map/ppermute | solution.py:25
  58.0 1.8 %collective-permute-start.11 = (f32[2,2,32,10,1]{2,1,4,3,0:T(2,128)S(1)}, f32[2,2,32,10,1]{2,1,4,3,0:T(2,128)S(1)}, u32[]{:S(2)}, u32[]{:S(2)}) collective-permute-start(f32[2,2,32,10,1]{2,1,4,3,0:T(2,128)S(1)} %copy.423), channel_id=1, source_target_pairs={{0,2},{2,0},{1,3},{3,1},{4,6},{6,4},{5,7},{7,5},{8,10},{10,8},{9,1... | collective-permute-start | bytes 15368 | tf_op jit(solution)/shard_map/ppermute | solution.py:25
  58.1 1.8 %collective-permute-start.10 = (f32[2,2,32,10,1]{2,1,4,3,0:T(2,128)S(1)}, f32[2,2,32,10,1]{2,1,4,3,0:T(2,128)S(1)}, u32[]{:S(2)}, u32[]{:S(2)}) collective-permute-start(f32[2,2,32,10,1]{2,1,4,3,0:T(2,128)S(1)} %copy.421), channel_id=1, source_target_pairs={{2,0},{0,2},{3,1},{1,3},{6,4},{4,6},{7,5},{5,7},{10,8},{8,10},{11,... | collective-permute-start | bytes 15368 | tf_op jit(solution)/shard_map/ppermute | solution.py:26
  62.7 9.1 %collective-permute-start.12 = (f32[2,2,32,1,128]{2,4,3,0,1:T(8,128)S(1)}, f32[2,2,32,1,128]{2,4,3,0,1:T(8,128)S(1)}, u32[]{:S(2)}, u32[]{:S(2)}) collective-permute-start(f32[2,2,32,1,128]{2,4,3,0,1:T(8,128)S(1)} %get-tuple-element.53), channel_id=1, source_target_pairs={{4,0},{8,4},{12,8},{0,12},{5,1},{9,5},{13,9},{1,13},{6,2},{10,6},{... | collective-permute-start | bytes 196616 | tf_op jit(solution)/shard_map/ppermute | solution.py:26
  65.0 13.4 %collective-permute-start.13 = (f32[2,2,32,1,128]{2,4,3,0,1:T(8,128)S(1)}, f32[2,2,32,1,128]{2,4,3,0,1:T(8,128)S(1)}, u32[]{:S(2)}, u32[]{:S(2)}) collective-permute-start(f32[2,2,32,1,128]{2,4,3,0,1:T(8,128)S(1)} %get-tuple-element.52), channel_id=1, source_target_pairs={{0,4},{4,8},{8,12},{12,0},{1,5},{5,9},{9,13},{13,1},{2,6},{6,10},{... | collective-permute-start | bytes 196616 | tf_op jit(solution)/shard_map/ppermute | solution.py:25
  78.5 1.8 %collective-permute-start.15 = (f32[2,2,32,10,1]{2,1,4,3,0:T(2,128)S(1)}, f32[2,2,32,10,1]{2,1,4,3,0:T(2,128)S(1)}, u32[]{:S(2)}, u32[]{:S(2)}) collective-permute-start(f32[2,2,32,10,1]{2,1,4,3,0:T(2,128)S(1)} %copy.427), channel_id=1, source_target_pairs={{0,2},{2,0},{1,3},{3,1},{4,6},{6,4},{5,7},{7,5},{8,10},{10,8},{9,1... | collective-permute-start | bytes 15368 | tf_op jit(solution)/shard_map/ppermute | solution.py:25
  78.6 1.8 %collective-permute-start.14 = (f32[2,2,32,10,1]{2,1,4,3,0:T(2,128)S(1)}, f32[2,2,32,10,1]{2,1,4,3,0:T(2,128)S(1)}, u32[]{:S(2)}, u32[]{:S(2)}) collective-permute-start(f32[2,2,32,10,1]{2,1,4,3,0:T(2,128)S(1)} %copy.425), channel_id=1, source_target_pairs={{2,0},{0,2},{3,1},{1,3},{6,4},{4,6},{7,5},{5,7},{10,8},{8,10},{11,... | collective-permute-start | bytes 15368 | tf_op jit(solution)/shard_map/ppermute | solution.py:26
  85.0 8.9 %collective-permute-start.16 = (f32[2,2,32,1,128]{2,4,3,0,1:T(8,128)S(1)}, f32[2,2,32,1,128]{2,4,3,0,1:T(8,128)S(1)}, u32[]{:S(2)}, u32[]{:S(2)}) collective-permute-start(f32[2,2,32,1,128]{2,4,3,0,1:T(8,128)S(1)} %get-tuple-element.45), channel_id=1, source_target_pairs={{4,0},{8,4},{12,8},{0,12},{5,1},{9,5},{13,9},{1,13},{6,2},{10,6},{... | collective-permute-start | bytes 196616 | tf_op jit(solution)/shard_map/ppermute | solution.py:26
  86.8 12.4 %collective-permute-start.17 = (f32[2,2,32,1,128]{2,4,3,0,1:T(8,128)S(1)}, f32[2,2,32,1,128]{2,4,3,0,1:T(8,128)S(1)}, u32[]{:S(2)}, u32[]{:S(2)}) collective-permute-start(f32[2,2,32,1,128]{2,4,3,0,1:T(8,128)S(1)} %get-tuple-element.44), channel_id=1, source_target_pairs={{0,4},{4,8},{8,12},{12,0},{1,5},{5,9},{9,13},{13,1},{2,6},{6,10},{... | collective-permute-start | bytes 196616 | tf_op jit(solution)/shard_map/ppermute | solution.py:25
  99.3 1.8 %collective-permute-start.19 = (f32[2,2,32,10,1]{2,1,4,3,0:T(2,128)S(1)}, f32[2,2,32,10,1]{2,1,4,3,0:T(2,128)S(1)}, u32[]{:S(2)}, u32[]{:S(2)}) collective-permute-start(f32[2,2,32,10,1]{2,1,4,3,0:T(2,128)S(1)} %copy.434), channel_id=1, source_target_pairs={{0,2},{2,0},{1,3},{3,1},{4,6},{6,4},{5,7},{7,5},{8,10},{10,8},{9,1... | collective-permute-start | bytes 15368 | tf_op jit(solution)/shard_map/ppermute | solution.py:25
  99.4 1.8 %collective-permute-start.18 = (f32[2,2,32,10,1]{2,1,4,3,0:T(2,128)S(1)}, f32[2,2,32,10,1]{2,1,4,3,0:T(2,128)S(1)}, u32[]{:S(2)}, u32[]{:S(2)}) collective-permute-start(f32[2,2,32,10,1]{2,1,4,3,0:T(2,128)S(1)} %copy.432), channel_id=1, source_target_pairs={{2,0},{0,2},{3,1},{1,3},{6,4},{4,6},{7,5},{5,7},{10,8},{8,10},{11,... | collective-permute-start | bytes 15368 | tf_op jit(solution)/shard_map/ppermute | solution.py:26
  105.4 8.5 %collective-permute-start.20 = (f32[2,2,32,1,128]{2,4,3,0,1:T(8,128)S(1)}, f32[2,2,32,1,128]{2,4,3,0,1:T(8,128)S(1)}, u32[]{:S(2)}, u32[]{:S(2)}) collective-permute-start(f32[2,2,32,1,128]{2,4,3,0,1:T(8,128)S(1)} %get-tuple-element.39), channel_id=1, source_target_pairs={{4,0},{8,4},{12,8},{0,12},{5,1},{9,5},{13,9},{1,13},{6,2},{10,6},{... | collective-permute-start | bytes 196616 | tf_op jit(solution)/shard_map/ppermute | solution.py:26
  107.2 13.0 %collective-permute-start.21 = (f32[2,2,32,1,128]{2,4,3,0,1:T(8,128)S(1)}, f32[2,2,32,1,128]{2,4,3,0,1:T(8,128)S(1)}, u32[]{:S(2)}, u32[]{:S(2)}) collective-permute-start(f32[2,2,32,1,128]{2,4,3,0,1:T(8,128)S(1)} %get-tuple-element.38), channel_id=1, source_target_pairs={{0,4},{4,8},{8,12},{12,0},{1,5},{5,9},{9,13},{13,1},{2,6},{6,10},{... | collective-permute-start | bytes 196616 | tf_op jit(solution)/shard_map/ppermute | solution.py:25
  120.3 1.8 %collective-permute-start.23 = (f32[2,2,32,10,1]{2,1,4,3,0:T(2,128)S(1)}, f32[2,2,32,10,1]{2,1,4,3,0:T(2,128)S(1)}, u32[]{:S(2)}, u32[]{:S(2)}) collective-permute-start(f32[2,2,32,10,1]{2,1,4,3,0:T(2,128)S(1)} %copy.439), channel_id=1, source_target_pairs={{0,2},{2,0},{1,3},{3,1},{4,6},{6,4},{5,7},{7,5},{8,10},{10,8},{9,1... | collective-permute-start | bytes 15368 | tf_op jit(solution)/shard_map/ppermute | solution.py:25
  120.4 1.8 %collective-permute-start.22 = (f32[2,2,32,10,1]{2,1,4,3,0:T(2,128)S(1)}, f32[2,2,32,10,1]{2,1,4,3,0:T(2,128)S(1)}, u32[]{:S(2)}, u32[]{:S(2)}) collective-permute-start(f32[2,2,32,10,1]{2,1,4,3,0:T(2,128)S(1)} %copy.437), channel_id=1, source_target_pairs={{2,0},{0,2},{3,1},{1,3},{6,4},{4,6},{7,5},{5,7},{10,8},{8,10},{11,... | collective-permute-start | bytes 15368 | tf_op jit(solution)/shard_map/ppermute | solution.py:26
  125.1 8.5 %collective-permute-start.24 = (f32[2,2,32,1,128]{2,4,3,0,1:T(8,128)S(1)}, f32[2,2,32,1,128]{2,4,3,0,1:T(8,128)S(1)}, u32[]{:S(2)}, u32[]{:S(2)}) collective-permute-start(f32[2,2,32,1,128]{2,4,3,0,1:T(8,128)S(1)} %get-tuple-element.33), channel_id=1, source_target_pairs={{4,0},{8,4},{12,8},{0,12},{5,1},{9,5},{13,9},{1,13},{6,2},{10,6},{... | collective-permute-start | bytes 196616 | tf_op jit(solution)/shard_map/ppermute | solution.py:26
  126.8 13.4 %collective-permute-start.25 = (f32[2,2,32,1,128]{2,4,3,0,1:T(8,128)S(1)}, f32[2,2,32,1,128]{2,4,3,0,1:T(8,128)S(1)}, u32[]{:S(2)}, u32[]{:S(2)}) collective-permute-start(f32[2,2,32,1,128]{2,4,3,0,1:T(8,128)S(1)} %get-tuple-element.32), channel_id=1, source_target_pairs={{0,4},{4,8},{8,12},{12,0},{1,5},{5,9},{9,13},{13,1},{2,6},{6,10},{... | collective-permute-start | bytes 196616 | tf_op jit(solution)/shard_map/ppermute | solution.py:25
  140.2 1.5 collective-permute-start.27
  140.3 1.4 collective-permute-start.26
Sparse Core Ops, SparseCore 0:
  145.1 9.7 reduce-scatter.1
where the time goes:
time: 162 us
  waiting for transfers between devices  65.3 us (40%)
  other arithmetic  50.6 us (31%)
  starting transfers between devices  23.9 us (15%)
  between operations  14.2 us (9%)
  local copies, waits for them, and re-layouts  7.72 us (5%)
    ppermute x14, waiting for transfers between devices, with_halo(): before = lax.ppermute(last, axis, up)  32.2 us
    ppermute x14, waiting for transfers between devices, with_halo(): after = lax.ppermute(leading, axis, down)  23.2 us
    ppermute x14, starting transfers between devices, with_halo(): after = lax.ppermute(leading, axis, down)  22.1 us
    reduce_scatter x1, waiting for transfers between devices, on_device(): lax.psum_scatter(partial_value, 'dose', scatter_dimension=0, tiled=True)  9.9 us
    sub x5, other arithmetic, diffuse(): return (lateral, upward + downward - 2.0 * center)  9.21 us
    sub x5, other arithmetic, diffuse(): padded[..., 2:, 1:-1] + padded[..., :-2, 1:-1] + padded[..., 1:-1, 2:]  7.74 us
    another operation x3, other arithmetic, on_device(): fields = jnp.stack((acid_now, quench_now), axis=1)  6.37 us
    another operation x9, other arithmetic, retreat(): return (jnp.stack((next_acid, next_quench), axis=1), next_protect)  4.88 us
  transfers between devices with their start and end apart: 29, of which 11 were waited for; matrix products, arithmetic and copies ran while one was open for 24% of the time, Pallas kernels for 0%

commit v1 on v0

v1 whole, which is shorter than its diff:
```python
import jax
import jax.numpy as jnp
from jax import lax
from jax.experimental import pallas as pl
from jax.experimental.pallas import tpu as pltpu
from jax.sharding import PartitionSpec as P

exposure_rate = 1.0
neutral_rate = 0.8
deprotect_rate = 0.5
acid_lateral = 0.23
acid_depth = 0.02
base_lateral = 0.2
base_depth = 0.02

HALO_AERIAL = 5
HALO_QUENCH = 4
HALO_COT = 3
HALO_ROWS = HALO_AERIAL + HALO_QUENCH + 2 * HALO_COT

SUB = 8


def pack_kernel(rows, depth, aerial, quench, cot, up, down, swap):
    core = lax.axis_index("ty")
    groups = depth // SUB
    area = depth * rows

    def put(dst, place, src, base, row):
        for k in range(groups):
            dst[place, k] = src[pl.ds(base + rows * k + row, SUB, stride=rows * groups), :]

    mine = core * area
    other = (1 - core) * area
    for dst, first in ((up, lambda width: rows - width), (down, lambda width: 0)):
        place = 0
        for src, base, width in (
            (cot, mine, HALO_COT),
            (aerial, 0, HALO_AERIAL),
            (quench, 0, HALO_QUENCH),
            (cot, other, HALO_COT),
        ):
            for i in range(width):
                put(dst, place, src, base, first(width) + i)
                place += 1
    for j, (src, base) in enumerate(((aerial, 0), (quench, 0), (cot, other))):
        for row in range(rows):
            put(swap, j * rows + row, src, base, row)


def main_kernel(rows, depth, doses, *refs):
    (levels, index, aerial, quench, cot, swap, before_own, after_own, before_par, after_par) = refs[:10]
    outs = refs[10 : 10 + 2 * doses]
    a0, q0, a1, q1, a2, q2, a3, ct, l3, l2, m2, l1, m1, full = refs[10 + 2 * doses :]
    core = lax.axis_index("ty")
    place = lax.axis_index("dose")
    groups = depth // SUB
    area = depth * rows
    count = 2 * groups
    lane = lax.broadcasted_iota(jnp.int32, (SUB, 128), 1)
    first_lane = lane == 0
    last_lane = lane == 127
    sub = lax.broadcasted_iota(jnp.int32, (SUB, 128), 0)
    first_sub = sub == 0
    last_sub = sub == SUB - 1
    dose = levels[index[core]]

    def source(raw, base, swap_at, halo_at_own, halo_at_par, width, row):
        if row < 0:
            own = [before_own[halo_at_own + width + row, k] for k in range(groups)]
            par = [before_par[halo_at_par + width + row, k] for k in range(groups)]
        elif row >= rows:
            own = [after_own[halo_at_own + row - rows, k] for k in range(groups)]
            par = [after_par[halo_at_par + row - rows, k] for k in range(groups)]
        else:
            own = [raw[pl.ds(base + rows * k + row, SUB, stride=rows * groups), :] for k in range(groups)]
            par = [swap[swap_at + row, k] for k in range(groups)]
        return own + par

    def load(ref, halo, row):
        return [ref[row + halo, i] for i in range(count)]

    def save(ref, halo, row, value):
        for i in range(count):
            ref[row + halo, i] = value[i]

    def sums(ref, halo, row, center):
        above = load(ref, halo, row - 1)
        below = load(ref, halo, row + 1)
        lateral, vertical = [], []
        for i in range(count):
            k = i % groups
            j = (i + groups) % count
            right = pltpu.roll(jnp.where(first_lane, center[j], center[i]), 127, 1)
            left = pltpu.roll(jnp.where(last_lane, center[j], center[i]), 1, 1)
            lateral.append((above[i] + below[i]) + (right + left))
            if k + 1 < groups:
                deeper = center[i + 1]
            else:
                deeper = jnp.where(last_sub, center[i], pltpu.roll(center[i - k], SUB - 1, 0))
            if k > 0:
                higher = center[i - 1]
            else:
                higher = jnp.where(first_sub, center[i], pltpu.roll(center[i + groups - 1], 1, 0))
            vertical.append(deeper + higher)
        return lateral, vertical

    def spread(ref, halo, row, center, along, depthwise):
        lateral, vertical = sums(ref, halo, row, center)
        keep = 1.0 - 4.0 * along - 2.0 * depthwise
        return [keep * c + along * s + depthwise * v for c, s, v in zip(center, lateral, vertical)]

    def left_over(value):
        return [1.0 - deprotect_rate * v for v in value]

    for row in range(-HALO_AERIAL, rows + HALO_AERIAL):
        light = source(aerial, 0, 0, HALO_COT, HALO_COT, HALO_AERIAL, row)
        save(a0, HALO_AERIAL, row, [1.0 - jnp.exp((-exposure_rate * dose) * v) for v in light])
    for row in range(-HALO_QUENCH, rows + HALO_QUENCH):
        at = HALO_COT + HALO_AERIAL
        save(q0, HALO_QUENCH, row, source(quench, 0, rows, at, at, HALO_QUENCH, row))
    for row in range(-HALO_COT, rows + HALO_COT):
        at = HALO_COT + HALO_AERIAL + HALO_QUENCH
        save(ct, HALO_COT, row, source(cot, core * area, 2 * rows, 0, at, HALO_COT, row))

    def forward(a_old, a_halo, q_old, q_halo, a_new, q_new):
        for row in range(1 - a_halo, rows + a_halo - 1):
            a_now = load(a_old, a_halo, row)
            q_now = load(q_old, q_halo, row)
            reaction = [neutral_rate * a * q for a, q in zip(a_now, q_now)]
            a_next = spread(a_old, a_halo, row, a_now, acid_lateral, acid_depth)
            save(a_new, a_halo - 1, row, [v - r for v, r in zip(a_next, reaction)])
            if q_new is not None and 1 - q_halo <= row < rows + q_halo - 1:
                q_next = spread(q_old, q_halo, row, q_now, base_lateral, base_depth)
                save(q_new, q_halo - 1, row, [v - r for v, r in zip(q_next, reaction)])

    forward(a0, 5, q0, 4, a1, q1)
    forward(a1, 4, q1, 3, a2, q2)
    forward(a2, 3, q2, 2, a3, None)

    def source_term(row, ones):
        value = [(-deprotect_rate) * v for v in load(ct, 3, row)]
        for ref, halo in ones:
            value = [v * m for v, m in zip(value, left_over(load(ref, halo, row)))]
        return value

    for row in range(-3, rows + 3):
        save(l3, 3, row, source_term(row, ((a0, 5), (a1, 4), (a2, 3))))
    for row in range(-2, rows + 2):
        l_old = load(l3, 3, row)
        term = source_term(row, ((a0, 5), (a1, 4), (a3, 2)))
        q_old = load(q2, 2, row)
        l_next = spread(l3, 3, row, l_old, acid_lateral, acid_depth)
        save(l2, 2, row, [v - neutral_rate * q * s + t for v, q, s, t in zip(l_next, q_old, l_old, term)])
        if -1 <= row < rows + 1:
            save(m2, 1, row, [-neutral_rate * a * s for a, s in zip(load(a2, 3, row), l_old)])
    for row in range(-1, rows + 1):
        l_old = load(l2, 2, row)
        m_old = load(m2, 1, row)
        both = [neutral_rate * (a + b) for a, b in zip(l_old, m_old)]
        term = source_term(row, ((a0, 5), (a2, 3), (a3, 2)))
        l_next = spread(l2, 2, row, l_old, acid_lateral, acid_depth)
        save(l1, 1, row, [v - q * s + t for v, q, s, t in zip(l_next, load(q1, 3, row), both, term)])
        if 0 <= row < rows:
            m_next = spread(m2, 1, row, m_old, base_lateral, base_depth)
            save(m1, 0, row, [v - a * s for v, a, s in zip(m_next, load(a1, 4, row), both)])
    for row in range(rows):
        l_old = load(l1, 1, row)
        both = [neutral_rate * (a + b) for a, b in zip(l_old, load(m1, 0, row))]
        term = source_term(row, ((a1, 4), (a2, 3), (a3, 2)))
        l_next = spread(l1, 1, row, l_old, acid_lateral, acid_depth)
        absorbed = [1.0 - a for a in load(a0, 5, row)]
        for i in range(count):
            value = l_next[i] - load(q0, 4, row)[i] * both[i] + term[i]
            value = value * ((exposure_rate * dose) * absorbed[i])
            half, k = divmod(i, groups)
            full[pl.ds(half * area + rows * k + row, SUB, stride=rows * groups), :] = value

    piece = area // doses
    for half in range(2):
        for k in range(doses):
            owner = lax.rem(place + k, doses)
            start = pl.multiple_of(half * area + owner * piece, SUB)
            outs[half * doses + k][...] = full[pl.ds(start, piece), :]


def on_device(aerial_image, quencher, cotangent, dose_levels, dose_index):
    depth, rows, lanes = aerial_image.shape
    groups = depth // SUB
    doses = lax.axis_size("dose")
    ring = lax.axis_size("tx")
    f32 = jnp.float32
    aerial = aerial_image.reshape(depth * rows, lanes)
    quench = quencher.reshape(depth * rows, lanes)
    cot = cotangent.reshape(2 * depth * rows, lanes)
    vmem = pl.BlockSpec(memory_space=pltpu.VMEM)
    smem = pl.BlockSpec(memory_space=pltpu.SMEM)

    def kernel_pack(*refs):
        pack_kernel(rows, depth, *refs)

    def field(n, parts=1):
        return jax.ShapeDtypeStruct((n, groups * parts, SUB, lanes), f32)

    up, down, swap = pl.pallas_call(
        kernel_pack,
        out_shape=(field(HALO_ROWS), field(HALO_ROWS), field(3 * rows)),
        in_specs=[vmem] * 3,
        out_specs=(vmem,) * 3,
    )(aerial, quench, cot)

    ahead = [(i, (i + 1) % ring) for i in range(ring)]
    back = [(j, i) for i, j in ahead]
    across = [(0, 1), (1, 0)]
    before_own = lax.ppermute(up, "tx", ahead)
    after_own = lax.ppermute(down, "tx", back)
    swapped = lax.ppermute(swap, "ty", across)
    before_par = lax.ppermute(before_own, "ty", across)
    after_par = lax.ppermute(after_own, "ty", across)

    def kernel_main(*refs):
        main_kernel(rows, depth, doses, *refs)

    def scratch(halo):
        return pltpu.VMEM((rows + 2 * halo, 2 * groups, SUB, lanes), f32)

    piece = depth * rows // doses
    parts = pl.pallas_call(
        kernel_main,
        out_shape=(jax.ShapeDtypeStruct((piece, lanes), f32),) * (2 * doses),
        in_specs=[smem] * 2 + [vmem] * 8,
        out_specs=(vmem,) * (2 * doses),
        scratch_shapes=[scratch(h) for h in (5, 4, 4, 3, 3, 2, 2, 3, 3, 2, 1, 1, 0)]
        + [pltpu.VMEM((2 * depth * rows, lanes), f32)],
    )(dose_levels, dose_index, aerial, quench, cot, swapped, before_own, after_own, before_par, after_par)

    total = parts[0]
    for half in range(2):
        for k in range(doses):
            if half or k:
                pairs = [(c * doses + d, (c ^ half) * doses + (d + k) % doses) for d in range(doses) for c in range(2)]
                total = total + lax.ppermute(parts[half * doses + k], ("ty", "dose"), pairs)
    return total.reshape(depth // doses, rows, lanes)


def solution(mesh):
    placed = (
        P("focus", "tx", "ty"),
        P(None, "tx", "ty"),
        P(("focus", "dose"), None, "tx", "ty"),
        P(),
        P(("focus", "dose")),
    )
    return jax.shard_map(
        on_device,
        mesh=mesh,
        in_specs=placed,
        out_specs=P(("focus", "dose"), "tx", "ty"),
        check_vma=False,
    )
```

time: 162 us -> 32.9 us (0.20)
  other arithmetic: 50.6 us -> 1.49 us
  waiting for transfers between devices: 65.3 us -> 16.3 us
  starting transfers between devices: 23.9 us -> 7.23 us
  between operations: 14.2 us -> 0.06 us
  local copies, waits for them, and re-layouts: 7.72 us -> 0.71 us
  Pallas kernels: 0 us -> 6.92 us
    ppermute x28 -> x8, waiting for transfers between devices: 55.4 us -> 16.3 us  [the longest x1 7.05 us: on_device(): before_own = lax.ppermute(up, 'tx', ahead)]
    sub x18 -> x0, other arithmetic: 24.5 us -> none  [the longest x5 9.21 us: diffuse(): return (lateral, upward + downward - 2.0 * center)]
    ppermute x28 -> x8, starting transfers between devices: 23.9 us -> 7.23 us  [the longest x1 3.05 us: on_device(): before_own = lax.ppermute(up, 'tx', ahead)]
    another operation x18 -> x0, other arithmetic: 14.5 us -> none  [the longest x3 6.37 us: on_device(): fields = jnp.stack((acid_now, quench_now), axis=1)]
    reduce_scatter x1 -> x0, waiting for transfers between devices: 9.9 us -> none  [on_device(): lax.psum_scatter(partial_value, 'dose', scatter_dimension=0, tiled=True)]
    pallas_call x0 -> x2, Pallas kernels: none -> 6.92 us  [the longest x1 4.58 us: on_device(): pl.pallas_call(kernel_main, out_shape=(jax.ShapeDtypeStruct((piece, lanes...]
    add x1 -> x0, other arithmetic: 4.46 us -> none  [diffuse(): padded[..., 2:, 1:-1] + padded[..., :-2, 1:-1] + padded[..., 1:-1, 2:]]
    reduce_sum x2 -> x0, other arithmetic: 3.23 us -> none  [the longest x1 2.3 us: on_device(): jnp.sum(adjoint[:, 0] * exposure_rate * dose_col * absorbed, axis=0)]
  transfers between devices with their start and end apart: 29 -> 8, of which waited for: 11 -> 5; matrix products, arithmetic and copies ran while one was open for 24% -> 0% of each run, Pallas kernels for 0% -> 0%
where the time goes in v1:
time: 32.9 us; the launch traced here: 32.7 us
  waiting for transfers between devices  16.3 us (50%)
  starting transfers between devices  7.23 us (22%)
  Pallas kernels  6.92 us (21%)
  other arithmetic  1.49 us (5%)
  local copies, waits for them, and re-layouts  0.71 us (2%)
    ppermute x1, waiting for transfers between devices, on_device(): before_own = lax.ppermute(up, 'tx', ahead)  7.05 us
    pallas_call x1, Pallas kernels, on_device(): pl.pallas_call(kernel_main, out_shape=(jax.ShapeDtypeStruct((piece, lanes...  4.58 us
    ppermute x3, waiting for transfers between devices, on_device(): total = total + lax.ppermute(parts[half * doses + k], ('ty', 'dose'), pairs)  3.94 us
    ppermute x1, waiting for transfers between devices, on_device(): after_own = lax.ppermute(down, 'tx', back)  3.8 us
    ppermute x1, starting transfers between devices, on_device(): before_own = lax.ppermute(up, 'tx', ahead)  3.05 us
    pallas_call x1, Pallas kernels, on_device(): pl.pallas_call(kernel_pack, out_shape=(field(HALO_ROWS), field(HALO_ROWS)...  2.34 us
    ppermute x3, starting transfers between devices, on_device(): total = total + lax.ppermute(parts[half * doses + k], ('ty', 'dose'), pairs)  2.14 us
    ppermute x1, starting transfers between devices, on_device(): after_own = lax.ppermute(down, 'tx', back)  2.03 us
  transfers between devices with their start and end apart: 8, of which 5 were waited for; matrix products, arithmetic and copies ran while one was open for 0% of the time, Pallas kernels for 0%

profile of v1, /device:TPU:0, one launch (start us, length us, event | category | flops | bytes accessed | tf_op | source)
XLA Modules:
  0.0 32.7 jit_solution(16442163044349192802)
XLA Ops:
  0.0 2.3 %shard_map.55 = (f32[15,4,8,128]{3,2,1,0:T(8,128)}, f32[15,4,8,128]{3,2,1,0:T(8,128)}, f32[24,4,8,128]{3,2,1,0:T(8,128)}) custom-call(f32[256,128]{1,0:T(8,128)} %bitcast.7, f32[256,128]{1,0:T(8,128)} %bitcast.9, f32[512,128]{1,0:T(8,128)} %bitcast.5), custom_call_target="tpu_custom_call" | custom-call | tf_op jit(solution)/shard_map/pallas_call | solution.py:205
  2.3 3.1 %collective-permute-start.1 = (f32[15,4,8,128]{3,2,1,0:T(8,128)}, f32[15,4,8,128]{3,2,1,0:T(8,128)S(1)}, u32[]{:S(2)}, u32[]{:S(2)}) collective-permute-start(f32[15,4,8,128]{3,2,1,0:T(8,128)} %get-tuple-element.13), channel_id=1, source_target_pairs={{0,4},{4,8},{8,12},{12,0},{1,5},{5,9},{9,13},{13,1},{2,6},{6,10},{... | collective-permute-start | bytes 737288 | tf_op jit(solution)/shard_map/ppermute | solution.py:215
  5.4 2.0 %collective-permute-start.2 = (f32[15,4,8,128]{3,2,1,0:T(8,128)}, f32[15,4,8,128]{3,2,1,0:T(8,128)S(1)}, u32[]{:S(2)}, u32[]{:S(2)}) collective-permute-start(f32[15,4,8,128]{3,2,1,0:T(8,128)} %get-tuple-element.14), channel_id=1, source_target_pairs={{4,0},{8,4},{12,8},{0,12},{5,1},{9,5},{13,9},{1,13},{6,2},{10,6},{... | collective-permute-start | bytes 737288 | tf_op jit(solution)/shard_map/ppermute | solution.py:216
  7.4 0.0 collective-permute-start
  7.4 7.1 %collective-permute-done.1.refs_6_ = f32[15,4,8,128]{3,2,1,0:T(8,128)S(1)} collective-permute-done((f32[15,4,8,128]{3,2,1,0:T(8,128)}, f32[15,4,8,128]{3,2,1,0:T(8,128)S(1)}, u32[]{:S(2)}, u32[]{:S(2)}) %collective-permute-start.1) | collective-permute-done | bytes 245792 | tf_op jit(solution)/shard_map/ppermute | solution.py:215
  14.5 0.0 copy-start.1
  14.5 0.0 collective-permute-start.3
  14.5 3.8 %collective-permute-done.2.refs_7_ = f32[15,4,8,128]{3,2,1,0:T(8,128)S(1)} collective-permute-done((f32[15,4,8,128]{3,2,1,0:T(8,128)}, f32[15,4,8,128]{3,2,1,0:T(8,128)S(1)}, u32[]{:S(2)}, u32[]{:S(2)}) %collective-permute-start.2) | collective-permute-done | bytes 245792 | tf_op jit(solution)/shard_map/ppermute | solution.py:216
  18.3 0.0 copy-start.2
  18.3 0.0 collective-permute-start.4
  18.3 0.0 collective-permute-done.refs_5_
  18.3 0.0 copy-start
  18.3 0.0 collective-permute-done.3.refs_8_
  18.3 0.0 copy-start.3
  18.3 1.5 %collective-permute-done.4.refs_9_ = f32[15,4,8,128]{3,2,1,0:T(8,128)S(1)} collective-permute-done((f32[15,4,8,128]{3,2,1,0:T(8,128)S(1)}, f32[15,4,8,128]{3,2,1,0:T(8,128)S(1)}, u32[]{:S(2)}, u32[]{:S(2)}) %collective-permute-start.4) | collective-permute-done | bytes 245792 | tf_op jit(solution)/shard_map/ppermute | solution.py:219
  19.8 0.0 copy-done.1
  19.8 0.0 copy-done.2
  19.8 0.0 copy-done
  19.8 0.0 copy-done.3
  19.8 0.0 copy-start.4
  19.8 0.7 %copy-done.4 = f32[15,4,8,128]{3,2,1,0:T(8,128)} copy-done((f32[15,4,8,128]{3,2,1,0:T(8,128)}, f32[15,4,8,128]{3,2,1,0:T(8,128)S(1)}, u32[]{:S(2)}) %copy-start.4) | copy-done | bytes 245784
  20.5 4.6 %shard_map.56 = (f32[128,128]{1,0:T(8,128)}, f32[128,128]{1,0:T(8,128)}, f32[128,128]{1,0:T(8,128)}, f32[128,128]{1,0:T(8,128)}) custom-call(f32[16]{0:T(128)} %refs_0_.1, s32[2]{0:T(128)} %refs_1_.1, f32[256,128]{1,0:T(8,128)} %bitcast.8, f32[256,128]{1,0:T(8,128)} %bitcast.10, f32[512,128]{1,0:T(8,128)} %bitcast.6, f32[24,4,8,128]{3,2,1,0:T(8,128)} %copy-done, ...), custom_call_target="tpu_custom_call" | custom-call | tf_op jit(solution)/shard_map/pallas_call | solution.py:228
  25.1 1.2 %collective-permute-start.7 = (f32[128,128]{1,0:T(8,128)}, f32[128,128]{1,0:T(8,128)S(1)}, u32[]{:S(2)}, u32[]{:S(2)}) collective-permute-start(f32[128,128]{1,0:T(8,128)} %get-tuple-element.18), channel_id=1, source_target_pairs={{0,3},{2,1},{1,2},{3,0},{4,7},{6,5},{5,6},{7,4},{8,11},{10,9},{9,1... | collective-permute-start | bytes 196616 | tf_op jit(solution)/shard_map/ppermute | solution.py:242
  26.3 0.4 %collective-permute-start.6 = (f32[128,128]{1,0:T(8,128)}, f32[128,128]{1,0:T(8,128)S(1)}, u32[]{:S(2)}, u32[]{:S(2)}) collective-permute-start(f32[128,128]{1,0:T(8,128)} %get-tuple-element.17), channel_id=1, source_target_pairs={{0,2},{2,0},{1,3},{3,1},{4,6},{6,4},{5,7},{7,5},{8,10},{10,8},{9,1... | collective-permute-start | bytes 196616 | tf_op jit(solution)/shard_map/ppermute | solution.py:242
  26.7 0.5 %collective-permute-start.5 = (f32[128,128]{1,0:T(8,128)}, f32[128,128]{1,0:T(8,128)S(1)}, u32[]{:S(2)}, u32[]{:S(2)}) collective-permute-start(f32[128,128]{1,0:T(8,128)} %get-tuple-element.16), channel_id=1, source_target_pairs={{0,1},{2,3},{1,0},{3,2},{4,5},{6,7},{5,4},{7,6},{8,9},{10,11},{9,8... | collective-permute-start | bytes 196616 | tf_op jit(solution)/shard_map/ppermute | solution.py:242
  27.3 2.1 %collective-permute-done.7 = f32[128,128]{1,0:T(8,128)S(1)} collective-permute-done((f32[128,128]{1,0:T(8,128)}, f32[128,128]{1,0:T(8,128)S(1)}, u32[]{:S(2)}, u32[]{:S(2)}) %collective-permute-start.7) | collective-permute-done | bytes 65568 | tf_op jit(solution)/shard_map/ppermute | solution.py:242
  29.4 0.0 collective-permute-done.6
  29.4 1.8 %collective-permute-done.5 = f32[128,128]{1,0:T(8,128)S(1)} collective-permute-done((f32[128,128]{1,0:T(8,128)}, f32[128,128]{1,0:T(8,128)S(1)}, u32[]{:S(2)}, u32[]{:S(2)}) %collective-permute-start.5) | collective-permute-done | bytes 65568 | tf_op jit(solution)/shard_map/ppermute | solution.py:242
  31.2 1.5 %add_bitcast_fusion = f32[16,8,128]{2,1,0:T(8,128)} fusion(f32[128,128]{1,0:T(8,128)S(1)} %collective-permute-done.7, f32[128,128]{1,0:T(8,128)S(1)} %collective-permute-done.6, f32[128,128]{1,0:T(8,128)} %get-tuple-element.15, f32[128,128]{1,0:T(8,128)S(1)} %collective-permute-done.5), kind=kLoop, calls=%fused_computation | loop fusion | flops 49152 | bytes 327680 | tf_op jit(solution)/shard_map/reshape | solution.py:243
Async XLA Ops:
  2.3 12.1 %collective-permute-start.1 = (f32[15,4,8,128]{3,2,1,0:T(8,128)}, f32[15,4,8,128]{3,2,1,0:T(8,128)S(1)}, u32[]{:S(2)}, u32[]{:S(2)}) collective-permute-start(f32[15,4,8,128]{3,2,1,0:T(8,128)} %get-tuple-element.13), channel_id=1, source_target_pairs={{0,4},{4,8},{8,12},{12,0},{1,5},{5,9},{9,13},{13,1},{2,6},{6,10},{... | collective-permute-start | bytes 737288 | tf_op jit(solution)/shard_map/ppermute | solution.py:215
  5.4 12.9 %collective-permute-start.2 = (f32[15,4,8,128]{3,2,1,0:T(8,128)}, f32[15,4,8,128]{3,2,1,0:T(8,128)S(1)}, u32[]{:S(2)}, u32[]{:S(2)}) collective-permute-start(f32[15,4,8,128]{3,2,1,0:T(8,128)} %get-tuple-element.14), channel_id=1, source_target_pairs={{4,0},{8,4},{12,8},{0,12},{5,1},{9,5},{13,9},{1,13},{6,2},{10,6},{... | collective-permute-start | bytes 737288 | tf_op jit(solution)/shard_map/ppermute | solution.py:216
  7.4 10.9 %collective-permute-start = (f32[24,4,8,128]{3,2,1,0:T(8,128)}, f32[24,4,8,128]{3,2,1,0:T(8,128)S(1)}, u32[]{:S(2)}, u32[]{:S(2)}) collective-permute-start(f32[24,4,8,128]{3,2,1,0:T(8,128)} %get-tuple-element.12), channel_id=1, source_target_pairs={{0,2},{2,0},{1,3},{3,1},{4,6},{6,4},{5,7},{7,5},{8,10},{10,8},{9,1... | collective-permute-start | bytes 1179656 | tf_op jit(solution)/shard_map/ppermute | solution.py:217
  14.5 5.3 %copy-start.1 = (f32[15,4,8,128]{3,2,1,0:T(8,128)}, f32[15,4,8,128]{3,2,1,0:T(8,128)S(1)}, u32[]{:S(2)}) copy-start(f32[15,4,8,128]{3,2,1,0:T(8,128)S(1)} %collective-permute-done.1.refs_6_) | copy-start | bytes 737284
  14.5 3.8 %collective-permute-start.3 = (f32[15,4,8,128]{3,2,1,0:T(8,128)S(1)}, f32[15,4,8,128]{3,2,1,0:T(8,128)S(1)}, u32[]{:S(2)}, u32[]{:S(2)}) collective-permute-start(f32[15,4,8,128]{3,2,1,0:T(8,128)S(1)} %collective-permute-done.1.refs_6_), channel_id=1, source_target_pairs={{0,2},{2,0},{1,3},{3,1},{4,6},{6,4},{5,7},{7,5},{8,10},{10,8},{9,1... | collective-permute-start | bytes 737288 | tf_op jit(solution)/shard_map/ppermute | solution.py:218
  18.3 1.5 %copy-start.2 = (f32[15,4,8,128]{3,2,1,0:T(8,128)}, f32[15,4,8,128]{3,2,1,0:T(8,128)S(1)}, u32[]{:S(2)}) copy-start(f32[15,4,8,128]{3,2,1,0:T(8,128)S(1)} %collective-permute-done.2.refs_7_) | copy-start | bytes 737284
  18.3 1.5 %collective-permute-start.4 = (f32[15,4,8,128]{3,2,1,0:T(8,128)S(1)}, f32[15,4,8,128]{3,2,1,0:T(8,128)S(1)}, u32[]{:S(2)}, u32[]{:S(2)}) collective-permute-start(f32[15,4,8,128]{3,2,1,0:T(8,128)S(1)} %collective-permute-done.2.refs_7_), channel_id=1, source_target_pairs={{0,2},{2,0},{1,3},{3,1},{4,6},{6,4},{5,7},{7,5},{8,10},{10,8},{9,1... | collective-permute-start | bytes 737288 | tf_op jit(solution)/shard_map/ppermute | solution.py:219
  18.3 1.5 %copy-start = (f32[24,4,8,128]{3,2,1,0:T(8,128)}, f32[24,4,8,128]{3,2,1,0:T(8,128)S(1)}, u32[]{:S(2)}) copy-start(f32[24,4,8,128]{3,2,1,0:T(8,128)S(1)} %collective-permute-done.refs_5_) | copy-start | bytes 1179652
  18.3 1.5 %copy-start.3 = (f32[15,4,8,128]{3,2,1,0:T(8,128)}, f32[15,4,8,128]{3,2,1,0:T(8,128)S(1)}, u32[]{:S(2)}) copy-start(f32[15,4,8,128]{3,2,1,0:T(8,128)S(1)} %collective-permute-done.3.refs_8_) | copy-start | bytes 737284
  19.8 0.7 %copy-start.4 = (f32[15,4,8,128]{3,2,1,0:T(8,128)}, f32[15,4,8,128]{3,2,1,0:T(8,128)S(1)}, u32[]{:S(2)}) copy-start(f32[15,4,8,128]{3,2,1,0:T(8,128)S(1)} %collective-permute-done.4.refs_9_) | copy-start | bytes 737284
  25.1 4.3 %collective-permute-start.7 = (f32[128,128]{1,0:T(8,128)}, f32[128,128]{1,0:T(8,128)S(1)}, u32[]{:S(2)}, u32[]{:S(2)}) collective-permute-start(f32[128,128]{1,0:T(8,128)} %get-tuple-element.18), channel_id=1, source_target_pairs={{0,3},{2,1},{1,2},{3,0},{4,7},{6,5},{5,6},{7,4},{8,11},{10,9},{9,1... | collective-permute-start | bytes 196616 | tf_op jit(solution)/shard_map/ppermute | solution.py:242
  26.3 3.1 %collective-permute-start.6 = (f32[128,128]{1,0:T(8,128)}, f32[128,128]{1,0:T(8,128)S(1)}, u32[]{:S(2)}, u32[]{:S(2)}) collective-permute-start(f32[128,128]{1,0:T(8,128)} %get-tuple-element.17), channel_id=1, source_target_pairs={{0,2},{2,0},{1,3},{3,1},{4,6},{6,4},{5,7},{7,5},{8,10},{10,8},{9,1... | collective-permute-start | bytes 196616 | tf_op jit(solution)/shard_map/ppermute | solution.py:242
  26.7 4.5 %collective-permute-start.5 = (f32[128,128]{1,0:T(8,128)}, f32[128,128]{1,0:T(8,128)S(1)}, u32[]{:S(2)}, u32[]{:S(2)}) collective-permute-start(f32[128,128]{1,0:T(8,128)} %get-tuple-element.16), channel_id=1, source_target_pairs={{0,1},{2,3},{1,0},{3,2},{4,5},{6,7},{5,4},{7,6},{8,9},{10,11},{9,8... | collective-permute-start | bytes 196616 | tf_op jit(solution)/shard_map/ppermute | solution.py:242

commit v2 on v0

v2 whole, which is shorter than its diff:
```python
import jax
import jax.numpy as jnp
from jax import lax
from jax.experimental import pallas as pl
from jax.experimental.pallas import tpu as pltpu
from jax.sharding import PartitionSpec as P

exposure_rate = 1.0
neutral_rate = 0.8
deprotect_rate = 0.5
acid_lateral = 0.23
acid_depth = 0.02
base_lateral = 0.2
base_depth = 0.02

HALO_AERIAL = 5
HALO_QUENCH = 4
HALO_COT = 3
SUB = 8
LIMIT = 20 << 20


def chip_row(rows, row):
    return row + lax.axis_index("ty") * (rows - 1 - 2 * row)


def vector(ref, rows, groups, k, row, base=0):
    return ref[pl.ds(base + rows * k + row, SUB, stride=rows * groups), :]


def pack_image_kernel(rows, groups, aerial, quench, straight, crossed):
    place = 0
    for src, width in ((aerial, HALO_AERIAL), (quench, HALO_QUENCH)):
        for i in range(width):
            for k in range(groups):
                straight[place, k] = vector(src, rows, groups, k, chip_row(rows, rows - width + i))
                crossed[place, k] = vector(src, rows, groups, k, chip_row(rows, width - 1 - i))
            place += 1


def pack_rest_kernel(rows, groups, local, aerial, quench, cot, straight, crossed, swap):
    area = rows * groups * SUB
    inner = rows // 2 + HALO_COT
    for d in range(local):
        for i in range(HALO_COT):
            for k in range(groups):
                place = d * HALO_COT + i
                straight[place, k] = vector(cot, rows, groups, k, chip_row(rows, rows - HALO_COT + i), d * area)
                crossed[place, k] = vector(cot, rows, groups, k, chip_row(rows, HALO_COT - 1 - i), d * area)
    place = 0
    parts = [(aerial, 0, rows), (quench, 0, rows)] + [(cot, d * area, inner) for d in range(local)]
    for src, base, width in parts:
        for i in range(width):
            for k in range(groups):
                swap[place, k] = vector(src, rows, groups, k, chip_row(rows, rows - 1 - i), base)
            place += 1


def load(ref, halo, row):
    return [ref[row + halo, i] for i in range(ref.shape[1])]


def save(ref, halo, row, value):
    for i in range(len(value)):
        ref[row + halo, i] = value[i]


def make_spread():
    lane = lax.broadcasted_iota(jnp.int32, (SUB, 128), 1)
    sub = lax.broadcasted_iota(jnp.int32, (SUB, 128), 0)
    first_lane = lane == 0
    last_lane = lane == 127
    first_sub = sub == 0
    last_sub = sub == SUB - 1

    def spread(ref, halo, row, center, along, depthwise):
        above = load(ref, halo, row - 1)
        below = load(ref, halo, row + 1)
        count = len(center)
        groups = count // 2
        keep = 1.0 - 4.0 * along - 2.0 * depthwise
        result = []
        for i in range(count):
            k = i % groups
            j = (i + groups) % count
            right = pltpu.roll(jnp.where(first_lane, center[j], center[i]), 127, 1)
            left = pltpu.roll(jnp.where(last_lane, center[j], center[i]), 1, 1)
            lateral = (above[i] + below[i]) + (right + left)
            if k + 1 < groups:
                deeper = center[i + 1]
            else:
                deeper = jnp.where(last_sub, center[i], pltpu.roll(center[i - k], SUB - 1, 0))
            if k > 0:
                higher = center[i - 1]
            else:
                higher = jnp.where(first_sub, center[i], pltpu.roll(center[i + groups - 1], 1, 0))
            result.append(keep * center[i] + along * lateral + depthwise * (deeper + higher))
        return result

    return spread


def history_rows(half):
    halos = {"c3": 3, "c2": 2, "c1": 1, "c0": 0, "q2": 2, "q1": 1, "q0": 0, "a2": 1, "a1": 0, "e": 0}
    places, total = {}, 0
    for name, halo in halos.items():
        places[name] = (halo, total)
        total += half + 2 * halo
    return places, total


def forward_kernel(rows, groups, local, levels, index, aerial, quench, swap, img_s, img_c, extra, hist, *scratch):
    a0, q0, a1, q1, a2, q2, a3 = scratch
    half = rows // 2
    places, total = history_rows(half)
    spread = make_spread()

    def source(raw, swap_at, halo_at, width, row):
        if row < 0:
            place = halo_at + width + row
            return [img_s[place, k] for k in range(groups)] + [img_c[place, k] for k in range(groups)]
        if row >= rows:
            return [extra[0, k] for k in range(groups)] + [extra[1, k] for k in range(groups)]
        own = [vector(raw, rows, groups, k, chip_row(rows, row)) for k in range(groups)]
        return own + [swap[swap_at + row, k] for k in range(groups)]

    for row in range(-HALO_QUENCH, half + HALO_QUENCH):
        save(q0, HALO_QUENCH, row, source(quench, rows, HALO_AERIAL, HALO_QUENCH, row))

    for d in range(local):
        dose = levels[index[d]]

        def keep(name, row, value):
            halo, place = places[name]
            save(hist, d * total + place + halo, row, value)

        for row in range(-HALO_AERIAL, half + HALO_AERIAL):
            light = source(aerial, 0, 0, HALO_AERIAL, row)
            absorbed = [jnp.exp((-exposure_rate * dose) * v) for v in light]
            save(a0, HALO_AERIAL, row, [1.0 - v for v in absorbed])
            if 0 <= row < half:
                keep("e", row, [(exposure_rate * dose) * v for v in absorbed])
                keep("q0", row, [neutral_rate * v for v in load(q0, HALO_QUENCH, row)])

        def forward(a_old, a_halo, q_old, q_halo, a_new, q_new):
            for row in range(1 - a_halo, half + a_halo - 1):
                a_now = load(a_old, a_halo, row)
                q_now = load(q_old, q_halo, row)
                reaction = [neutral_rate * a * q for a, q in zip(a_now, q_now)]
                a_next = spread(a_old, a_halo, row, a_now, acid_lateral, acid_depth)
                save(a_new, a_halo - 1, row, [v - r for v, r in zip(a_next, reaction)])
                if q_new is not None and 1 - q_halo <= row < half + q_halo - 1:
                    q_next = spread(q_old, q_halo, row, q_now, base_lateral, base_depth)
                    save(q_new, q_halo - 1, row, [v - r for v, r in zip(q_next, reaction)])

        forward(a0, 5, q0, 4, a1, q1)
        forward(a1, 4, q1, 3, a2, q2)
        forward(a2, 3, q2, 2, a3, None)

        for row in range(-3, half + 3):
            acids = {0: load(a0, 5, row), 1: load(a1, 4, row), 2: load(a2, 3, row)}
            if -2 <= row < half + 2:
                acids[3] = load(a3, 2, row)
            left = {n: [1.0 - deprotect_rate * v for v in value] for n, value in acids.items()}

            def times(*names):
                value = [(-deprotect_rate) * v for v in left[names[0]]]
                for n in names[1:]:
                    value = [v * m for v, m in zip(value, left[n])]
                return value

            keep("c3", row, times(0, 1, 2))
            if -2 <= row < half + 2:
                keep("c2", row, times(0, 1, 3))
                keep("q2", row, [neutral_rate * v for v in load(q2, 2, row)])
            if -1 <= row < half + 1:
                keep("c1", row, times(0, 2, 3))
                keep("q1", row, [neutral_rate * v for v in load(q1, 3, row)])
                keep("a2", row, [neutral_rate * v for v in acids[2]])
            if 0 <= row < half:
                keep("c0", row, times(1, 2, 3))
                keep("a1", row, [neutral_rate * v for v in acids[1]])


def backward_kernel(rows, groups, local, doses, hist, cot, swap, cot_s, cot_c, *refs):
    outs = refs[: 2 * doses]
    ct, l3, l2, m2, l1, m1, acc, full = refs[2 * doses :]
    half = rows // 2
    area = rows * groups * SUB
    depth = groups * SUB
    inner = half + HALO_COT
    place = lax.axis_index("dose")
    places, total = history_rows(half)
    spread = make_spread()

    for d in range(local):

        def past(name, row):
            halo, at = places[name]
            return load(hist, d * total + at + halo, row)

        for row in range(-3, half + 3):
            if row < 0:
                at = d * HALO_COT + HALO_COT + row
                value = [cot_s[at, k] for k in range(groups)] + [cot_c[at, k] for k in range(groups)]
            else:
                value = [vector(cot, rows, groups, k, chip_row(rows, row), d * area) for k in range(groups)]
                value += [swap[2 * rows + d * inner + row, k] for k in range(groups)]
            save(ct, 3, row, value)
            save(l3, 3, row, [c * v for c, v in zip(past("c3", row), value)])

        for row in range(-2, half + 2):
            old = load(l3, 3, row)
            new = spread(l3, 3, row, old, acid_lateral, acid_depth)
            parts = zip(new, past("q2", row), old, past("c2", row), load(ct, 3, row))
            save(l2, 2, row, [v - q * s + c * t for v, q, s, c, t in parts])
            if -1 <= row < half + 1:
                save(m2, 1, row, [-(a * s) for a, s in zip(past("a2", row), old)])
        for row in range(-1, half + 1):
            old = load(l2, 2, row)
            base = load(m2, 1, row)
            both = [a + b for a, b in zip(old, base)]
            new = spread(l2, 2, row, old, acid_lateral, acid_depth)
            parts = zip(new, past("q1", row), both, past("c1", row), load(ct, 3, row))
            save(l1, 1, row, [v - q * s + c * t for v, q, s, c, t in parts])
            if 0 <= row < half:
                new = spread(m2, 1, row, base, base_lateral, base_depth)
                save(m1, 0, row, [v - a * s for v, a, s in zip(new, past("a1", row), both)])
        for row in range(half):
            old = load(l1, 1, row)
            both = [a + b for a, b in zip(old, load(m1, 0, row))]
            new = spread(l1, 1, row, old, acid_lateral, acid_depth)
            parts = zip(new, past("q0", row), both, past("c0", row), load(ct, 3, row), past("e", row))
            value = [(v - q * s + c * t) * e for v, q, s, c, t, e in parts]
            if d > 0:
                value = [v + w for v, w in zip(value, load(acc, 0, row))]
            if d + 1 < local:
                save(acc, 0, row, value)
            else:
                for i in range(2 * groups):
                    side, k = divmod(i, groups)
                    full[side, row, pl.ds(k, SUB, stride=groups), :] = value[i]

    piece = depth // doses
    for side in range(2):
        for k in range(doses):
            start = pl.multiple_of(lax.rem(place + k, doses) * piece, SUB)
            for row in range(half):
                outs[side * doses + k][row] = full[side, row, pl.ds(start, piece), :]


def join_kernel(rows, piece, doses, *refs):
    parts, out = refs[:-1], refs[-1]
    half = rows // 2
    core = lax.axis_index("ty")
    for side in range(2):
        for row in range(half):
            owner = core + side * (1 - 2 * core)
            at = row + owner * (rows - 1 - 2 * row)
            for g in range(piece // SUB):
                value = parts[side * doses][row, pl.ds(g * SUB, SUB), :]
                for k in range(1, doses):
                    value = value + parts[side * doses + k][row, pl.ds(g * SUB, SUB), :]
                out[pl.ds(g * SUB * rows + at, SUB, stride=rows), :] = value


def on_device(aerial_image, quencher, cotangent, dose_levels, dose_index):
    depth, rows, lanes = aerial_image.shape
    local = cotangent.shape[0]
    groups = depth // SUB
    half = rows // 2
    doses = lax.axis_size("dose")
    ring = lax.axis_size("tx")
    f32 = jnp.float32
    aerial = aerial_image.reshape(depth * rows, lanes)
    quench = quencher.reshape(depth * rows, lanes)
    cot = cotangent.reshape(local * depth * rows, lanes)
    vmem = pl.BlockSpec(memory_space=pltpu.VMEM)
    smem = pl.BlockSpec(memory_space=pltpu.SMEM)

    def call(kernel, fixed, args, outs, scratch=(), scalars=0, flops=0):
        def body(*refs):
            kernel(*fixed, *refs)

        moved = sum(4 * x.size for x in list(args) + list(outs))
        return pl.pallas_call(
            body,
            name=kernel.__name__,
            out_shape=tuple(outs),
            in_specs=[smem] * scalars + [vmem] * (len(args) - scalars),
            out_specs=(vmem,) * len(outs),
            scratch_shapes=list(scratch),
            compiler_params=pltpu.CompilerParams(vmem_limit_bytes=LIMIT),
            cost_estimate=pl.CostEstimate(flops=flops, bytes_accessed=moved, transcendentals=0),
        )(*args)

    def field(n, vectors=groups):
        return jax.ShapeDtypeStruct((n, vectors, SUB, lanes), f32)

    def scratch(halo):
        return pltpu.VMEM((half + 2 * halo, 2 * groups, SUB, lanes), f32)

    def device(t, c):
        return (t % ring) * 2 + c

    straight = [(device(t, c), device(t + 1 - 2 * c, c)) for t in range(ring) for c in range(2)]
    crossed = [(device(t, c), device(t - 1 + 2 * c, 1 - c)) for t in range(ring) for c in range(2)]
    across = [(0, 1), (1, 0)]

    def along(value, pairs):
        return lax.ppermute(value, ("tx", "ty"), pairs)

    n_image = HALO_AERIAL + HALO_QUENCH
    n_cot = local * HALO_COT
    n_swap = 2 * rows + local * (half + HALO_COT)
    send_s, send_c = call(pack_image_kernel, (rows, groups), (aerial, quench), (field(n_image), field(n_image)))
    img_s = along(send_s, straight)
    img_c = along(send_c, crossed)
    send_s, send_c, swap = call(
        pack_rest_kernel, (rows, groups, local), (aerial, quench, cot), (field(n_cot), field(n_cot), field(n_swap))
    )
    swap = lax.ppermute(swap, "ty", across)
    cot_s = along(send_s, straight)
    cot_c = along(send_c, crossed)
    last = HALO_AERIAL - 1
    extra = jnp.concatenate((img_c[last : last + 1], img_s[last : last + 1]), axis=0)
    extra = lax.ppermute(extra, "ty", across)

    places, total = history_rows(half)
    (hist,) = call(
        forward_kernel,
        (rows, groups, local),
        (dose_levels, dose_index, aerial, quench, swap, img_s, img_c, extra),
        (field(local * total, 2 * groups),),
        [scratch(h) for h in (5, 4, 4, 3, 3, 2, 2)],
        scalars=2,
        flops=20_000_000,
    )
    piece = depth // doses
    parts = call(
        backward_kernel,
        (rows, groups, local, doses),
        (hist, cot, swap, cot_s, cot_c),
        (jax.ShapeDtypeStruct((half, piece, lanes), f32),) * (2 * doses),
        [scratch(h) for h in (3, 3, 2, 1, 1, 0, 0)] + [pltpu.VMEM((2, half, depth, lanes), f32)],
        flops=10_000_000,
    )

    arrived = []
    for side in range(2):
        for k in range(doses):
            part = parts[side * doses + k]
            if side or k:
                pairs = [(c * doses + d, (c ^ side) * doses + (d + k) % doses) for d in range(doses) for c in range(2)]
                part = lax.ppermute(part, ("ty", "dose"), pairs)
            arrived.append(part)
    (out,) = call(join_kernel, (rows, piece, doses), arrived, (jax.ShapeDtypeStruct((piece * rows, lanes), f32),))
    return out.reshape(piece, rows, lanes)


def solution(mesh):
    placed = (
        P("focus", "tx", "ty"),
        P(None, "tx", "ty"),
        P(("focus", "dose"), None, "tx", "ty"),
        P(),
        P(("focus", "dose")),
    )
    return jax.shard_map(
        on_device,
        mesh=mesh,
        in_specs=placed,
        out_specs=P(("focus", "dose"), "tx", "ty"),
        check_vma=False,
    )
```

time: 162 us -> 28.4 us (0.18)
  waiting for transfers between devices: 65.3 us -> 9.28 us
  other arithmetic: 50.6 us -> 0.01 us
  starting transfers between devices: 23.9 us -> 9.66 us
  between operations: 14.2 us -> 0.05 us
  Pallas kernels: 0 us -> 5.09 us
  local copies, waits for them, and re-layouts: 7.72 us -> 4.08 us
    ppermute x28 -> x9, waiting for transfers between devices: 55.4 us -> 9.28 us  [the longest x4 5.94 us: along(): return lax.ppermute(value, ('tx', 'ty'), pairs)]
    sub x18 -> x0, other arithmetic: 24.5 us -> none  [the longest x5 9.21 us: diffuse(): return (lateral, upward + downward - 2.0 * center)]
    another operation x18 -> x0, other arithmetic: 14.5 us -> none  [the longest x3 6.37 us: on_device(): fields = jnp.stack((acid_now, quench_now), axis=1)]
    ppermute x28 -> x9, starting transfers between devices: 23.9 us -> 9.66 us  [the longest x4 6.5 us: along(): return lax.ppermute(value, ('tx', 'ty'), pairs)]
    reduce_scatter x1 -> x0, waiting for transfers between devices: 9.9 us -> none  [on_device(): lax.psum_scatter(partial_value, 'dose', scatter_dimension=0, tiled=True)]
    pallas_call x0 -> x5, Pallas kernels: none -> 5.09 us  [call(): pl.pallas_call(body, name=kernel.__name__, out_shape=tuple(outs), in_spec...]
    add x1 -> x0, other arithmetic: 4.46 us -> none  [diffuse(): padded[..., 2:, 1:-1] + padded[..., :-2, 1:-1] + padded[..., 1:-1, 2:]]
    reduce_sum x2 -> x0, other arithmetic: 3.23 us -> none  [the longest x1 2.3 us: on_device(): jnp.sum(adjoint[:, 0] * exposure_rate * dose_col * absorbed, axis=0)]
  transfers between devices with their start and end apart: 29 -> 9, of which waited for: 11 -> 5; matrix products, arithmetic and copies ran while one was open for 24% -> 0% of each run, Pallas kernels for 0% -> 11%
where the time goes in v2:
time: 28.4 us; the launch traced here: 28.2 us
  starting transfers between devices  9.66 us (34%)
  waiting for transfers between devices  9.28 us (33%)
  Pallas kernels  5.09 us (18%)
  local copies, waits for them, and re-layouts  4.08 us (14%)
    ppermute x4, starting transfers between devices, along(): return lax.ppermute(value, ('tx', 'ty'), pairs)  6.5 us
    ppermute x4, waiting for transfers between devices, along(): return lax.ppermute(value, ('tx', 'ty'), pairs)  5.94 us
    pallas_call x5, Pallas kernels, call(): pl.pallas_call(body, name=kernel.__name__, out_shape=tuple(outs), in_spec...  5.09 us
    unnamed x12, local copies, waits for them, and re-layouts  4.07 us
    ppermute x3, waiting for transfers between devices, on_device(): part = lax.ppermute(part, ('ty', 'dose'), pairs)  2.48 us
    ppermute x3, starting transfers between devices, on_device(): part = lax.ppermute(part, ('ty', 'dose'), pairs)  2.2 us
    ppermute x1, waiting for transfers between devices, on_device(): extra = lax.ppermute(extra, 'ty', across)  0.86 us
  transfers between devices with their start and end apart: 9, of which 5 were waited for; matrix products, arithmetic and copies ran while one was open for 0% of the time, Pallas kernels for 11%

profile of v2, /device:TPU:0, one launch (start us, length us, event | category | flops | bytes accessed | tf_op | source)
XLA Modules:
  0.0 28.2 jit_solution(17209194496114134727)
XLA Ops:
  0.0 0.0 copy-start
  0.0 0.9 %copy-done = f32[32,8,128]{2,1,0:T(8,128)S(1)} copy-done((f32[32,8,128]{2,1,0:T(8,128)S(1)}, f32[32,8,128]{2,1,0:T(8,128)}, u32[]{:S(2)}) %copy-start) | copy-done | bytes 131096
  0.9 0.0 copy-start.1
  0.9 0.9 %copy-done.1 = f32[32,8,128]{2,1,0:T(8,128)S(1)} copy-done((f32[32,8,128]{2,1,0:T(8,128)S(1)}, f32[32,8,128]{2,1,0:T(8,128)}, u32[]{:S(2)}) %copy-start.1) | copy-done | bytes 131096
  1.8 0.0 copy-start.2
  1.8 0.9 %copy-done.2 = f32[2,32,8,128]{3,2,1,0:T(8,128)S(1)} copy-done((f32[2,32,8,128]{3,2,1,0:T(8,128)S(1)}, f32[2,32,8,128]{3,2,1,0:T(8,128)}, u32[]{:S(2)}) %copy-start.2) | copy-done | bytes 262168
  2.8 0.0 copy-start.3
  2.8 0.4 %pack_rest_kernel.1 = (f32[6,4,8,128]{3,2,1,0:T(8,128)S(1)}, f32[6,4,8,128]{3,2,1,0:T(8,128)S(1)}, f32[30,4,8,128]{3,2,1,0:T(8,128)S(1)}) custom-call(f32[256,128]{1,0:T(8,128)S(1)} %bitcast.4, f32[256,128]{1,0:T(8,128)S(1)} %bitcast.7, f32[512,128]{1,0:T(8,128)S(1)} %bitcast.10), custom_call_target="tpu_custom_call" | custom-call | bytes 1212416 | tf_op jit(solution)/shard_map/pack_rest_kernel/pallas_call | solution.py:286
  3.2 0.6 %collective-permute-start = (f32[30,4,8,128]{3,2,1,0:T(8,128)S(1)}, f32[30,4,8,128]{3,2,1,0:T(8,128)S(1)}, u32[]{:S(2)}, u32[]{:S(2)}) collective-permute-start(f32[30,4,8,128]{3,2,1,0:T(8,128)S(1)} %get-tuple-element.14), channel_id=1, source_target_pairs={{0,2},{2,0},{1,3},{3,1},{4,6},{6,4},{5,7},{7,5},{8,10},{10,8},{9,1... | collective-permute-start | bytes 1474568 | tf_op jit(solution)/shard_map/ppermute | solution.py:322
  3.7 0.2 pack_image_kernel.1
  3.9 2.6 %collective-permute-start.1 = (f32[9,4,8,128]{3,2,1,0:T(8,128)S(1)}, f32[9,4,8,128]{3,2,1,0:T(8,128)S(1)}, u32[]{:S(2)}, u32[]{:S(2)}) collective-permute-start(f32[9,4,8,128]{3,2,1,0:T(8,128)S(1)} %get-tuple-element.15), channel_id=1, source_target_pairs={{0,4},{2,14},{4,8},{6,2},{8,12},{10,6},{12,0},{14,10},{1,5},{3,15}... | collective-permute-start | bytes 442376 | tf_op jit(solution)/shard_map/ppermute | solution.py:311
  6.5 2.3 %collective-permute-start.2 = (f32[9,4,8,128]{3,2,1,0:T(8,128)S(1)}, f32[9,4,8,128]{3,2,1,0:T(8,128)S(1)}, u32[]{:S(2)}, u32[]{:S(2)}) collective-permute-start(f32[9,4,8,128]{3,2,1,0:T(8,128)S(1)} %get-tuple-element.16), channel_id=1, source_target_pairs={{0,14},{2,4},{4,2},{6,8},{8,6},{10,12},{12,10},{14,0},{1,15},{3,5}... | collective-permute-start | bytes 442376 | tf_op jit(solution)/shard_map/ppermute | solution.py:311
  8.8 1.6 %collective-permute-start.4 = (f32[6,4,8,128]{3,2,1,0:T(8,128)S(1)}, f32[6,4,8,128]{3,2,1,0:T(8,128)S(1)}, u32[]{:S(2)}, u32[]{:S(2)}) collective-permute-start(f32[6,4,8,128]{3,2,1,0:T(8,128)S(1)} %get-tuple-element.17), channel_id=1, source_target_pairs={{0,4},{2,14},{4,8},{6,2},{8,12},{10,6},{12,0},{14,10},{1,5},{3,15}... | collective-permute-start | bytes 294920 | tf_op jit(solution)/shard_map/ppermute | solution.py:311
  10.4 0.0 collective-permute-start.5
  10.4 3.0 %collective-permute-done.1.refs_5_ = f32[9,4,8,128]{3,2,1,0:T(8,128)S(1)} collective-permute-done((f32[9,4,8,128]{3,2,1,0:T(8,128)S(1)}, f32[9,4,8,128]{3,2,1,0:T(8,128)S(1)}, u32[]{:S(2)}, u32[]{:S(2)}) %collective-permute-start.1) | collective-permute-done | bytes 147488 | tf_op jit(solution)/shard_map/ppermute | solution.py:311
  13.4 3.0 %collective-permute-done.2.refs_6_ = f32[9,4,8,128]{3,2,1,0:T(8,128)S(1)} collective-permute-done((f32[9,4,8,128]{3,2,1,0:T(8,128)S(1)}, f32[9,4,8,128]{3,2,1,0:T(8,128)S(1)}, u32[]{:S(2)}, u32[]{:S(2)}) %collective-permute-start.2) | collective-permute-done | bytes 147488 | tf_op jit(solution)/shard_map/ppermute | solution.py:311
  16.3 0.4 %collective-permute-start.3 = (f32[2,4,8,128]{3,2,1,0:T(8,128)S(1)}, f32[2,4,8,128]{3,2,1,0:T(8,128)S(1)}, u32[]{:S(2)}, u32[]{:S(2)}) collective-permute-start(f32[2,4,8,128]{3,2,1,0:T(8,128)S(1)} %pad_maximum_fusion), channel_id=1, source_target_pairs={{0,2},{2,0},{1,3},{3,1},{4,6},{6,4},{5,7},{7,5},{8,10},{10,8},{9,1... | collective-permute-start | bytes 98312 | tf_op jit(solution)/shard_map/ppermute | solution.py:327
  16.7 0.9 %collective-permute-done.3.refs_7_ = f32[2,4,8,128]{3,2,1,0:T(8,128)S(1)} collective-permute-done((f32[2,4,8,128]{3,2,1,0:T(8,128)S(1)}, f32[2,4,8,128]{3,2,1,0:T(8,128)S(1)}, u32[]{:S(2)}, u32[]{:S(2)}) %collective-permute-start.3) | collective-permute-done | bytes 32800 | tf_op jit(solution)/shard_map/ppermute | solution.py:327
  17.6 0.0 collective-permute-done.refs_4_.refs_2_
  17.6 0.0 copy-start.4
  17.6 0.7 %copy-done.4 = f32[16]{0:T(128)S(1)} copy-done((f32[16]{0:T(128)S(1)}, f32[16]{0:T(128)}, u32[]{:S(2)}) %copy-start.4) | copy-done | bytes 88
  18.3 0.0 copy-start.5
  18.3 0.7 %copy-done.5 = s32[2]{0:T(128)S(1)} copy-done((s32[2]{0:T(128)S(1)}, s32[2]{0:T(128)}, u32[]{:S(2)}) %copy-start.5) | copy-done | bytes 32
  18.9 2.8 %forward_kernel.1.refs_0_ = f32[120,8,8,128]{3,2,1,0:T(8,128)S(1)} custom-call(f32[16]{0:T(128)S(1)} %copy-done.4, s32[2]{0:T(128)S(1)} %copy-done.5, f32[256,128]{1,0:T(8,128)S(1)} %bitcast.6, f32[256,128]{1,0:T(8,128)S(1)} %bitcast.9, f32[30,4,8,128]{3,2,1,0:T(8,128)S(1)} %collective-permute-done.refs_4_.refs_2_, ...), custom_call_target="tpu_custom_call" | custom-call | flops 20000000 | bytes 5013576 | tf_op jit(solution)/shard_map/forward_kernel/pallas_call | solution.py:286
  21.7 0.0 collective-permute-done.4.refs_3_
  21.7 0.0 collective-permute-done.5.refs_4_
  21.8 0.0 copy-done.3
  21.8 1.1 %backward_kernel.1 = (f32[4,16,128]{2,1,0:T(8,128)S(1)}, f32[4,16,128]{2,1,0:T(8,128)S(1)}, f32[4,16,128]{2,1,0:T(8,128)S(1)}, f32[4,16,128]{2,1,0:T(8,128)S(1)}) custom-call(f32[120,8,8,128]{3,2,1,0:T(8,128)S(1)} %forward_kernel.1.refs_0_, f32[512,128]{1,0:T(8,128)S(1)} %bitcast.11, f32[30,4,8,128]{3,2,1,0:T(8,128)S(1)} %collective-permute-done.refs_4_.refs_2_, ...), custom_call_target="tpu_custom_call" | custom-call | flops 10000000 | bytes 5013504 | tf_op jit(solution)/shard_map/backward_kernel/pallas_call | solution.py:286
  22.8 1.3 %collective-permute-start.6 = (f32[4,16,128]{2,1,0:T(8,128)S(1)}, f32[4,16,128]{2,1,0:T(8,128)S(1)}, u32[]{:S(2)}, u32[]{:S(2)}) collective-permute-start(f32[4,16,128]{2,1,0:T(8,128)S(1)} %get-tuple-element.20), channel_id=1, source_target_pairs={{0,1},{2,3},{1,0},{3,2},{4,5},{6,7},{5,4},{7,6},{8,9},{10,11},{9,8... | collective-permute-start | bytes 98312 | tf_op jit(solution)/shard_map/ppermute | solution.py:355
  24.1 0.1 collective-permute-start.7
  24.2 0.9 %collective-permute-start.8 = (f32[4,16,128]{2,1,0:T(8,128)S(1)}, f32[4,16,128]{2,1,0:T(8,128)S(1)}, u32[]{:S(2)}, u32[]{:S(2)}) collective-permute-start(f32[4,16,128]{2,1,0:T(8,128)S(1)} %get-tuple-element.22), channel_id=1, source_target_pairs={{0,3},{2,1},{1,2},{3,0},{4,7},{6,5},{5,6},{7,4},{8,11},{10,9},{9,1... | collective-permute-start | bytes 98312 | tf_op jit(solution)/shard_map/ppermute | solution.py:355
  25.0 1.8 %collective-permute-done.6.refs_1_ = f32[4,16,128]{2,1,0:T(8,128)S(1)} collective-permute-done((f32[4,16,128]{2,1,0:T(8,128)S(1)}, f32[4,16,128]{2,1,0:T(8,128)S(1)}, u32[]{:S(2)}, u32[]{:S(2)}) %collective-permute-start.6) | collective-permute-done | bytes 32800 | tf_op jit(solution)/shard_map/ppermute | solution.py:355
  26.8 0.0 collective-permute-done.7.refs_2_
  26.8 0.7 %collective-permute-done.8.refs_3_ = f32[4,16,128]{2,1,0:T(8,128)S(1)} collective-permute-done((f32[4,16,128]{2,1,0:T(8,128)S(1)}, f32[4,16,128]{2,1,0:T(8,128)S(1)}, u32[]{:S(2)}, u32[]{:S(2)}) %collective-permute-start.8) | collective-permute-done | bytes 32800 | tf_op jit(solution)/shard_map/ppermute | solution.py:355
  27.5 0.6 %join_kernel.1 = f32[128,128]{1,0:T(8,128)} custom-call(f32[4,16,128]{2,1,0:T(8,128)S(1)} %get-tuple-element.19.refs_0_, f32[4,16,128]{2,1,0:T(8,128)S(1)} %collective-permute-done.6.refs_1_, f32[4,16,128]{2,1,0:T(8,128)S(1)} %collective-permute-done.7.refs_2_, f32[4,16,128]{2,1,0:T(8,128)S(1)} %collective-permute-done.8.refs_3_), custom_call_target="tpu_custom_call" | custom-call | bytes 196608 | tf_op jit(solution)/shard_map/join_kernel/pallas_call | solution.py:286
  (3 shorter events, 0.0 us)
Async XLA Ops:
  0.0 0.9 %copy-start = (f32[32,8,128]{2,1,0:T(8,128)S(1)}, f32[32,8,128]{2,1,0:T(8,128)}, u32[]{:S(2)}) copy-start(f32[32,8,128]{2,1,0:T(8,128)} %param.5) | copy-start | bytes 393220
  0.9 0.9 %copy-start.1 = (f32[32,8,128]{2,1,0:T(8,128)S(1)}, f32[32,8,128]{2,1,0:T(8,128)}, u32[]{:S(2)}) copy-start(f32[32,8,128]{2,1,0:T(8,128)} %param.6) | copy-start | bytes 393220
  1.8 0.9 %copy-start.2 = (f32[2,32,8,128]{3,2,1,0:T(8,128)S(1)}, f32[2,32,8,128]{3,2,1,0:T(8,128)}, u32[]{:S(2)}) copy-start(f32[2,32,8,128]{3,2,1,0:T(8,128)} %param.7) | copy-start | bytes 786436
  2.8 19.0 %copy-start.3 = (f32[2,32,8,128]{3,2,1,0:T(8,128)S(1)}, f32[2,32,8,128]{3,2,1,0:T(8,128)}, u32[]{:S(2)}) copy-start(f32[2,32,8,128]{3,2,1,0:T(8,128)} %param.7) | copy-start | bytes 786436
  3.2 14.4 %collective-permute-start = (f32[30,4,8,128]{3,2,1,0:T(8,128)S(1)}, f32[30,4,8,128]{3,2,1,0:T(8,128)S(1)}, u32[]{:S(2)}, u32[]{:S(2)}) collective-permute-start(f32[30,4,8,128]{3,2,1,0:T(8,128)S(1)} %get-tuple-element.14), channel_id=1, source_target_pairs={{0,2},{2,0},{1,3},{3,1},{4,6},{6,4},{5,7},{7,5},{8,10},{10,8},{9,1... | collective-permute-start | bytes 1474568 | tf_op jit(solution)/shard_map/ppermute | solution.py:322
  3.9 9.5 %collective-permute-start.1 = (f32[9,4,8,128]{3,2,1,0:T(8,128)S(1)}, f32[9,4,8,128]{3,2,1,0:T(8,128)S(1)}, u32[]{:S(2)}, u32[]{:S(2)}) collective-permute-start(f32[9,4,8,128]{3,2,1,0:T(8,128)S(1)} %get-tuple-element.15), channel_id=1, source_target_pairs={{0,4},{2,14},{4,8},{6,2},{8,12},{10,6},{12,0},{14,10},{1,5},{3,15}... | collective-permute-start | bytes 442376 | tf_op jit(solution)/shard_map/ppermute | solution.py:311
  6.5 9.8 %collective-permute-start.2 = (f32[9,4,8,128]{3,2,1,0:T(8,128)S(1)}, f32[9,4,8,128]{3,2,1,0:T(8,128)S(1)}, u32[]{:S(2)}, u32[]{:S(2)}) collective-permute-start(f32[9,4,8,128]{3,2,1,0:T(8,128)S(1)} %get-tuple-element.16), channel_id=1, source_target_pairs={{0,14},{2,4},{4,2},{6,8},{8,6},{10,12},{12,10},{14,0},{1,15},{3,5}... | collective-permute-start | bytes 442376 | tf_op jit(solution)/shard_map/ppermute | solution.py:311
  8.8 12.9 %collective-permute-start.4 = (f32[6,4,8,128]{3,2,1,0:T(8,128)S(1)}, f32[6,4,8,128]{3,2,1,0:T(8,128)S(1)}, u32[]{:S(2)}, u32[]{:S(2)}) collective-permute-start(f32[6,4,8,128]{3,2,1,0:T(8,128)S(1)} %get-tuple-element.17), channel_id=1, source_target_pairs={{0,4},{2,14},{4,8},{6,2},{8,12},{10,6},{12,0},{14,10},{1,5},{3,15}... | collective-permute-start | bytes 294920 | tf_op jit(solution)/shard_map/ppermute | solution.py:311
  10.4 11.4 %collective-permute-start.5 = (f32[6,4,8,128]{3,2,1,0:T(8,128)S(1)}, f32[6,4,8,128]{3,2,1,0:T(8,128)S(1)}, u32[]{:S(2)}, u32[]{:S(2)}) collective-permute-start(f32[6,4,8,128]{3,2,1,0:T(8,128)S(1)} %get-tuple-element.18), channel_id=1, source_target_pairs={{0,14},{2,4},{4,2},{6,8},{8,6},{10,12},{12,10},{14,0},{1,15},{3,5}... | collective-permute-start | bytes 294920 | tf_op jit(solution)/shard_map/ppermute | solution.py:311
  16.3 1.3 %collective-permute-start.3 = (f32[2,4,8,128]{3,2,1,0:T(8,128)S(1)}, f32[2,4,8,128]{3,2,1,0:T(8,128)S(1)}, u32[]{:S(2)}, u32[]{:S(2)}) collective-permute-start(f32[2,4,8,128]{3,2,1,0:T(8,128)S(1)} %pad_maximum_fusion), channel_id=1, source_target_pairs={{0,2},{2,0},{1,3},{3,1},{4,6},{6,4},{5,7},{7,5},{8,10},{10,8},{9,1... | collective-permute-start | bytes 98312 | tf_op jit(solution)/shard_map/ppermute | solution.py:327
  17.6 0.7 %copy-start.4 = (f32[16]{0:T(128)S(1)}, f32[16]{0:T(128)}, u32[]{:S(2)}) copy-start(f32[16]{0:T(128)} %refs_0_.1) | copy-start | bytes 196
  18.3 0.7 %copy-start.5 = (s32[2]{0:T(128)S(1)}, s32[2]{0:T(128)}, u32[]{:S(2)}) copy-start(s32[2]{0:T(128)} %refs_1_.1) | copy-start | bytes 28
  22.8 4.0 %collective-permute-start.6 = (f32[4,16,128]{2,1,0:T(8,128)S(1)}, f32[4,16,128]{2,1,0:T(8,128)S(1)}, u32[]{:S(2)}, u32[]{:S(2)}) collective-permute-start(f32[4,16,128]{2,1,0:T(8,128)S(1)} %get-tuple-element.20), channel_id=1, source_target_pairs={{0,1},{2,3},{1,0},{3,2},{4,5},{6,7},{5,4},{7,6},{8,9},{10,11},{9,8... | collective-permute-start | bytes 98312 | tf_op jit(solution)/shard_map/ppermute | solution.py:355
  24.1 2.7 %collective-permute-start.7 = (f32[4,16,128]{2,1,0:T(8,128)S(1)}, f32[4,16,128]{2,1,0:T(8,128)S(1)}, u32[]{:S(2)}, u32[]{:S(2)}) collective-permute-start(f32[4,16,128]{2,1,0:T(8,128)S(1)} %get-tuple-element.21), channel_id=1, source_target_pairs={{0,2},{2,0},{1,3},{3,1},{4,6},{6,4},{5,7},{7,5},{8,10},{10,8},{9,1... | collective-permute-start | bytes 98312 | tf_op jit(solution)/shard_map/ppermute | solution.py:355
  24.2 3.3 %collective-permute-start.8 = (f32[4,16,128]{2,1,0:T(8,128)S(1)}, f32[4,16,128]{2,1,0:T(8,128)S(1)}, u32[]{:S(2)}, u32[]{:S(2)}) collective-permute-start(f32[4,16,128]{2,1,0:T(8,128)S(1)} %get-tuple-element.22), channel_id=1, source_target_pairs={{0,3},{2,1},{1,2},{3,0},{4,7},{6,5},{5,6},{7,4},{8,11},{10,9},{9,1... | collective-permute-start | bytes 98312 | tf_op jit(solution)/shard_map/ppermute | solution.py:355

commit v3 on v2

v3 whole, which is shorter than its diff:
```python
import jax
import jax.numpy as jnp
from jax import lax
from jax.experimental import pallas as pl
from jax.experimental.pallas import tpu as pltpu
from jax.sharding import PartitionSpec as P


exposure_rate = 1.0
neutral_rate = 0.8
deprotect_rate = 0.5
acid_lateral = 0.23
acid_depth = 0.02
base_lateral = 0.2
base_depth = 0.02

HALO_AERIAL = 5
HALO_QUENCH = 4
HALO_COT = 3
SUB = 8
LIMIT = 20 << 20


def chip_row(rows, row):
    return row + lax.axis_index("ty") * (rows - 1 - 2 * row)


def vector(ref, rows, groups, k, row, base=0):
    return ref[pl.ds(base + rows * k + row, SUB, stride=rows * groups), :]


def pack_kernel(rows, groups, local, *refs):
    image_hbm, quench_hbm, cot_hbm = refs[:3]
    image_s, image_c, cot_s, cot_c, swap, aerial, quench, cot = refs[3:11]
    sems = refs[11]
    pairs = ((image_hbm, aerial), (quench_hbm, quench), (cot_hbm, cot))
    copies = [pltpu.make_async_copy(src, dst, sems.at[i]) for i, (src, dst) in enumerate(pairs)]
    for copy in copies:
        copy.start()
    area = rows * groups * SUB
    inner = rows // 2 + HALO_COT
    copies[0].wait()
    copies[1].wait()
    place = 0
    for src, width in ((aerial, HALO_AERIAL), (quench, HALO_QUENCH)):
        for i in range(width):
            for k in range(groups):
                image_s[place, k] = vector(src, rows, groups, k, chip_row(rows, rows - width + i))
                image_c[place, k] = vector(src, rows, groups, k, chip_row(rows, width - 1 - i))
            place += 1
    copies[2].wait()
    for d in range(local):
        for i in range(HALO_COT):
            for k in range(groups):
                place = d * HALO_COT + i
                cot_s[place, k] = vector(cot, rows, groups, k, chip_row(rows, rows - HALO_COT + i), d * area)
                cot_c[place, k] = vector(cot, rows, groups, k, chip_row(rows, HALO_COT - 1 - i), d * area)
    place = 0
    parts = [(aerial, 0, rows), (quench, 0, rows)] + [(cot, d * area, inner) for d in range(local)]
    for src, base, width in parts:
        for i in range(width):
            for k in range(groups):
                swap[place, k] = vector(src, rows, groups, k, chip_row(rows, rows - 1 - i), base)
            place += 1


def load(ref, halo, row):
    return [ref[row + halo, i] for i in range(ref.shape[1])]


def save(ref, halo, row, value):
    for i in range(len(value)):
        ref[row + halo, i] = value[i]


def make_spread():
    lane = lax.broadcasted_iota(jnp.int32, (SUB, 128), 1)
    sub = lax.broadcasted_iota(jnp.int32, (SUB, 128), 0)
    first_lane = lane == 0
    last_lane = lane == 127
    first_sub = sub == 0
    last_sub = sub == SUB - 1

    def spread(above, center, below, along, depthwise):
        count = len(center)
        groups = count // 2
        keep = 1.0 - 4.0 * along - 2.0 * depthwise
        result = []
        for i in range(count):
            k = i % groups
            j = (i + groups) % count
            right = pltpu.roll(jnp.where(first_lane, center[j], center[i]), 127, 1)
            left = pltpu.roll(jnp.where(last_lane, center[j], center[i]), 1, 1)
            lateral = (above[i] + below[i]) + (right + left)
            if k + 1 < groups:
                deeper = center[i + 1]
            else:
                deeper = jnp.where(last_sub, center[i], pltpu.roll(center[i - k], SUB - 1, 0))
            if k > 0:
                higher = center[i - 1]
            else:
                higher = jnp.where(first_sub, center[i], pltpu.roll(center[i + groups - 1], 1, 0))
            result.append(keep * center[i] + along * lateral + depthwise * (deeper + higher))
        return result

    return spread


def near_rows(rows):
    half = rows // 2
    return {
        "q0": (0, rows),
        "a0": (0, rows),
        "a1": (1, rows - 1),
        "a2": (2, rows - 2),
        "a3": (3, rows - 3),
        "q1": (1, rows - 1),
        "q2": (2, rows - 2),
        "c3": (2, half + 3),
        "c2": (3, half + 2),
        "c1": (3, half + 1),
        "c0": (3, half),
        "e": (0, half),
        "dose": (0, 1),
    }


def far_rows():
    return {
        "q0": (-4, 0),
        "a0": (-5, 0),
        "a1": (-4, 1),
        "a2": (-3, 2),
        "a3": (-2, 3),
        "q1": (-3, 1),
        "q2": (-2, 2),
        "c3": (-3, 2),
        "c2": (-2, 3),
        "c1": (-1, 3),
        "c0": (0, 3),
    }


def places_of(table, local):
    places, total = {}, 0
    for name, (first, end) in table.items():
        for d in range(local):
            for row in range(first, end):
                if name == "q0" and d > 0:
                    places[name, d, row] = places[name, 0, row]
                else:
                    places[name, d, row] = total
                    total += 1
    return places, total


class Fields:
    def __init__(self, rows, local, near, far=None, more=None):
        self.stores = [(near, places_of(near_rows(rows), local)[0])]
        if far is not None:
            self.stores.append((far, places_of(far_rows(), local)[0]))
        self.more = {} if more is None else more

    def get(self, name, d, row):
        if (name, d, row) in self.more:
            return self.more[name, d, row]
        for ref, places in self.stores:
            if (name, d, row) in places:
                at = places[name, d, row]
                return [ref[at, i] for i in range(ref.shape[1])]
        raise KeyError((name, row))

    def put(self, name, d, row, value):
        ref, places = self.stores[-1]
        at = places[name, d, row]
        for i in range(len(value)):
            ref[at, i] = value[i]


def left_of(acid):
    return [1.0 - deprotect_rate * v for v in acid]


def next_acid(spread, fields, d, n, row):
    name = "a%d" % n
    above, center, below = (fields.get(name, d, row + i) for i in (-1, 0, 1))
    quench = fields.get("q%d" % n, d, row)
    new = spread(above, center, below, acid_lateral, acid_depth)
    reaction = [neutral_rate * a * q for a, q in zip(center, quench)]
    return [v - r for v, r in zip(new, reaction)], reaction


def forward_rows(spread, fields, d, table):
    for n in range(3):
        first, end = table["a%d" % (n + 1)]
        for row in range(first, end):
            new, reaction = next_acid(spread, fields, d, n, row)
            fields.put("a%d" % (n + 1), d, row, new)
            if n < 2:
                q_first, q_end = table["q%d" % (n + 1)]
                if q_first <= row < q_end:
                    name = "q%d" % n
                    above, center, below = (fields.get(name, d, row + i) for i in (-1, 0, 1))
                    new = spread(above, center, below, base_lateral, base_depth)
                    fields.put("q%d" % (n + 1), d, row, [v - r for v, r in zip(new, reaction)])

    first = min(table[c][0] for c in ("c3", "c2", "c1", "c0"))
    end = max(table[c][1] for c in ("c3", "c2", "c1", "c0"))
    for row in range(first, end):
        wanted = [n for n in range(4) if table["c%d" % n][0] <= row < table["c%d" % n][1]]
        left = {}

        def of(n):
            if n not in left:
                left[n] = left_of(fields.get("a%d" % n, d, row))
            return left[n]

        for n in wanted:
            parts = [m for m in range(4) if m != n]
            if n >= 2 and table["e"][1] > 0 and row == table["c%d" % n][1] - 1:
                parts = parts[:2]
            value = [(-deprotect_rate) * v for v in of(parts[0])]
            for m in parts[1:]:
                value = [v * w for v, w in zip(value, of(m))]
            fields.put("c%d" % n, d, row, value)


def near_kernel(rows, groups, local, levels, index, aerial, quench, swap, near):
    half = rows // 2
    spread = make_spread()
    fields = Fields(rows, local, near)

    def source(raw, at, row):
        own = [vector(raw, rows, groups, k, chip_row(rows, row)) for k in range(groups)]
        return own + [swap[at + row, k] for k in range(groups)]

    for row in range(rows):
        fields.put("q0", 0, row, source(quench, rows, row))
    for d in range(local):
        dose = jnp.full((SUB, near.shape[3]), levels[index[d]], jnp.float32)
        fields.put("dose", d, 0, [dose] * (2 * groups))
        rate = -exposure_rate * dose
        for row in range(rows):
            absorbed = [jnp.exp(rate * v) for v in source(aerial, 0, row)]
            fields.put("a0", d, row, [1.0 - v for v in absorbed])
            if row < half:
                fields.put("e", d, row, [exposure_rate * dose * v for v in absorbed])
        forward_rows(spread, fields, d, near_rows(rows))


def far_kernel(rows, groups, local, near, image_s, image_c, far):
    spread = make_spread()
    fields = Fields(rows, local, near, far)
    table = dict(far_rows(), e=(0, 0))

    def source(at, row):
        return [image_s[at + row, k] for k in range(groups)] + [image_c[at + row, k] for k in range(groups)]

    for row in range(-HALO_QUENCH, 0):
        fields.put("q0", 0, row, source(HALO_AERIAL + HALO_QUENCH, row))
    for d in range(local):
        rate = -exposure_rate * fields.get("dose", d, 0)[0]
        for row in range(-HALO_AERIAL, 0):
            fields.put("a0", d, row, [1.0 - jnp.exp(rate * v) for v in source(HALO_AERIAL, row)])
        forward_rows(spread, fields, d, table)


def backward_kernel(rows, groups, local, doses, near, far, extra, cot, swap, cot_s, cot_c, *refs):
    outs = refs[: 2 * doses]
    ct, l3, l2, m2, l1, m1, acc, full = refs[2 * doses :]
    half = rows // 2
    area = rows * groups * SUB
    depth = groups * SUB
    inner = half + HALO_COT
    place = lax.axis_index("dose")
    spread = make_spread()

    def around(ref, halo, row):
        return [load(ref, halo, row + i) for i in (-1, 0, 1)]

    for d in range(local):
        more = {}
        fields = Fields(rows, local, near, far, more)
        rate = -exposure_rate * fields.get("dose", d, 0)[0]
        light = [extra[side, k] for side in range(2) for k in range(groups)]
        more["a0", d, rows] = [1.0 - jnp.exp(rate * v) for v in light]
        for n in range(3):
            row = rows - 1 - n
            more["a%d" % (n + 1), d, row] = next_acid(spread, fields, d, n, row)[0]
        for n, row in ((3, half + 2), (2, half + 1)):
            left = left_of(fields.get("a%d" % (5 - n), d, row))
            more["c%d" % n, d, row] = [v * m for v, m in zip(fields.get("c%d" % n, d, row), left)]

        for row in range(-3, half + 3):
            if row < 0:
                at = d * HALO_COT + HALO_COT + row
                value = [cot_s[at, k] for k in range(groups)] + [cot_c[at, k] for k in range(groups)]
            else:
                value = [vector(cot, rows, groups, k, chip_row(rows, row), d * area) for k in range(groups)]
                value += [swap[2 * rows + d * inner + row, k] for k in range(groups)]
            save(ct, 3, row, value)
            save(l3, 3, row, [c * v for c, v in zip(fields.get("c3", d, row), value)])

        def step(ref, halo, row, both, n):
            above, center, below = around(ref, halo, row)
            new = spread(above, center, below, acid_lateral, acid_depth)
            parts = zip(new, fields.get("q%d" % n, d, row), both, fields.get("c%d" % n, d, row), load(ct, 3, row))
            return [v - q * (neutral_rate * s) + c * t for v, q, s, c, t in parts]

        for row in range(-2, half + 2):
            old = load(l3, 3, row)
            save(l2, 2, row, step(l3, 3, row, old, 2))
            if -1 <= row < half + 1:
                save(m2, 1, row, [-(neutral_rate * a * s) for a, s in zip(fields.get("a2", d, row), old)])
        for row in range(-1, half + 1):
            both = [a + b for a, b in zip(load(l2, 2, row), load(m2, 1, row))]
            save(l1, 1, row, step(l2, 2, row, both, 1))
            if 0 <= row < half:
                new = spread(*around(m2, 1, row), base_lateral, base_depth)
                parts = zip(new, fields.get("a1", d, row), both)
                save(m1, 0, row, [v - a * (neutral_rate * s) for v, a, s in parts])
        for row in range(half):
            both = [a + b for a, b in zip(load(l1, 1, row), load(m1, 0, row))]
            value = [v * e for v, e in zip(step(l1, 1, row, both, 0), fields.get("e", d, row))]
            if d > 0:
                value = [v + w for v, w in zip(value, load(acc, 0, row))]
            if d + 1 < local:
                save(acc, 0, row, value)
            else:
                for i in range(2 * groups):
                    side, k = divmod(i, groups)
                    full[side, row, pl.ds(k, SUB, stride=groups), :] = value[i]

    piece = depth // doses
    for side in range(2):
        for k in range(doses):
            start = pl.multiple_of(lax.rem(place + k, doses) * piece, SUB)
            for row in range(half):
                outs[side * doses + k][row] = full[side, row, pl.ds(start, piece), :]


def join_kernel(rows, piece, doses, *refs):
    parts, out = refs[:-1], refs[-1]
    half = rows // 2
    core = lax.axis_index("ty")
    for side in range(2):
        for row in range(half):
            owner = core + side * (1 - 2 * core)
            at = row + owner * (rows - 1 - 2 * row)
            for g in range(piece // SUB):
                value = parts[side * doses][row, pl.ds(g * SUB, SUB), :]
                for k in range(1, doses):
                    value = value + parts[side * doses + k][row, pl.ds(g * SUB, SUB), :]
                out[pl.ds(g * SUB * rows + at, SUB, stride=rows), :] = value


def gradient(aerial_image, quencher, cotangent, dose_levels, dose_index):
    depth, rows, lanes = aerial_image.shape
    local = cotangent.shape[0]
    groups = depth // SUB
    half = rows // 2
    doses = lax.axis_size("dose")
    ring = lax.axis_size("tx")
    assert rows == half + HALO_QUENCH and HALO_AERIAL == HALO_QUENCH + 1
    f32 = jnp.float32
    aerial = aerial_image.reshape(depth * rows, lanes)
    quench = quencher.reshape(depth * rows, lanes)
    cot = cotangent.reshape(local * depth * rows, lanes)
    vmem = pl.BlockSpec(memory_space=pltpu.VMEM)
    smem = pl.BlockSpec(memory_space=pltpu.SMEM)

    def call(kernel, fixed, args, outs, scratch=(), scalars=0, flops=0, space=pltpu.VMEM):
        def body(*refs):
            kernel(*fixed, *refs)

        moved = sum(4 * x.size for x in list(args) + list(outs))
        return pl.pallas_call(
            body,
            out_shape=tuple(outs),
            in_specs=[smem] * scalars + [pl.BlockSpec(memory_space=space)] * (len(args) - scalars),
            out_specs=(vmem,) * len(outs),
            scratch_shapes=list(scratch),
            compiler_params=pltpu.CompilerParams(vmem_limit_bytes=LIMIT),
            cost_estimate=pl.CostEstimate(flops=flops, bytes_accessed=moved, transcendentals=0),
        )(*args)

    def field(n, vectors=groups):
        return jax.ShapeDtypeStruct((n, vectors, SUB, lanes), f32)

    def scratch(halo):
        return pltpu.VMEM((half + 2 * halo, 2 * groups, SUB, lanes), f32)

    def device(t, c):
        return (t % ring) * 2 + c

    straight = [(device(t, c), device(t + 1 - 2 * c, c)) for t in range(ring) for c in range(2)]
    crossed = [(device(t, c), device(t - 1 + 2 * c, 1 - c)) for t in range(ring) for c in range(2)]
    across = [(0, 1), (1, 0)]

    def along(value, pairs):
        return lax.ppermute(value, ("tx", "ty"), pairs)

    n_image = HALO_AERIAL + HALO_QUENCH
    n_cot = local * HALO_COT
    n_swap = 2 * rows + local * (half + HALO_COT)
    flat = [jax.ShapeDtypeStruct(x.shape, f32) for x in (aerial, quench, cot)]
    sends = [field(n) for n in (n_image, n_image, n_cot, n_cot, n_swap)]
    image_s, image_c, cot_s, cot_c, swap, aerial, quench, cot = call(
        pack_kernel,
        (rows, groups, local),
        [pltpu.with_memory_space_constraint(x, pltpu.HBM) for x in (aerial, quench, cot)],
        sends + flat,
        [pltpu.SemaphoreType.DMA((3,))],
        space=pltpu.HBM,
    )
    image_s = along(image_s, straight)
    image_c = along(image_c, crossed)
    swap = lax.ppermute(swap, "ty", across)
    cot_s = along(cot_s, straight)
    cot_c = along(cot_c, crossed)

    (near,) = call(
        near_kernel,
        (rows, groups, local),
        (dose_levels, dose_index, aerial, quench, swap),
        (field(places_of(near_rows(rows), local)[1], 2 * groups),),
        scalars=2,
        flops=10_000_000,
    )
    last = HALO_AERIAL - 1
    extra = jnp.concatenate((image_c[last : last + 1], image_s[last : last + 1]), axis=0)
    extra = lax.ppermute(extra, "ty", across)
    (far,) = call(
        far_kernel,
        (rows, groups, local),
        (near, image_s, image_c),
        (field(places_of(far_rows(), local)[1], 2 * groups),),
        flops=10_000_000,
    )
    piece = depth // doses
    parts = call(
        backward_kernel,
        (rows, groups, local, doses),
        (near, far, extra, cot, swap, cot_s, cot_c),
        (jax.ShapeDtypeStruct((half, piece, lanes), f32),) * (2 * doses),
        [scratch(h) for h in (3, 3, 2, 1, 1, 0, 0)] + [pltpu.VMEM((2, half, depth, lanes), f32)],
        flops=10_000_000,
    )

    arrived = []
    for side in range(2):
        for k in range(doses):
            part = parts[side * doses + k]
            if side or k:
                pairs = [(c * doses + d, (c ^ side) * doses + (d + k) % doses) for d in range(doses) for c in range(2)]
                part = lax.ppermute(part, ("ty", "dose"), pairs)
            arrived.append(part)
    (out,) = call(join_kernel, (rows, piece, doses), arrived, (jax.ShapeDtypeStruct((piece * rows, lanes), f32),))
    return out.reshape(piece, rows, lanes)


def solution(mesh):
    placed = (
        P("focus", "tx", "ty"),
        P(None, "tx", "ty"),
        P(("focus", "dose"), None, "tx", "ty"),
        P(),
        P(("focus", "dose")),
    )
    return jax.shard_map(
        gradient,
        mesh=mesh,
        in_specs=placed,
        out_specs=P(("focus", "dose"), "tx", "ty"),
        check_vma=False,
    )
```

time: 28.4 us -> 26.5 us (0.933)
  local copies, waits for them, and re-layouts: 4.08 us -> 1.31 us
  Pallas kernels: 5.09 us -> 6.05 us
  starting transfers between devices: 9.66 us -> 9.06 us
  waiting for transfers between devices: 9.28 us -> 9.83 us
    unnamed x12 -> x4, local copies, waits for them, and re-layouts: 4.07 us -> 1.31 us
    ppermute x4, waiting for transfers between devices: 5.94 us -> 6.92 us  [along(): return lax.ppermute(value, ('tx', 'ty'), pairs)]
    pallas_call x5, Pallas kernels: 5.09 us -> 6.05 us  [call(): pl.pallas_call(body, out_shape=tuple(outs), in_specs=[smem] * scalars + [...]
    ppermute x5, waiting for transfers between devices: 3.34 us -> 2.91 us  [the longest x3 2.9 us: gradient(): part = lax.ppermute(part, ('ty', 'dose'), pairs)]
    ppermute x5, starting transfers between devices: 3.16 us -> 2.76 us  [the longest x3 2.2 us: gradient(): part = lax.ppermute(part, ('ty', 'dose'), pairs)]
  transfers between devices with their start and end apart: 9 -> 9, of which waited for: 5 -> 4; matrix products, arithmetic and copies ran while one was open for 0% -> 0% of each run, Pallas kernels for 11% -> 10%
where the time goes in v3:
time: 26.5 us; the launch traced here: 26.3 us
  waiting for transfers between devices  9.83 us (37%)
  starting transfers between devices  9.06 us (34%)
  Pallas kernels  6.05 us (23%)
  local copies, waits for them, and re-layouts  1.31 us (5%)
    ppermute x4, waiting for transfers between devices, along(): return lax.ppermute(value, ('tx', 'ty'), pairs)  6.92 us
    ppermute x4, starting transfers between devices, along(): return lax.ppermute(value, ('tx', 'ty'), pairs)  6.3 us
    pallas_call x5, Pallas kernels, call(): pl.pallas_call(body, out_shape=tuple(outs), in_specs=[smem] * scalars + [...  6.05 us
    ppermute x3, waiting for transfers between devices, gradient(): part = lax.ppermute(part, ('ty', 'dose'), pairs)  2.9 us
    ppermute x3, starting transfers between devices, gradient(): part = lax.ppermute(part, ('ty', 'dose'), pairs)  2.2 us
    unnamed x4, local copies, waits for them, and re-layouts  1.31 us
    ppermute x1, starting transfers between devices, gradient(): swap = lax.ppermute(swap, 'ty', across)  0.56 us
  transfers between devices with their start and end apart: 9, of which 4 were waited for; matrix products, arithmetic and copies ran while one was open for 0% of the time, Pallas kernels for 10%

profile of v3, /device:TPU:0, one launch (start us, length us, event | category | flops | bytes accessed | tf_op | source)
XLA Modules:
  0.0 26.3 jit_solution(9681784403392431219)
XLA Ops:
  0.0 1.6 %shard_map.55 = (f32[9,4,8,128]{3,2,1,0:T(8,128)S(1)}, f32[9,4,8,128]{3,2,1,0:T(8,128)S(1)}, f32[6,4,8,128]{3,2,1,0:T(8,128)S(1)}, f32[6,4,8,128]{3,2,1,0:T(8,12...) custom-call(f32[256,128]{1,0:T(8,128)} %bitcast.5, ...), custom_call_target="tpu_custom_call" | custom-call | bytes 2031616 | tf_op jit(solution)/shard_map/pallas_call | solution.py:377
  1.6 0.6 %collective-permute-start = (f32[30,4,8,128]{3,2,1,0:T(8,128)S(1)}, f32[30,4,8,128]{3,2,1,0:T(8,128)S(1)}, u32[]{:S(2)}, u32[]{:S(2)}) collective-permute-start(f32[30,4,8,128]{3,2,1,0:T(8,128)S(1)} %get-tuple-element.19), channel_id=1, source_target_pairs={{0,2},{2,0},{1,3},{3,1},{4,6},{6,4},{5,7},{7,5},{8,10},{10,8},{9,1... | collective-permute-start | bytes 1474568 | tf_op jit(solution)/shard_map/ppermute | solution.py:418
  2.1 4.7 %collective-permute-start.2 = (f32[9,4,8,128]{3,2,1,0:T(8,128)S(1)}, f32[9,4,8,128]{3,2,1,0:T(8,128)S(1)}, u32[]{:S(2)}, u32[]{:S(2)}) collective-permute-start(f32[9,4,8,128]{3,2,1,0:T(8,128)S(1)} %get-tuple-element.21), channel_id=1, source_target_pairs={{0,14},{2,4},{4,2},{6,8},{8,6},{10,12},{12,10},{14,0},{1,15},{3,5}... | collective-permute-start | bytes 442376 | tf_op jit(solution)/shard_map/ppermute | solution.py:401
  6.8 0.0 collective-permute-start.1
  6.8 0.0 collective-permute-start.4
  6.8 1.6 %collective-permute-start.5 = (f32[6,4,8,128]{3,2,1,0:T(8,128)S(1)}, f32[6,4,8,128]{3,2,1,0:T(8,128)S(1)}, u32[]{:S(2)}, u32[]{:S(2)}) collective-permute-start(f32[6,4,8,128]{3,2,1,0:T(8,128)S(1)} %get-tuple-element.24), channel_id=1, source_target_pairs={{0,14},{2,4},{4,2},{6,8},{8,6},{10,12},{12,10},{14,0},{1,15},{3,5}... | collective-permute-start | bytes 294920 | tf_op jit(solution)/shard_map/ppermute | solution.py:401
  8.4 2.7 %collective-permute-done.2.refs_2_ = f32[9,4,8,128]{3,2,1,0:T(8,128)S(1)} collective-permute-done((f32[9,4,8,128]{3,2,1,0:T(8,128)S(1)}, f32[9,4,8,128]{3,2,1,0:T(8,128)S(1)}, u32[]{:S(2)}, u32[]{:S(2)}) %collective-permute-start.2) | collective-permute-done | bytes 147488 | tf_op jit(solution)/shard_map/ppermute | solution.py:401
  11.1 4.2 %collective-permute-done.1.refs_1_ = f32[9,4,8,128]{3,2,1,0:T(8,128)S(1)} collective-permute-done((f32[9,4,8,128]{3,2,1,0:T(8,128)S(1)}, f32[9,4,8,128]{3,2,1,0:T(8,128)S(1)}, u32[]{:S(2)}, u32[]{:S(2)}) %collective-permute-start.1) | collective-permute-done | bytes 147488 | tf_op jit(solution)/shard_map/ppermute | solution.py:401
  15.4 0.0 collective-permute-start.3
  15.4 0.0 collective-permute-done.refs_4_
  15.4 0.0 copy-start
  15.4 0.6 %copy-done = f32[16]{0:T(128)S(1)} copy-done((f32[16]{0:T(128)S(1)}, f32[16]{0:T(128)}, u32[]{:S(2)}) %copy-start) | copy-done | bytes 88
  16.0 0.0 copy-start.1
  16.0 0.7 %copy-done.1 = s32[2]{0:T(128)S(1)} copy-done((s32[2]{0:T(128)S(1)}, s32[2]{0:T(128)}, u32[]{:S(2)}) %copy-start.1) | copy-done | bytes 32
  16.7 1.6 %shard_map.56.refs_0_ = f32[100,8,8,128]{3,2,1,0:T(8,128)S(1)} custom-call(f32[16]{0:T(128)S(1)} %copy-done, s32[2]{0:T(128)S(1)} %copy-done.1, f32[256,128]{1,0:T(8,128)S(1)} %get-tuple-element.17.refs_2_, f32[256,128]{1,0:T(8,128)S(1)} %get-tuple-element.18.refs_3_, f32[30,4,8,128]{3,2,1,0:T(8,128)S(1)} %collective-permute-done.refs_4_), custom_call_target="tpu_custom_call" | custom-call | flops 10000000 | bytes 4030536 | tf_op jit(solution)/shard_map/pallas_call | solution.py:377
  18.3 1.1 %shard_map.57.refs_1_ = f32[94,8,8,128]{3,2,1,0:T(8,128)S(1)} custom-call(f32[100,8,8,128]{3,2,1,0:T(8,128)S(1)} %shard_map.56.refs_0_, f32[9,4,8,128]{3,2,1,0:T(8,128)S(1)} %collective-permute-done.1.refs_1_, f32[9,4,8,128]{3,2,1,0:T(8,128)S(1)} %collective-permute-done.2.refs_2_), custom_call_target="tpu_custom_call" | custom-call | flops 10000000 | bytes 6651904 | tf_op jit(solution)/shard_map/pallas_call | solution.py:377
  19.4 0.0 collective-permute-done.4.refs_5_
  19.4 0.0 collective-permute-done.5.refs_6_
  19.4 0.0 collective-permute-done.3.refs_2_
  19.4 1.2 %shard_map.58 = (f32[4,16,128]{2,1,0:T(8,128)S(1)}, f32[4,16,128]{2,1,0:T(8,128)S(1)}, f32[4,16,128]{2,1,0:T(8,128)S(1)}, f32[4,16,128]{2,1,0:T(8,128)S(1)}) custom-call(f32[100,8,8,128]{3,2,1,0:T(8,128)S(1)} %shard_map.56.refs_0_, f32[94,8,8,128]{3,2,1,0:T(8,128)S(1)} %shard_map.57.refs_1_, f32[2,4,8,128]{3,2,1,0:T(8,128)S(1)} %collective-permute-done.3.refs_2_, ...), custom_call_target="tpu_custom_call" | custom-call | flops 10000000 | bytes 7471104 | tf_op jit(solution)/shard_map/pallas_call | solution.py:377
  20.6 1.6 %collective-permute-start.6 = (f32[4,16,128]{2,1,0:T(8,128)S(1)}, f32[4,16,128]{2,1,0:T(8,128)S(1)}, u32[]{:S(2)}, u32[]{:S(2)}) collective-permute-start(f32[4,16,128]{2,1,0:T(8,128)S(1)} %get-tuple-element.26), channel_id=1, source_target_pairs={{0,1},{2,3},{1,0},{3,2},{4,5},{6,7},{5,4},{7,6},{8,9},{10,11},{9,8... | collective-permute-start | bytes 98312 | tf_op jit(solution)/shard_map/ppermute | solution.py:456
  22.1 0.2 collective-permute-start.7
  22.3 0.4 %collective-permute-start.8 = (f32[4,16,128]{2,1,0:T(8,128)S(1)}, f32[4,16,128]{2,1,0:T(8,128)S(1)}, u32[]{:S(2)}, u32[]{:S(2)}) collective-permute-start(f32[4,16,128]{2,1,0:T(8,128)S(1)} %get-tuple-element.28), channel_id=1, source_target_pairs={{0,3},{2,1},{1,2},{3,0},{4,7},{6,5},{5,6},{7,4},{8,11},{10,9},{9,1... | collective-permute-start | bytes 98312 | tf_op jit(solution)/shard_map/ppermute | solution.py:456
  22.8 1.8 %collective-permute-done.6.refs_1_ = f32[4,16,128]{2,1,0:T(8,128)S(1)} collective-permute-done((f32[4,16,128]{2,1,0:T(8,128)S(1)}, f32[4,16,128]{2,1,0:T(8,128)S(1)}, u32[]{:S(2)}, u32[]{:S(2)}) %collective-permute-start.6) | collective-permute-done | bytes 32800 | tf_op jit(solution)/shard_map/ppermute | solution.py:456
  24.6 0.0 collective-permute-done.7.refs_2_
  24.6 1.1 %collective-permute-done.8.refs_3_ = f32[4,16,128]{2,1,0:T(8,128)S(1)} collective-permute-done((f32[4,16,128]{2,1,0:T(8,128)S(1)}, f32[4,16,128]{2,1,0:T(8,128)S(1)}, u32[]{:S(2)}, u32[]{:S(2)}) %collective-permute-start.8) | collective-permute-done | bytes 32800 | tf_op jit(solution)/shard_map/ppermute | solution.py:456
  25.7 0.6 %shard_map.59 = f32[128,128]{1,0:T(8,128)} custom-call(f32[4,16,128]{2,1,0:T(8,128)S(1)} %get-tuple-element.25.refs_0_, f32[4,16,128]{2,1,0:T(8,128)S(1)} %collective-permute-done.6.refs_1_, f32[4,16,128]{2,1,0:T(8,128)S(1)} %collective-permute-done.7.refs_2_, f32[4,16,128]{2,1,0:T(8,128)S(1)} %collective-permute-done.8.refs_3_), custom_call_target="tpu_custom_call" | custom-call | bytes 196608 | tf_op jit(solution)/shard_map/pallas_call | solution.py:377
  (3 shorter events, 0.0 us)
Async XLA Ops:
  1.6 13.8 %collective-permute-start = (f32[30,4,8,128]{3,2,1,0:T(8,128)S(1)}, f32[30,4,8,128]{3,2,1,0:T(8,128)S(1)}, u32[]{:S(2)}, u32[]{:S(2)}) collective-permute-start(f32[30,4,8,128]{3,2,1,0:T(8,128)S(1)} %get-tuple-element.19), channel_id=1, source_target_pairs={{0,2},{2,0},{1,3},{3,1},{4,6},{6,4},{5,7},{7,5},{8,10},{10,8},{9,1... | collective-permute-start | bytes 1474568 | tf_op jit(solution)/shard_map/ppermute | solution.py:418
  2.1 9.0 %collective-permute-start.2 = (f32[9,4,8,128]{3,2,1,0:T(8,128)S(1)}, f32[9,4,8,128]{3,2,1,0:T(8,128)S(1)}, u32[]{:S(2)}, u32[]{:S(2)}) collective-permute-start(f32[9,4,8,128]{3,2,1,0:T(8,128)S(1)} %get-tuple-element.21), channel_id=1, source_target_pairs={{0,14},{2,4},{4,2},{6,8},{8,6},{10,12},{12,10},{14,0},{1,15},{3,5}... | collective-permute-start | bytes 442376 | tf_op jit(solution)/shard_map/ppermute | solution.py:401
  6.8 8.5 %collective-permute-start.1 = (f32[9,4,8,128]{3,2,1,0:T(8,128)S(1)}, f32[9,4,8,128]{3,2,1,0:T(8,128)S(1)}, u32[]{:S(2)}, u32[]{:S(2)}) collective-permute-start(f32[9,4,8,128]{3,2,1,0:T(8,128)S(1)} %get-tuple-element.20), channel_id=1, source_target_pairs={{0,4},{2,14},{4,8},{6,2},{8,12},{10,6},{12,0},{14,10},{1,5},{3,15}... | collective-permute-start | bytes 442376 | tf_op jit(solution)/shard_map/ppermute | solution.py:401
  6.8 12.5 %collective-permute-start.4 = (f32[6,4,8,128]{3,2,1,0:T(8,128)S(1)}, f32[6,4,8,128]{3,2,1,0:T(8,128)S(1)}, u32[]{:S(2)}, u32[]{:S(2)}) collective-permute-start(f32[6,4,8,128]{3,2,1,0:T(8,128)S(1)} %get-tuple-element.23), channel_id=1, source_target_pairs={{0,4},{2,14},{4,8},{6,2},{8,12},{10,6},{12,0},{14,10},{1,5},{3,15}... | collective-permute-start | bytes 294920 | tf_op jit(solution)/shard_map/ppermute | solution.py:401
  6.8 12.5 %collective-permute-start.5 = (f32[6,4,8,128]{3,2,1,0:T(8,128)S(1)}, f32[6,4,8,128]{3,2,1,0:T(8,128)S(1)}, u32[]{:S(2)}, u32[]{:S(2)}) collective-permute-start(f32[6,4,8,128]{3,2,1,0:T(8,128)S(1)} %get-tuple-element.24), channel_id=1, source_target_pairs={{0,14},{2,4},{4,2},{6,8},{8,6},{10,12},{12,10},{14,0},{1,15},{3,5}... | collective-permute-start | bytes 294920 | tf_op jit(solution)/shard_map/ppermute | solution.py:401
  15.4 4.0 %collective-permute-start.3 = (f32[2,4,8,128]{3,2,1,0:T(8,128)S(1)}, f32[2,4,8,128]{3,2,1,0:T(8,128)S(1)}, u32[]{:S(2)}, u32[]{:S(2)}) collective-permute-start(f32[2,4,8,128]{3,2,1,0:T(8,128)S(1)} %pad_maximum_fusion), channel_id=1, source_target_pairs={{0,2},{2,0},{1,3},{3,1},{4,6},{6,4},{5,7},{7,5},{8,10},{10,8},{9,1... | collective-permute-start | bytes 98312 | tf_op jit(solution)/shard_map/ppermute | solution.py:432
  15.4 0.7 %copy-start = (f32[16]{0:T(128)S(1)}, f32[16]{0:T(128)}, u32[]{:S(2)}) copy-start(f32[16]{0:T(128)} %refs_0_.1) | copy-start | bytes 196
  16.0 0.7 %copy-start.1 = (s32[2]{0:T(128)S(1)}, s32[2]{0:T(128)}, u32[]{:S(2)}) copy-start(s32[2]{0:T(128)} %refs_1_.1) | copy-start | bytes 28
  20.6 4.0 %collective-permute-start.6 = (f32[4,16,128]{2,1,0:T(8,128)S(1)}, f32[4,16,128]{2,1,0:T(8,128)S(1)}, u32[]{:S(2)}, u32[]{:S(2)}) collective-permute-start(f32[4,16,128]{2,1,0:T(8,128)S(1)} %get-tuple-element.26), channel_id=1, source_target_pairs={{0,1},{2,3},{1,0},{3,2},{4,5},{6,7},{5,4},{7,6},{8,9},{10,11},{9,8... | collective-permute-start | bytes 98312 | tf_op jit(solution)/shard_map/ppermute | solution.py:456
  22.1 2.4 %collective-permute-start.7 = (f32[4,16,128]{2,1,0:T(8,128)S(1)}, f32[4,16,128]{2,1,0:T(8,128)S(1)}, u32[]{:S(2)}, u32[]{:S(2)}) collective-permute-start(f32[4,16,128]{2,1,0:T(8,128)S(1)} %get-tuple-element.27), channel_id=1, source_target_pairs={{0,2},{2,0},{1,3},{3,1},{4,6},{6,4},{5,7},{7,5},{8,10},{10,8},{9,1... | collective-permute-start | bytes 98312 | tf_op jit(solution)/shard_map/ppermute | solution.py:456
  22.3 3.3 %collective-permute-start.8 = (f32[4,16,128]{2,1,0:T(8,128)S(1)}, f32[4,16,128]{2,1,0:T(8,128)S(1)}, u32[]{:S(2)}, u32[]{:S(2)}) collective-permute-start(f32[4,16,128]{2,1,0:T(8,128)S(1)} %get-tuple-element.28), channel_id=1, source_target_pairs={{0,3},{2,1},{1,2},{3,0},{4,7},{6,5},{5,6},{7,4},{8,11},{10,9},{9,1... | collective-permute-start | bytes 98312 | tf_op jit(solution)/shard_map/ppermute | solution.py:456

commit v4 on v3

--- a/solution.py
+++ b/solution.py
@@ -29,16 +29,11 @@
     return ref[pl.ds(base + rows * k + row, SUB, stride=rows * groups), :]
 
 
-def pack_kernel(rows, groups, local, *refs):
-    image_hbm, quench_hbm, cot_hbm = refs[:3]
-    image_s, image_c, cot_s, cot_c, swap, aerial, quench, cot = refs[3:11]
-    sems = refs[11]
+def image_kernel(rows, groups, image_hbm, quench_hbm, cot_hbm, image_s, image_c, aerial, quench, cot, sems):
     pairs = ((image_hbm, aerial), (quench_hbm, quench), (cot_hbm, cot))
     copies = [pltpu.make_async_copy(src, dst, sems.at[i]) for i, (src, dst) in enumerate(pairs)]
     for copy in copies:
         copy.start()
-    area = rows * groups * SUB
-    inner = rows // 2 + HALO_COT
     copies[0].wait()
     copies[1].wait()
     place = 0
@@ -49,6 +44,11 @@
                 image_c[place, k] = vector(src, rows, groups, k, chip_row(rows, width - 1 - i))
             place += 1
     copies[2].wait()
+
+
+def rest_kernel(rows, groups, local, aerial, quench, cot, cot_s, cot_c, swap):
+    area = rows * groups * SUB
+    inner = rows // 2 + HALO_COT
     for d in range(local):
         for i in range(HALO_COT):
             for k in range(groups):
@@ -62,15 +62,6 @@
             for k in range(groups):
                 swap[place, k] = vector(src, rows, groups, k, chip_row(rows, rows - 1 - i), base)
             place += 1
-
-
-def load(ref, halo, row):
-    return [ref[row + halo, i] for i in range(ref.shape[1])]
-
-
-def save(ref, halo, row, value):
-    for i in range(len(value)):
-        ref[row + halo, i] = value[i]
 
 
 def make_spread():
@@ -125,7 +116,7 @@
     }
 
 
-def far_rows():
+def far_rows(rows):
     return {
         "q0": (-4, 0),
         "a0": (-5, 0),
@@ -154,12 +145,35 @@
     return places, total
 
 
+def back_near_rows(rows):
+    half = rows // 2
+    return {
+        "ct": (0, half + 3),
+        "l3": (0, half + 3),
+        "l2": (1, half + 2),
+        "m2": (0, half + 1),
+        "l1": (2, half + 1),
+        "m1": (1, half),
+        "g": (3, half),
+    }
+
+
+def back_far_rows(rows):
+    return {
+        "ct": (-3, 0),
+        "l3": (-3, 0),
+        "l2": (-2, 1),
+        "m2": (-1, 0),
+        "l1": (-1, 2),
+        "m1": (0, 1),
+        "g": (0, 3),
+    }
+
+
 class Fields:
-    def __init__(self, rows, local, near, far=None, more=None):
-        self.stores = [(near, places_of(near_rows(rows), local)[0])]
-        if far is not None:
-            self.stores.append((far, places_of(far_rows(), local)[0]))
-        self.more = {} if more is None else more
+    def __init__(self, rows, local, *stores):
+        self.stores = [(ref, places_of(table(rows), local)[0]) for ref, table in stores]
+        self.more = {}
 
     def get(self, name, d, row):
         if (name, d, row) in self.more:
@@ -170,6 +184,9 @@
                 return [ref[at, i] for i in range(ref.shape[1])]
         raise KeyError((name, row))
 
+    def around(self, name, d, row):
+        return [self.get(name, d, row + i) for i in (-1, 0, 1)]
+
     def put(self, name, d, row, value):
         ref, places = self.stores[-1]
         at = places[name, d, row]
@@ -183,7 +200,7 @@
 
 def next_acid(spread, fields, d, n, row):
     name = "a%d" % n
-    above, center, below = (fields.get(name, d, row + i) for i in (-1, 0, 1))
+    above, center, below = fields.around(name, d, row)
     quench = fields.get("q%d" % n, d, row)
     new = spread(above, center, below, acid_lateral, acid_depth)
     reaction = [neutral_rate * a * q for a, q in zip(center, quench)]
@@ -200,8 +217,7 @@
                 q_first, q_end = table["q%d" % (n + 1)]
                 if q_first <= row < q_end:
                     name = "q%d" % n
-                    above, center, below = (fields.get(name, d, row + i) for i in (-1, 0, 1))
-                    new = spread(above, center, below, base_lateral, base_depth)
+                    new = spread(*fields.around(name, d, row), base_lateral, base_depth)
                     fields.put("q%d" % (n + 1), d, row, [v - r for v, r in zip(new, reaction)])
 
     first = min(table[c][0] for c in ("c3", "c2", "c1", "c0"))
@@ -228,7 +244,7 @@
 def near_kernel(rows, groups, local, levels, index, aerial, quench, swap, near):
     half = rows // 2
     spread = make_spread()
-    fields = Fields(rows, local, near)
+    fields = Fields(rows, local, (near, near_rows))
 
     def source(raw, at, row):
         own = [vector(raw, rows, groups, k, chip_row(rows, row)) for k in range(groups)]
@@ -250,8 +266,8 @@
 
 def far_kernel(rows, groups, local, near, image_s, image_c, far):
     spread = make_spread()
-    fields = Fields(rows, local, near, far)
-    table = dict(far_rows(), e=(0, 0))
+    fields = Fields(rows, local, (near, near_rows), (far, far_rows))
+    table = dict(far_rows(rows), e=(0, 0))
 
     def source(at, row):
         return [image_s[at + row, k] for k in range(groups)] + [image_c[at + row, k] for k in range(groups)]
@@ -265,72 +281,84 @@
         forward_rows(spread, fields, d, table)
 
 
-def backward_kernel(rows, groups, local, doses, near, far, extra, cot, swap, cot_s, cot_c, *refs):
+def backward_rows(spread, past, back, d, table):
+    def step(name, row, both, n):
+        new = spread(*back.around(name, d, row), acid_lateral, acid_depth)
+        parts = zip(new, past.get("q%d" % n, d, row), both, past.get("c%d" % n, d, row), back.get("ct", d, row))
+        return [v - q * (neutral_rate * s) + c * t for v, q, s, c, t in parts]
+
+    for row in range(*table["l3"]):
+        back.put("l3", d, row, [c * v for c, v in zip(past.get("c3", d, row), back.get("ct", d, row))])
+    for row in range(*table["m2"]):
+        parts = zip(past.get("a2", d, row), back.get("l3", d, row))
+        back.put("m2", d, row, [-(neutral_rate * a * s) for a, s in parts])
+    for row in range(*table["l2"]):
+        back.put("l2", d, row, step("l3", row, back.get("l3", d, row), 2))
+    for n, name in ((1, "l1"), (0, "g")):
+        old, side = ("l2", "m2") if n else ("l1", "m1")
+        wanted = set(range(*table[name]))
+        if n:
+            wanted |= set(range(*table["m1"]))
+        for row in sorted(wanted):
+            both = [a + b for a, b in zip(back.get(old, d, row), back.get(side, d, row))]
+            if row in range(*table[name]):
+                new = step(old, row, both, n)
+                if n == 0:
+                    new = [v * e for v, e in zip(new, past.get("e", d, row))]
+                back.put(name, d, row, new)
+            if n and row in range(*table["m1"]):
+                new = spread(*back.around("m2", d, row), base_lateral, base_depth)
+                parts = zip(new, past.get("a1", d, row), both)
+                back.put("m1", d, row, [v - a * (neutral_rate * s) for v, a, s in parts])
+
+
+def back_near_kernel(rows, groups, local, near, far, extra, cot, swap, back_near):
+    half = rows // 2
+    area = rows * groups * SUB
+    inner = half + HALO_COT
+    spread = make_spread()
+    for d in range(local):
+        past = Fields(rows, local, (near, near_rows), (far, far_rows))
+        rate = -exposure_rate * past.get("dose", d, 0)[0]
+        light = [extra[side, k] for side in range(2) for k in range(groups)]
+        past.more["a0", d, rows] = [1.0 - jnp.exp(rate * v) for v in light]
+        for n in range(3):
+            row = rows - 1 - n
+            past.more["a%d" % (n + 1), d, row] = next_acid(spread, past, d, n, row)[0]
+        for n, row in ((3, half + 2), (2, half + 1)):
+            left = left_of(past.get("a%d" % (5 - n), d, row))
+            past.more["c%d" % n, d, row] = [v * m for v, m in zip(past.get("c%d" % n, d, row), left)]
+        back = Fields(rows, local, (back_near, back_near_rows))
+        table = back_near_rows(rows)
+        for row in range(*table["ct"]):
+            value = [vector(cot, rows, groups, k, chip_row(rows, row), d * area) for k in range(groups)]
+            back.put("ct", d, row, value + [swap[2 * rows + d * inner + row, k] for k in range(groups)])
+        backward_rows(spread, past, back, d, table)
+
+
+def back_far_kernel(rows, groups, local, doses, near, far, back_near, cot_s, cot_c, *refs):
     outs = refs[: 2 * doses]
-    ct, l3, l2, m2, l1, m1, acc, full = refs[2 * doses :]
-    half = rows // 2
-    area = rows * groups * SUB
+    store, full = refs[2 * doses :]
+    half = rows // 2
     depth = groups * SUB
-    inner = half + HALO_COT
     place = lax.axis_index("dose")
     spread = make_spread()
-
-    def around(ref, halo, row):
-        return [load(ref, halo, row + i) for i in (-1, 0, 1)]
-
+    past = Fields(rows, local, (near, near_rows), (far, far_rows))
+    back = Fields(rows, local, (back_near, back_near_rows), (store, back_far_rows))
+    table = back_far_rows(rows)
     for d in range(local):
-        more = {}
-        fields = Fields(rows, local, near, far, more)
-        rate = -exposure_rate * fields.get("dose", d, 0)[0]
-        light = [extra[side, k] for side in range(2) for k in range(groups)]
-        more["a0", d, rows] = [1.0 - jnp.exp(rate * v) for v in light]
-        for n in range(3):
-            row = rows - 1 - n
-            more["a%d" % (n + 1), d, row] = next_acid(spread, fields, d, n, row)[0]
-        for n, row in ((3, half + 2), (2, half + 1)):
-            left = left_of(fields.get("a%d" % (5 - n), d, row))
-            more["c%d" % n, d, row] = [v * m for v, m in zip(fields.get("c%d" % n, d, row), left)]
-
-        for row in range(-3, half + 3):
-            if row < 0:
-                at = d * HALO_COT + HALO_COT + row
-                value = [cot_s[at, k] for k in range(groups)] + [cot_c[at, k] for k in range(groups)]
-            else:
-                value = [vector(cot, rows, groups, k, chip_row(rows, row), d * area) for k in range(groups)]
-                value += [swap[2 * rows + d * inner + row, k] for k in range(groups)]
-            save(ct, 3, row, value)
-            save(l3, 3, row, [c * v for c, v in zip(fields.get("c3", d, row), value)])
-
-        def step(ref, halo, row, both, n):
-            above, center, below = around(ref, halo, row)
-            new = spread(above, center, below, acid_lateral, acid_depth)
-            parts = zip(new, fields.get("q%d" % n, d, row), both, fields.get("c%d" % n, d, row), load(ct, 3, row))
-            return [v - q * (neutral_rate * s) + c * t for v, q, s, c, t in parts]
-
-        for row in range(-2, half + 2):
-            old = load(l3, 3, row)
-            save(l2, 2, row, step(l3, 3, row, old, 2))
-            if -1 <= row < half + 1:
-                save(m2, 1, row, [-(neutral_rate * a * s) for a, s in zip(fields.get("a2", d, row), old)])
-        for row in range(-1, half + 1):
-            both = [a + b for a, b in zip(load(l2, 2, row), load(m2, 1, row))]
-            save(l1, 1, row, step(l2, 2, row, both, 1))
-            if 0 <= row < half:
-                new = spread(*around(m2, 1, row), base_lateral, base_depth)
-                parts = zip(new, fields.get("a1", d, row), both)
-                save(m1, 0, row, [v - a * (neutral_rate * s) for v, a, s in parts])
-        for row in range(half):
-            both = [a + b for a, b in zip(load(l1, 1, row), load(m1, 0, row))]
-            value = [v * e for v, e in zip(step(l1, 1, row, both, 0), fields.get("e", d, row))]
-            if d > 0:
-                value = [v + w for v, w in zip(value, load(acc, 0, row))]
-            if d + 1 < local:
-                save(acc, 0, row, value)
-            else:
-                for i in range(2 * groups):
-                    side, k = divmod(i, groups)
-                    full[side, row, pl.ds(k, SUB, stride=groups), :] = value[i]
-
+        for row in range(*table["ct"]):
+            at = d * HALO_COT + HALO_COT + row
+            value = [cot_s[at, k] for k in range(groups)] + [cot_c[at, k] for k in range(groups)]
+            back.put("ct", d, row, value)
+        backward_rows(spread, past, back, d, table)
+    for row in range(half):
+        value = back.get("g", 0, row)
+        for d in range(1, local):
+            value = [v + w for v, w in zip(value, back.get("g", d, row))]
+        for i in range(2 * groups):
+            side, k = divmod(i, groups)
+            full[side, row, pl.ds(k, SUB, stride=groups), :] = value[i]
     piece = depth // doses
     for side in range(2):
         for k in range(doses):
@@ -387,9 +415,6 @@
     def field(n, vectors=groups):
         return jax.ShapeDtypeStruct((n, vectors, SUB, lanes), f32)
 
-    def scratch(halo):
-        return pltpu.VMEM((half + 2 * halo, 2 * groups, SUB, lanes), f32)
-
     def device(t, c):
         return (t % ring) * 2 + c
 
@@ -404,17 +429,18 @@
     n_cot = local * HALO_COT
     n_swap = 2 * rows + local * (half + HALO_COT)
     flat = [jax.ShapeDtypeStruct(x.shape, f32) for x in (aerial, quench, cot)]
-    sends = [field(n) for n in (n_image, n_image, n_cot, n_cot, n_swap)]
-    image_s, image_c, cot_s, cot_c, swap, aerial, quench, cot = call(
-        pack_kernel,
-        (rows, groups, local),
+    image_s, image_c, aerial, quench, cot = call(
+        image_kernel,
+        (rows, groups),
         [pltpu.with_memory_space_constraint(x, pltpu.HBM) for x in (aerial, quench, cot)],
-        sends + flat,
+        [field(n_image), field(n_image)] + flat,
         [pltpu.SemaphoreType.DMA((3,))],
         space=pltpu.HBM,
     )
     image_s = along(image_s, straight)
     image_c = along(image_c, crossed)
+    sends = [field(n) for n in (n_cot, n_cot, n_swap)]
+    cot_s, cot_c, swap = call(rest_kernel, (rows, groups, local), (aerial, quench, cot), sends)
     swap = lax.ppermute(swap, "ty", across)
     cot_s = along(cot_s, straight)
     cot_c = along(cot_c, crossed)
@@ -434,16 +460,26 @@
         far_kernel,
         (rows, groups, local),
         (near, image_s, image_c),
-        (field(places_of(far_rows(), local)[1], 2 * groups),),
+        (field(places_of(far_rows(rows), local)[1], 2 * groups),),
+        flops=10_000_000,
+    )
+    (back_near,) = call(
+        back_near_kernel,
+        (rows, groups, local),
+        (near, far, extra, cot, swap),
+        (field(places_of(back_near_rows(rows), local)[1], 2 * groups),),
         flops=10_000_000,
     )
     piece = depth // doses
     parts = call(
-        backward_kernel,
+        back_far_kernel,
         (rows, groups, local, doses),
-        (near, far, extra, cot, swap, cot_s, cot_c),
+        (near, far, back_near, cot_s, cot_c),
         (jax.ShapeDtypeStruct((half, piece, lanes), f32),) * (2 * doses),
-        [scratch(h) for h in (3, 3, 2, 1, 1, 0, 0)] + [pltpu.VMEM((2, half, depth, lanes), f32)],
+        [
+            pltpu.VMEM((places_of(back_far_rows(rows), local)[1], 2 * groups, SUB, lanes), f32),
+            pltpu.VMEM((2, half, depth, lanes), f32),
+        ],
         flops=10_000_000,
     )
 

time: 26.5 us -> 25.8 us (0.974)
  waiting for transfers between devices: 9.83 us -> 8.34 us
  starting transfers between devices: 9.06 us -> 9.65 us
    ppermute x4, waiting for transfers between devices: 6.92 us -> 5.91 us  [along(): return lax.ppermute(value, ('tx', 'ty'), pairs)]
    ppermute x3, waiting for transfers between devices: 2.9 us -> 2.43 us  [gradient(): part = lax.ppermute(part, ('ty', 'dose'), pairs)]
    ppermute x1, starting transfers between devices: 0.01 us -> 0.43 us  [gradient(): extra = lax.ppermute(extra, 'ty', across)]
    pallas_call x5 -> x7, Pallas kernels: 6.05 us -> 6.26 us  [call(): pl.pallas_call(body, out_shape=tuple(outs), in_specs=[smem] * scalars + [...]
  transfers between devices with their start and end apart: 9 -> 9, of which waited for: 4 -> 4; matrix products, arithmetic and copies ran while one was open for 0% -> 0% of each run, Pallas kernels for 10% -> 13%
where the time goes in v4:
time: 25.8 us; the launch traced here: 25.6 us
  starting transfers between devices  9.65 us (37%)
  waiting for transfers between devices  8.34 us (32%)
  Pallas kernels  6.26 us (24%)
  local copies, waits for them, and re-layouts  1.31 us (5%)
    ppermute x4, starting transfers between devices, along(): return lax.ppermute(value, ('tx', 'ty'), pairs)  6.45 us
    pallas_call x7, Pallas kernels, call(): pl.pallas_call(body, out_shape=tuple(outs), in_specs=[smem] * scalars + [...  6.26 us
    ppermute x4, waiting for transfers between devices, along(): return lax.ppermute(value, ('tx', 'ty'), pairs)  5.91 us
    ppermute x3, waiting for transfers between devices, gradient(): part = lax.ppermute(part, ('ty', 'dose'), pairs)  2.43 us
    ppermute x3, starting transfers between devices, gradient(): part = lax.ppermute(part, ('ty', 'dose'), pairs)  2.21 us
    unnamed x4, local copies, waits for them, and re-layouts  1.31 us
    ppermute x1, starting transfers between devices, gradient(): swap = lax.ppermute(swap, 'ty', across)  0.56 us
  transfers between devices with their start and end apart: 9, of which 4 were waited for; matrix products, arithmetic and copies ran while one was open for 0% of the time, Pallas kernels for 13%

profile of v4, /device:TPU:0, one launch (start us, length us, event | category | flops | bytes accessed | tf_op | source)
XLA Modules:
  0.0 25.6 jit_solution(14489826627282073022)
XLA Ops:
  0.0 1.1 %shard_map.55 = (f32[9,4,8,128]{3,2,1,0:T(8,128)S(1)}, f32[9,4,8,128]{3,2,1,0:T(8,128)S(1)}, f32[256,128]{1,0:T(8,128)S(1)}, f32[256,128]{1,0:T(8,128)S(1)}, f32[512,128]{1,0:T(8,128)S(1)}) custom-call(f32[256,128]{1,0:T(8,128)} %bitcast.5, f32[256,128]{1,0:T(8,128)} %bitcast.6, f32[512,128]{1,0:T(8,128)} %bitcast.4), custom_call_target="tpu_custom_call" | custom-call | bytes 1343488 | tf_op jit(solution)/shard_map/pallas_call | solution.py:405
  1.2 0.4 %shard_map.56 = (f32[6,4,8,128]{3,2,1,0:T(8,128)S(1)}, f32[6,4,8,128]{3,2,1,0:T(8,128)S(1)}, f32[30,4,8,128]{3,2,1,0:T(8,128)S(1)}) custom-call(f32[256,128]{1,0:T(8,128)S(1)} %get-tuple-element.17.refs_0_.refs_2_, f32[256,128]{1,0:T(8,128)S(1)} %get-tuple-element.18.refs_1_.refs_3_, f32[512,128]{1,0:T(8,128)S(1)} %get-tuple-element.19.refs_2_.refs_3_), custom_call_target="tpu_custom_call" | custom-call | bytes 1212416 | tf_op jit(solution)/shard_map/pallas_call | solution.py:405
  1.6 0.6 %collective-permute-start = (f32[30,4,8,128]{3,2,1,0:T(8,128)S(1)}, f32[30,4,8,128]{3,2,1,0:T(8,128)S(1)}, u32[]{:S(2)}, u32[]{:S(2)}) collective-permute-start(f32[30,4,8,128]{3,2,1,0:T(8,128)S(1)} %get-tuple-element.20), channel_id=1, source_target_pairs={{0,2},{2,0},{1,3},{3,1},{4,6},{6,4},{5,7},{7,5},{8,10},{10,8},{9,1... | collective-permute-start | bytes 1474568 | tf_op jit(solution)/shard_map/ppermute | solution.py:444
  2.1 2.6 %collective-permute-start.1 = (f32[9,4,8,128]{3,2,1,0:T(8,128)S(1)}, f32[9,4,8,128]{3,2,1,0:T(8,128)S(1)}, u32[]{:S(2)}, u32[]{:S(2)}) collective-permute-start(f32[9,4,8,128]{3,2,1,0:T(8,128)S(1)} %get-tuple-element.21), channel_id=1, source_target_pairs={{0,4},{2,14},{4,8},{6,2},{8,12},{10,6},{12,0},{14,10},{1,5},{3,15}... | collective-permute-start | bytes 442376 | tf_op jit(solution)/shard_map/ppermute | solution.py:426
  4.8 2.2 %collective-permute-start.2 = (f32[9,4,8,128]{3,2,1,0:T(8,128)S(1)}, f32[9,4,8,128]{3,2,1,0:T(8,128)S(1)}, u32[]{:S(2)}, u32[]{:S(2)}) collective-permute-start(f32[9,4,8,128]{3,2,1,0:T(8,128)S(1)} %get-tuple-element.22), channel_id=1, source_target_pairs={{0,14},{2,4},{4,2},{6,8},{8,6},{10,12},{12,10},{14,0},{1,15},{3,5}... | collective-permute-start | bytes 442376 | tf_op jit(solution)/shard_map/ppermute | solution.py:426
  7.0 1.6 %collective-permute-start.4 = (f32[6,4,8,128]{3,2,1,0:T(8,128)S(1)}, f32[6,4,8,128]{3,2,1,0:T(8,128)S(1)}, u32[]{:S(2)}, u32[]{:S(2)}) collective-permute-start(f32[6,4,8,128]{3,2,1,0:T(8,128)S(1)} %get-tuple-element.23), channel_id=1, source_target_pairs={{0,4},{2,14},{4,8},{6,2},{8,12},{10,6},{12,0},{14,10},{1,5},{3,15}... | collective-permute-start | bytes 294920 | tf_op jit(solution)/shard_map/ppermute | solution.py:426
  8.6 0.0 collective-permute-start.5
  8.6 3.0 %collective-permute-done.1.refs_1_ = f32[9,4,8,128]{3,2,1,0:T(8,128)S(1)} collective-permute-done((f32[9,4,8,128]{3,2,1,0:T(8,128)S(1)}, f32[9,4,8,128]{3,2,1,0:T(8,128)S(1)}, u32[]{:S(2)}, u32[]{:S(2)}) %collective-permute-start.1) | collective-permute-done | bytes 147488 | tf_op jit(solution)/shard_map/ppermute | solution.py:426
  11.6 2.9 %collective-permute-done.2.refs_2_ = f32[9,4,8,128]{3,2,1,0:T(8,128)S(1)} collective-permute-done((f32[9,4,8,128]{3,2,1,0:T(8,128)S(1)}, f32[9,4,8,128]{3,2,1,0:T(8,128)S(1)}, u32[]{:S(2)}, u32[]{:S(2)}) %collective-permute-start.2) | collective-permute-done | bytes 147488 | tf_op jit(solution)/shard_map/ppermute | solution.py:426
  14.5 0.4 %collective-permute-start.3 = (f32[2,4,8,128]{3,2,1,0:T(8,128)S(1)}, f32[2,4,8,128]{3,2,1,0:T(8,128)S(1)}, u32[]{:S(2)}, u32[]{:S(2)}) collective-permute-start(f32[2,4,8,128]{3,2,1,0:T(8,128)S(1)} %pad_maximum_fusion), channel_id=1, source_target_pairs={{0,2},{2,0},{1,3},{3,1},{4,6},{6,4},{5,7},{7,5},{8,10},{10,8},{9,1... | collective-permute-start | bytes 98312 | tf_op jit(solution)/shard_map/ppermute | solution.py:458
  14.9 0.0 collective-permute-done.refs_4_
  14.9 0.0 copy-start
  14.9 0.7 %copy-done = f32[16]{0:T(128)S(1)} copy-done((f32[16]{0:T(128)S(1)}, f32[16]{0:T(128)}, u32[]{:S(2)}) %copy-start) | copy-done | bytes 88
  15.6 0.0 copy-start.1
  15.6 0.7 %copy-done.1 = s32[2]{0:T(128)S(1)} copy-done((s32[2]{0:T(128)S(1)}, s32[2]{0:T(128)}, u32[]{:S(2)}) %copy-start.1) | copy-done | bytes 32
  16.3 1.6 %shard_map.57.refs_0_ = f32[100,8,8,128]{3,2,1,0:T(8,128)S(1)} custom-call(f32[16]{0:T(128)S(1)} %copy-done, s32[2]{0:T(128)S(1)} %copy-done.1, f32[256,128]{1,0:T(8,128)S(1)} %get-tuple-element.17.refs_0_.refs_2_, f32[256,128]{1,0:T(8,128)S(1)} %get-tuple-element.18.refs_1_.refs_3_, f32[30,4,8,128]{3,2,1,0:T(8,128)S(1)} %collective-permute-done.refs_4_), custom_call_target="tpu_custom_call" | custom-call | flops 10000000 | bytes 4030536 | tf_op jit(solution)/shard_map/pallas_call | solution.py:405
  17.8 1.1 %shard_map.58.refs_1_ = f32[94,8,8,128]{3,2,1,0:T(8,128)S(1)} custom-call(f32[100,8,8,128]{3,2,1,0:T(8,128)S(1)} %shard_map.57.refs_0_, f32[9,4,8,128]{3,2,1,0:T(8,128)S(1)} %collective-permute-done.1.refs_1_, f32[9,4,8,128]{3,2,1,0:T(8,128)S(1)} %collective-permute-done.2.refs_2_), custom_call_target="tpu_custom_call" | custom-call | flops 10000000 | bytes 6651904 | tf_op jit(solution)/shard_map/pallas_call | solution.py:405
  18.9 0.0 collective-permute-done.3.refs_2_
  18.9 0.8 %shard_map.59.refs_2_ = f32[62,8,8,128]{3,2,1,0:T(8,128)S(1)} custom-call(f32[100,8,8,128]{3,2,1,0:T(8,128)S(1)} %shard_map.57.refs_0_, f32[94,8,8,128]{3,2,1,0:T(8,128)S(1)} %shard_map.58.refs_1_, f32[2,4,8,128]{3,2,1,0:T(8,128)S(1)} %collective-permute-done.3.refs_2_, f32[512,128]{1,0:T(8,128)S(1)} %get-tuple-element.19.refs_2_.refs_3_, ...), custom_call_target="tpu_custom_call" | custom-call | flops 10000000 | bytes 9175040 | tf_op jit(solution)/shard_map/pallas_call | solution.py:405
  19.7 0.0 collective-permute-done.4.refs_3_
  19.7 0.0 collective-permute-done.5.refs_4_
  19.7 0.6 %shard_map.60 = (f32[4,16,128]{2,1,0:T(8,128)S(1)}, f32[4,16,128]{2,1,0:T(8,128)S(1)}, f32[4,16,128]{2,1,0:T(8,128)S(1)}, f32[4,16,128]{2,1,0:T(8,128)S(1)}) custom-call(f32[100,8,8,128]{3,2,1,0:T(8,128)S(1)} %shard_map.57.refs_0_, f32[94,8,8,128]{3,2,1,0:T(8,128)S(1)} %shard_map.58.refs_1_, f32[62,8,8,128]{3,2,1,0:T(8,128)S(1)} %shard_map.59.refs_2_, ...), custom_call_target="tpu_custom_call" | custom-call | flops 10000000 | bytes 8716288 | tf_op jit(solution)/shard_map/pallas_call | solution.py:405
  20.4 1.3 %collective-permute-start.6 = (f32[4,16,128]{2,1,0:T(8,128)S(1)}, f32[4,16,128]{2,1,0:T(8,128)S(1)}, u32[]{:S(2)}, u32[]{:S(2)}) collective-permute-start(f32[4,16,128]{2,1,0:T(8,128)S(1)} %get-tuple-element.26), channel_id=1, source_target_pairs={{0,1},{2,3},{1,0},{3,2},{4,5},{6,7},{5,4},{7,6},{8,9},{10,11},{9,8... | collective-permute-start | bytes 98312 | tf_op jit(solution)/shard_map/ppermute | solution.py:492
  21.6 0.0 collective-permute-start.7
  21.6 0.9 %collective-permute-start.8 = (f32[4,16,128]{2,1,0:T(8,128)S(1)}, f32[4,16,128]{2,1,0:T(8,128)S(1)}, u32[]{:S(2)}, u32[]{:S(2)}) collective-permute-start(f32[4,16,128]{2,1,0:T(8,128)S(1)} %get-tuple-element.28), channel_id=1, source_target_pairs={{0,3},{2,1},{1,2},{3,0},{4,7},{6,5},{5,6},{7,4},{8,11},{10,9},{9,1... | collective-permute-start | bytes 98312 | tf_op jit(solution)/shard_map/ppermute | solution.py:492
  22.6 1.8 %collective-permute-done.6.refs_1_ = f32[4,16,128]{2,1,0:T(8,128)S(1)} collective-permute-done((f32[4,16,128]{2,1,0:T(8,128)S(1)}, f32[4,16,128]{2,1,0:T(8,128)S(1)}, u32[]{:S(2)}, u32[]{:S(2)}) %collective-permute-start.6) | collective-permute-done | bytes 32800 | tf_op jit(solution)/shard_map/ppermute | solution.py:492
  24.3 0.0 collective-permute-done.7.refs_2_
  24.3 0.7 %collective-permute-done.8.refs_3_ = f32[4,16,128]{2,1,0:T(8,128)S(1)} collective-permute-done((f32[4,16,128]{2,1,0:T(8,128)S(1)}, f32[4,16,128]{2,1,0:T(8,128)S(1)}, u32[]{:S(2)}, u32[]{:S(2)}) %collective-permute-start.8) | collective-permute-done | bytes 32800 | tf_op jit(solution)/shard_map/ppermute | solution.py:492
  25.0 0.6 %shard_map.61 = f32[128,128]{1,0:T(8,128)} custom-call(f32[4,16,128]{2,1,0:T(8,128)S(1)} %get-tuple-element.25.refs_0_, f32[4,16,128]{2,1,0:T(8,128)S(1)} %collective-permute-done.6.refs_1_, f32[4,16,128]{2,1,0:T(8,128)S(1)} %collective-permute-done.7.refs_2_, f32[4,16,128]{2,1,0:T(8,128)S(1)} %collective-permute-done.8.refs_3_), custom_call_target="tpu_custom_call" | custom-call | bytes 196608 | tf_op jit(solution)/shard_map/pallas_call | solution.py:405
  (3 shorter events, 0.0 us)
Async XLA Ops:
  1.6 13.4 %collective-permute-start = (f32[30,4,8,128]{3,2,1,0:T(8,128)S(1)}, f32[30,4,8,128]{3,2,1,0:T(8,128)S(1)}, u32[]{:S(2)}, u32[]{:S(2)}) collective-permute-start(f32[30,4,8,128]{3,2,1,0:T(8,128)S(1)} %get-tuple-element.20), channel_id=1, source_target_pairs={{0,2},{2,0},{1,3},{3,1},{4,6},{6,4},{5,7},{7,5},{8,10},{10,8},{9,1... | collective-permute-start | bytes 1474568 | tf_op jit(solution)/shard_map/ppermute | solution.py:444
  2.1 9.5 %collective-permute-start.1 = (f32[9,4,8,128]{3,2,1,0:T(8,128)S(1)}, f32[9,4,8,128]{3,2,1,0:T(8,128)S(1)}, u32[]{:S(2)}, u32[]{:S(2)}) collective-permute-start(f32[9,4,8,128]{3,2,1,0:T(8,128)S(1)} %get-tuple-element.21), channel_id=1, source_target_pairs={{0,4},{2,14},{4,8},{6,2},{8,12},{10,6},{12,0},{14,10},{1,5},{3,15}... | collective-permute-start | bytes 442376 | tf_op jit(solution)/shard_map/ppermute | solution.py:426
  4.8 9.7 %collective-permute-start.2 = (f32[9,4,8,128]{3,2,1,0:T(8,128)S(1)}, f32[9,4,8,128]{3,2,1,0:T(8,128)S(1)}, u32[]{:S(2)}, u32[]{:S(2)}) collective-permute-start(f32[9,4,8,128]{3,2,1,0:T(8,128)S(1)} %get-tuple-element.22), channel_id=1, source_target_pairs={{0,14},{2,4},{4,2},{6,8},{8,6},{10,12},{12,10},{14,0},{1,15},{3,5}... | collective-permute-start | bytes 442376 | tf_op jit(solution)/shard_map/ppermute | solution.py:426
  7.0 12.7 %collective-permute-start.4 = (f32[6,4,8,128]{3,2,1,0:T(8,128)S(1)}, f32[6,4,8,128]{3,2,1,0:T(8,128)S(1)}, u32[]{:S(2)}, u32[]{:S(2)}) collective-permute-start(f32[6,4,8,128]{3,2,1,0:T(8,128)S(1)} %get-tuple-element.23), channel_id=1, source_target_pairs={{0,4},{2,14},{4,8},{6,2},{8,12},{10,6},{12,0},{14,10},{1,5},{3,15}... | collective-permute-start | bytes 294920 | tf_op jit(solution)/shard_map/ppermute | solution.py:426
  8.6 11.1 %collective-permute-start.5 = (f32[6,4,8,128]{3,2,1,0:T(8,128)S(1)}, f32[6,4,8,128]{3,2,1,0:T(8,128)S(1)}, u32[]{:S(2)}, u32[]{:S(2)}) collective-permute-start(f32[6,4,8,128]{3,2,1,0:T(8,128)S(1)} %get-tuple-element.24), channel_id=1, source_target_pairs={{0,14},{2,4},{4,2},{6,8},{8,6},{10,12},{12,10},{14,0},{1,15},{3,5}... | collective-permute-start | bytes 294920 | tf_op jit(solution)/shard_map/ppermute | solution.py:426
  14.5 4.4 %collective-permute-start.3 = (f32[2,4,8,128]{3,2,1,0:T(8,128)S(1)}, f32[2,4,8,128]{3,2,1,0:T(8,128)S(1)}, u32[]{:S(2)}, u32[]{:S(2)}) collective-permute-start(f32[2,4,8,128]{3,2,1,0:T(8,128)S(1)} %pad_maximum_fusion), channel_id=1, source_target_pairs={{0,2},{2,0},{1,3},{3,1},{4,6},{6,4},{5,7},{7,5},{8,10},{10,8},{9,1... | collective-permute-start | bytes 98312 | tf_op jit(solution)/shard_map/ppermute | solution.py:458
  14.9 0.7 %copy-start = (f32[16]{0:T(128)S(1)}, f32[16]{0:T(128)}, u32[]{:S(2)}) copy-start(f32[16]{0:T(128)} %refs_0_.1) | copy-start | bytes 196
  15.6 0.7 %copy-start.1 = (s32[2]{0:T(128)S(1)}, s32[2]{0:T(128)}, u32[]{:S(2)}) copy-start(s32[2]{0:T(128)} %refs_1_.1) | copy-start | bytes 28
  20.4 4.0 %collective-permute-start.6 = (f32[4,16,128]{2,1,0:T(8,128)S(1)}, f32[4,16,128]{2,1,0:T(8,128)S(1)}, u32[]{:S(2)}, u32[]{:S(2)}) collective-permute-start(f32[4,16,128]{2,1,0:T(8,128)S(1)} %get-tuple-element.26), channel_id=1, source_target_pairs={{0,1},{2,3},{1,0},{3,2},{4,5},{6,7},{5,4},{7,6},{8,9},{10,11},{9,8... | collective-permute-start | bytes 98312 | tf_op jit(solution)/shard_map/ppermute | solution.py:492
  21.6 2.7 %collective-permute-start.7 = (f32[4,16,128]{2,1,0:T(8,128)S(1)}, f32[4,16,128]{2,1,0:T(8,128)S(1)}, u32[]{:S(2)}, u32[]{:S(2)}) collective-permute-start(f32[4,16,128]{2,1,0:T(8,128)S(1)} %get-tuple-element.27), channel_id=1, source_target_pairs={{0,2},{2,0},{1,3},{3,1},{4,6},{6,4},{5,7},{7,5},{8,10},{10,8},{9,1... | collective-permute-start | bytes 98312 | tf_op jit(solution)/shard_map/ppermute | solution.py:492
  21.6 3.3 %collective-permute-start.8 = (f32[4,16,128]{2,1,0:T(8,128)S(1)}, f32[4,16,128]{2,1,0:T(8,128)S(1)}, u32[]{:S(2)}, u32[]{:S(2)}) collective-permute-start(f32[4,16,128]{2,1,0:T(8,128)S(1)} %get-tuple-element.28), channel_id=1, source_target_pairs={{0,3},{2,1},{1,2},{3,0},{4,7},{6,5},{5,6},{7,4},{8,11},{10,9},{9,1... | collective-permute-start | bytes 98312 | tf_op jit(solution)/shard_map/ppermute | solution.py:492

commit v5 on v4

--- a/solution.py
+++ b/solution.py
@@ -21,46 +21,122 @@
 LIMIT = 20 << 20
 
 
+class Window:
+    def __init__(self, depth, doses):
+        self.depth, self.doses = depth, doses
+        self.piece = depth // doses
+        self.ends = 0 if doses == 1 else 1 if doses == 2 else 2
+        self.size = min(depth, self.piece + SUB * self.ends)
+        self.groups = self.size // SUB
+
+    def layers(self, halo):
+        return min(self.depth, self.piece + halo * self.ends)
+
+    def clamp(self, owner, halo, size):
+        return jnp.minimum(jnp.maximum(owner * self.piece - halo, 0), self.depth - size)
+
+    def start(self, owner):
+        return self.clamp(owner, SUB, self.size)
+
+    def sent(self, owner, halo):
+        return self.clamp(owner, halo, self.layers(halo))
+
+
+def dense_places(window, parts):
+    places, at = [], window.size - window.layers(parts[0][0])
+    for halo, count in parts:
+        places.append(at)
+        at += count * window.layers(halo)
+    at += window.size - window.layers(parts[-1][0])
+    return places, -(-at // SUB) * SUB
+
+
+def image_parts():
+    return ((HALO_AERIAL, HALO_AERIAL), (HALO_QUENCH, HALO_QUENCH))
+
+
+def cot_parts(count):
+    return ((HALO_COT, count),)
+
+
 def chip_row(rows, row):
     return row + lax.axis_index("ty") * (rows - 1 - 2 * row)
 
 
-def vector(ref, rows, groups, k, row, base=0):
-    return ref[pl.ds(base + rows * k + row, SUB, stride=rows * groups), :]
-
-
-def image_kernel(rows, groups, image_hbm, quench_hbm, cot_hbm, image_s, image_c, aerial, quench, cot, sems):
-    pairs = ((image_hbm, aerial), (quench_hbm, quench), (cot_hbm, cot))
+def vector(ref, rows, groups, first, row, base=0):
+    return ref[pl.ds(base + rows * first + row, SUB, stride=rows * groups), :]
+
+
+def put_dense(dst, at, src, base, rows, row, first, layers):
+    for g in range(0, layers, SUB):
+        n = min(SUB, layers - g)
+        dst[pl.ds(at + g, n), :] = src[pl.ds(base + rows * (first + g) + row, n, stride=rows), :]
+
+
+def clear_ends(dst):
+    zero = jnp.zeros((SUB, dst.shape[1]), jnp.float32)
+    dst[pl.ds(0, SUB), :] = zero
+    dst[pl.ds(dst.shape[0] - SUB, SUB), :] = zero
+
+
+def from_dense(src, at, window, owner, halo):
+    start = at - (window.sent(owner, halo) - window.start(owner))
+    return [src[pl.ds(start + k, SUB, stride=window.groups), :] for k in range(window.groups)]
+
+
+def image_kernel(rows, window, local, *refs):
+    image_hbm, quench_hbm, cot_hbm, levels_hbm, index_hbm = refs[:5]
+    image_s, image_c, dose, aerial, quench, cot, levels, index, sems = refs[5:]
+    pairs = ((image_hbm, aerial), (quench_hbm, quench), (cot_hbm, cot), (levels_hbm, levels), (index_hbm, index))
     copies = [pltpu.make_async_copy(src, dst, sems.at[i]) for i, (src, dst) in enumerate(pairs)]
     for copy in copies:
         copy.start()
+    clear_ends(image_s)
+    clear_ends(image_c)
+    owner = lax.axis_index("dose")
+    places, _ = dense_places(window, image_parts())
     copies[0].wait()
     copies[1].wait()
-    place = 0
-    for src, width in ((aerial, HALO_AERIAL), (quench, HALO_QUENCH)):
+    for src, at, width in ((aerial, places[0], HALO_AERIAL), (quench, places[1], HALO_QUENCH)):
+        layers, first = window.layers(width), window.sent(owner, width)
         for i in range(width):
-            for k in range(groups):
-                image_s[place, k] = vector(src, rows, groups, k, chip_row(rows, rows - width + i))
-                image_c[place, k] = vector(src, rows, groups, k, chip_row(rows, width - 1 - i))
-            place += 1
-    copies[2].wait()
-
-
-def rest_kernel(rows, groups, local, aerial, quench, cot, cot_s, cot_c, swap):
-    area = rows * groups * SUB
+            for dst, row in ((image_s, rows - width + i), (image_c, width - 1 - i)):
+                put_dense(dst, at + i * layers, src, 0, rows, chip_row(rows, row), first, layers)
+    for copy in copies[2:]:
+        copy.wait()
+    for d in range(local):
+        dose[d] = jnp.full(dose.shape[1:], levels[index[d]], jnp.float32)
+
+
+def rest_kernel(rows, window, local, aerial, quench, cot, swap, *dense):
+    depth, groups, doses = window.depth, window.groups, window.doses
+    area = rows * depth
     inner = rows // 2 + HALO_COT
-    for d in range(local):
-        for i in range(HALO_COT):
-            for k in range(groups):
-                place = d * HALO_COT + i
-                cot_s[place, k] = vector(cot, rows, groups, k, chip_row(rows, rows - HALO_COT + i), d * area)
-                cot_c[place, k] = vector(cot, rows, groups, k, chip_row(rows, HALO_COT - 1 - i), d * area)
+    owner = lax.axis_index("dose")
+    layers = window.layers(HALO_COT)
+    sends = dense[: 2 * doses]
+    wholes = dense[2 * doses :]
+    for ref in dense:
+        clear_ends(ref)
+    lead = window.size - layers
+    for k in range(doses):
+        first = window.sent(lax.rem(owner + k, doses), HALO_COT)
+        for d in range(local):
+            for i in range(HALO_COT):
+                at = lead + (d * HALO_COT + i) * layers
+                put_dense(sends[2 * k], at, cot, d * area, rows, chip_row(rows, rows - HALO_COT + i), first, layers)
+                put_dense(sends[2 * k + 1], at, cot, d * area, rows, chip_row(rows, HALO_COT - 1 - i), first, layers)
+            if k:
+                for row in range(rows):
+                    at = lead + (d * rows + row) * layers
+                    put_dense(wholes[k - 1], at, cot, d * area, rows, row, first, layers)
     place = 0
     parts = [(aerial, 0, rows), (quench, 0, rows)] + [(cot, d * area, inner) for d in range(local)]
+    start = window.start(owner)
     for src, base, width in parts:
         for i in range(width):
             for k in range(groups):
-                swap[place, k] = vector(src, rows, groups, k, chip_row(rows, rows - 1 - i), base)
+                swap[place, k] = vector(src, rows, groups, start + k, chip_row(rows, rows - 1 - i), base)
             place += 1
 
 
@@ -241,19 +317,23 @@
             fields.put("c%d" % n, d, row, value)
 
 
-def near_kernel(rows, groups, local, levels, index, aerial, quench, swap, near):
+def near_kernel(rows, window, local, *refs):
+    doses, groups = window.doses, window.groups
+    dose_refs, (aerial, quench, swap, near) = refs[:doses], refs[doses:]
     half = rows // 2
     spread = make_spread()
-    fields = Fields(rows, local, (near, near_rows))
+    total = local * doses
+    fields = Fields(rows, total, (near, near_rows))
+    start = window.start(lax.axis_index("dose"))
 
     def source(raw, at, row):
-        own = [vector(raw, rows, groups, k, chip_row(rows, row)) for k in range(groups)]
+        own = [vector(raw, rows, groups, start + k, chip_row(rows, row)) for k in range(groups)]
         return own + [swap[at + row, k] for k in range(groups)]
 
     for row in range(rows):
         fields.put("q0", 0, row, source(quench, rows, row))
-    for d in range(local):
-        dose = jnp.full((SUB, near.shape[3]), levels[index[d]], jnp.float32)
+    for d in range(total):
+        dose = dose_refs[d // local][d % local]
         fields.put("dose", d, 0, [dose] * (2 * groups))
         rate = -exposure_rate * dose
         for row in range(rows):
@@ -264,20 +344,23 @@
         forward_rows(spread, fields, d, near_rows(rows))
 
 
-def far_kernel(rows, groups, local, near, image_s, image_c, far):
+def far_kernel(rows, window, total, near, image_s, image_c, far):
     spread = make_spread()
-    fields = Fields(rows, local, (near, near_rows), (far, far_rows))
+    fields = Fields(rows, total, (near, near_rows), (far, far_rows))
     table = dict(far_rows(rows), e=(0, 0))
-
-    def source(at, row):
-        return [image_s[at + row, k] for k in range(groups)] + [image_c[at + row, k] for k in range(groups)]
+    owner = lax.axis_index("dose")
+    places, _ = dense_places(window, image_parts())
+
+    def source(part, halo, row):
+        at = places[part] + (halo + row) * window.layers(halo)
+        return [v for src in (image_s, image_c) for v in from_dense(src, at, window, owner, halo)]
 
     for row in range(-HALO_QUENCH, 0):
-        fields.put("q0", 0, row, source(HALO_AERIAL + HALO_QUENCH, row))
-    for d in range(local):
+        fields.put("q0", 0, row, source(1, HALO_QUENCH, row))
+    for d in range(total):
         rate = -exposure_rate * fields.get("dose", d, 0)[0]
         for row in range(-HALO_AERIAL, 0):
-            fields.put("a0", d, row, [1.0 - jnp.exp(rate * v) for v in source(HALO_AERIAL, row)])
+            fields.put("a0", d, row, [1.0 - jnp.exp(rate * v) for v in source(0, HALO_AERIAL, row)])
         forward_rows(spread, fields, d, table)
 
 
@@ -312,15 +395,24 @@
                 back.put("m1", d, row, [v - a * (neutral_rate * s) for v, a, s in parts])
 
 
-def back_near_kernel(rows, groups, local, near, far, extra, cot, swap, back_near):
+def back_near_kernel(rows, window, local, near, far, extra_own, extra_par, cot, swap, *refs):
+    doses, groups = window.doses, window.groups
+    wholes, back_near = refs[:-1], refs[-1]
     half = rows // 2
-    area = rows * groups * SUB
+    area = rows * window.depth
     inner = half + HALO_COT
+    total = local * doses
     spread = make_spread()
-    for d in range(local):
-        past = Fields(rows, local, (near, near_rows), (far, far_rows))
+    owner = lax.axis_index("dose")
+    start = window.start(owner)
+    layers = window.layers(HALO_COT)
+    lead = window.size - layers
+    places, _ = dense_places(window, image_parts())
+    last = places[0] + (HALO_AERIAL - 1) * window.layers(HALO_AERIAL)
+    for d in range(total):
+        past = Fields(rows, total, (near, near_rows), (far, far_rows))
         rate = -exposure_rate * past.get("dose", d, 0)[0]
-        light = [extra[side, k] for side in range(2) for k in range(groups)]
+        light = [v for src in (extra_own, extra_par) for v in from_dense(src, last, window, owner, HALO_AERIAL)]
         past.more["a0", d, rows] = [1.0 - jnp.exp(rate * v) for v in light]
         for n in range(3):
             row = rows - 1 - n
@@ -328,76 +420,79 @@
         for n, row in ((3, half + 2), (2, half + 1)):
             left = left_of(past.get("a%d" % (5 - n), d, row))
             past.more["c%d" % n, d, row] = [v * m for v, m in zip(past.get("c%d" % n, d, row), left)]
-        back = Fields(rows, local, (back_near, back_near_rows))
+        back = Fields(rows, total, (back_near, back_near_rows))
         table = back_near_rows(rows)
+        k, i = divmod(d, local)
         for row in range(*table["ct"]):
-            value = [vector(cot, rows, groups, k, chip_row(rows, row), d * area) for k in range(groups)]
-            back.put("ct", d, row, value + [swap[2 * rows + d * inner + row, k] for k in range(groups)])
+            if k == 0:
+                value = [vector(cot, rows, groups, start + g, chip_row(rows, row), i * area) for g in range(groups)]
+                value += [swap[2 * rows + i * inner + row, g] for g in range(groups)]
+            else:
+                at = lead + (i * rows + chip_row(rows, row)) * layers
+                sides = (wholes[2 * k - 2], wholes[2 * k - 1])
+                value = [v for src in sides for v in from_dense(src, at, window, owner, HALO_COT)]
+            back.put("ct", d, row, value)
         backward_rows(spread, past, back, d, table)
 
 
-def back_far_kernel(rows, groups, local, doses, near, far, back_near, cot_s, cot_c, *refs):
-    outs = refs[: 2 * doses]
-    store, full = refs[2 * doses :]
+def back_far_kernel(rows, window, local, near, far, back_near, *refs):
+    doses, groups = window.doses, window.groups
+    sends = refs[: 2 * doses]
+    mine, other, store, full = refs[2 * doses :]
     half = rows // 2
-    depth = groups * SUB
-    place = lax.axis_index("dose")
+    total = local * doses
+    owner = lax.axis_index("dose")
+    layers = window.layers(HALO_COT)
+    lead = window.size - layers
     spread = make_spread()
-    past = Fields(rows, local, (near, near_rows), (far, far_rows))
-    back = Fields(rows, local, (back_near, back_near_rows), (store, back_far_rows))
+    past = Fields(rows, total, (near, near_rows), (far, far_rows))
+    back = Fields(rows, total, (back_near, back_near_rows), (store, back_far_rows))
     table = back_far_rows(rows)
-    for d in range(local):
+    for d in range(total):
+        k, i = divmod(d, local)
         for row in range(*table["ct"]):
-            at = d * HALO_COT + HALO_COT + row
-            value = [cot_s[at, k] for k in range(groups)] + [cot_c[at, k] for k in range(groups)]
-            back.put("ct", d, row, value)
+            at = lead + (i * HALO_COT + HALO_COT + row) * layers
+            sides = (sends[2 * k], sends[2 * k + 1])
+            back.put("ct", d, row, [v for src in sides for v in from_dense(src, at, window, owner, HALO_COT)])
         backward_rows(spread, past, back, d, table)
     for row in range(half):
         value = back.get("g", 0, row)
-        for d in range(1, local):
+        for d in range(1, total):
             value = [v + w for v, w in zip(value, back.get("g", d, row))]
         for i in range(2 * groups):
             side, k = divmod(i, groups)
             full[side, row, pl.ds(k, SUB, stride=groups), :] = value[i]
-    piece = depth // doses
-    for side in range(2):
-        for k in range(doses):
-            start = pl.multiple_of(lax.rem(place + k, doses) * piece, SUB)
-            for row in range(half):
-                outs[side * doses + k][row] = full[side, row, pl.ds(start, piece), :]
-
-
-def join_kernel(rows, piece, doses, *refs):
-    parts, out = refs[:-1], refs[-1]
-    half = rows // 2
+    start = pl.multiple_of(owner * window.piece - window.start(owner), SUB)
+    for side, out in enumerate((mine, other)):
+        for row in range(half):
+            out[row] = full[side, row, pl.ds(start, window.piece), :]
+
+
+def join_kernel(rows, piece, mine, other, out):
     core = lax.axis_index("ty")
-    for side in range(2):
-        for row in range(half):
-            owner = core + side * (1 - 2 * core)
+    for owner, part in ((core, mine), (1 - core, other)):
+        for row in range(rows // 2):
             at = row + owner * (rows - 1 - 2 * row)
-            for g in range(piece // SUB):
-                value = parts[side * doses][row, pl.ds(g * SUB, SUB), :]
-                for k in range(1, doses):
-                    value = value + parts[side * doses + k][row, pl.ds(g * SUB, SUB), :]
-                out[pl.ds(g * SUB * rows + at, SUB, stride=rows), :] = value
+            for g in range(0, piece, SUB):
+                out[pl.ds(g * rows + at, SUB, stride=rows), :] = part[row, pl.ds(g, SUB), :]
 
 
 def gradient(aerial_image, quencher, cotangent, dose_levels, dose_index):
     depth, rows, lanes = aerial_image.shape
     local = cotangent.shape[0]
-    groups = depth // SUB
     half = rows // 2
     doses = lax.axis_size("dose")
     ring = lax.axis_size("tx")
     assert rows == half + HALO_QUENCH and HALO_AERIAL == HALO_QUENCH + 1
+    window = Window(depth, doses)
+    groups, piece = window.groups, window.piece
+    total = local * doses
     f32 = jnp.float32
     aerial = aerial_image.reshape(depth * rows, lanes)
     quench = quencher.reshape(depth * rows, lanes)
     cot = cotangent.reshape(local * depth * rows, lanes)
-    vmem = pl.BlockSpec(memory_space=pltpu.VMEM)
-    smem = pl.BlockSpec(memory_space=pltpu.SMEM)
-
-    def call(kernel, fixed, args, outs, scratch=(), scalars=0, flops=0, space=pltpu.VMEM):
+
+    def call(kernel, fixed, args, outs, scratch=(), flops=0, space=pltpu.VMEM):
         def body(*refs):
             kernel(*fixed, *refs)
 
@@ -405,93 +500,96 @@
         return pl.pallas_call(
             body,
             out_shape=tuple(outs),
-            in_specs=[smem] * scalars + [pl.BlockSpec(memory_space=space)] * (len(args) - scalars),
-            out_specs=(vmem,) * len(outs),
+            in_specs=[pl.BlockSpec(memory_space=space)] * len(args),
+            out_specs=(pl.BlockSpec(memory_space=pltpu.VMEM),) * len(outs),
             scratch_shapes=list(scratch),
             compiler_params=pltpu.CompilerParams(vmem_limit_bytes=LIMIT),
             cost_estimate=pl.CostEstimate(flops=flops, bytes_accessed=moved, transcendentals=0),
         )(*args)
 
-    def field(n, vectors=groups):
-        return jax.ShapeDtypeStruct((n, vectors, SUB, lanes), f32)
-
-    def device(t, c):
-        return (t % ring) * 2 + c
-
-    straight = [(device(t, c), device(t + 1 - 2 * c, c)) for t in range(ring) for c in range(2)]
-    crossed = [(device(t, c), device(t - 1 + 2 * c, 1 - c)) for t in range(ring) for c in range(2)]
-    across = [(0, 1), (1, 0)]
-
-    def along(value, pairs):
-        return lax.ppermute(value, ("tx", "ty"), pairs)
-
-    n_image = HALO_AERIAL + HALO_QUENCH
-    n_cot = local * HALO_COT
-    n_swap = 2 * rows + local * (half + HALO_COT)
+    def array(*shape):
+        return jax.ShapeDtypeStruct(shape + (lanes,), f32)
+
+    def store(table):
+        return (places_of(table(rows), total)[1], 2 * groups, SUB)
+
+    def along(value, cross=0, step=1, k=0):
+        pairs = []
+        for t in range(ring):
+            for c in range(2):
+                for d in range(doses):
+                    up = step * (1 - 2 * (c ^ cross))
+                    target = (((t + up) % ring) * 2 + (c ^ cross)) * doses + (d + k) % doses
+                    pairs.append(((t * 2 + c) * doses + d, target))
+        return lax.ppermute(value, ("tx", "ty", "dose"), pairs)
+
+    def across(value):
+        return along(value, cross=1, step=0)
+
+    images = array(dense_places(window, image_parts())[1])
+    halos = array(dense_places(window, cot_parts(local * HALO_COT))[1])
+    whole = array(dense_places(window, cot_parts(local * rows))[1])
     flat = [jax.ShapeDtypeStruct(x.shape, f32) for x in (aerial, quench, cot)]
-    image_s, image_c, aerial, quench, cot = call(
+    image_s, image_c, dose, aerial, quench, cot = call(
         image_kernel,
-        (rows, groups),
-        [pltpu.with_memory_space_constraint(x, pltpu.HBM) for x in (aerial, quench, cot)],
-        [field(n_image), field(n_image)] + flat,
-        [pltpu.SemaphoreType.DMA((3,))],
+        (rows, window, local),
+        [pltpu.with_memory_space_constraint(x, pltpu.HBM) for x in (aerial, quench, cot, dose_levels, dose_index)],
+        [images, images, array(local, SUB)] + flat,
+        [
+            pltpu.SMEM(dose_levels.shape, f32),
+            pltpu.SMEM(dose_index.shape, jnp.int32),
+            pltpu.SemaphoreType.DMA((5,)),
+        ],
         space=pltpu.HBM,
     )
-    image_s = along(image_s, straight)
-    image_c = along(image_c, crossed)
-    sends = [field(n) for n in (n_cot, n_cot, n_swap)]
-    cot_s, cot_c, swap = call(rest_kernel, (rows, groups, local), (aerial, quench, cot), sends)
-    swap = lax.ppermute(swap, "ty", across)
-    cot_s = along(cot_s, straight)
-    cot_c = along(cot_c, crossed)
+    image_s = along(image_s)
+    image_c = along(image_c, cross=1)
+    swap_rows = 2 * rows + local * (half + HALO_COT)
+    rest = call(
+        rest_kernel,
+        (rows, window, local),
+        (aerial, quench, cot),
+        [array(swap_rows, groups, SUB)] + [halos] * (2 * doses) + [whole] * (doses - 1),
+    )
+    swap = across(rest[0])
+    values = [dose] + [along(dose, step=0, k=k) for k in range(1, doses)]
+    wholes = []
+    for k in range(1, doses):
+        arrived = along(rest[2 * doses + k], step=0, k=k)
+        wholes += [arrived, across(arrived)]
+    sends = []
+    for k in range(doses):
+        sends.append(along(rest[1 + 2 * k], k=k))
+        sends.append(along(rest[2 + 2 * k], cross=1, k=k))
 
     (near,) = call(
-        near_kernel,
-        (rows, groups, local),
-        (dose_levels, dose_index, aerial, quench, swap),
-        (field(places_of(near_rows(rows), local)[1], 2 * groups),),
-        scalars=2,
-        flops=10_000_000,
-    )
-    last = HALO_AERIAL - 1
-    extra = jnp.concatenate((image_c[last : last + 1], image_s[last : last + 1]), axis=0)
-    extra = lax.ppermute(extra, "ty", across)
+        near_kernel, (rows, window, local), values + [aerial, quench, swap], [array(*store(near_rows))], flops=10_000_000
+    )
+    extra_own = across(image_c)
+    extra_par = across(image_s)
     (far,) = call(
-        far_kernel,
-        (rows, groups, local),
-        (near, image_s, image_c),
-        (field(places_of(far_rows(rows), local)[1], 2 * groups),),
-        flops=10_000_000,
+        far_kernel, (rows, window, total), (near, image_s, image_c), [array(*store(far_rows))], flops=10_000_000
     )
     (back_near,) = call(
         back_near_kernel,
-        (rows, groups, local),
-        (near, far, extra, cot, swap),
-        (field(places_of(back_near_rows(rows), local)[1], 2 * groups),),
+        (rows, window, local),
+        [near, far, extra_own, extra_par, cot, swap] + wholes,
+        [array(*store(back_near_rows))],
         flops=10_000_000,
     )
-    piece = depth // doses
-    parts = call(
+    mine, other = call(
         back_far_kernel,
-        (rows, groups, local, doses),
-        (near, far, back_near, cot_s, cot_c),
-        (jax.ShapeDtypeStruct((half, piece, lanes), f32),) * (2 * doses),
+        (rows, window, local),
+        [near, far, back_near] + sends,
+        [array(half, piece)] * 2,
         [
-            pltpu.VMEM((places_of(back_far_rows(rows), local)[1], 2 * groups, SUB, lanes), f32),
-            pltpu.VMEM((2, half, depth, lanes), f32),
+            pltpu.VMEM(store(back_far_rows) + (lanes,), f32),
+            pltpu.VMEM((2, half, window.size, lanes), f32),
         ],
         flops=10_000_000,
     )
-
-    arrived = []
-    for side in range(2):
-        for k in range(doses):
-            part = parts[side * doses + k]
-            if side or k:
-                pairs = [(c * doses + d, (c ^ side) * doses + (d + k) % doses) for d in range(doses) for c in range(2)]
-                part = lax.ppermute(part, ("ty", "dose"), pairs)
-            arrived.append(part)
-    (out,) = call(join_kernel, (rows, piece, doses), arrived, (jax.ShapeDtypeStruct((piece * rows, lanes), f32),))
+    other = across(other)
+    (out,) = call(join_kernel, (rows, piece), (mine, other), [array(piece * rows)])
     return out.reshape(piece, rows, lanes)
 
 

time: 25.8 us -> 30.8 us (1.19)
  starting transfers between devices: 9.65 us -> 13.8 us
  local copies, waits for them, and re-layouts: 1.31 us -> 0 us
  Pallas kernels: 6.26 us -> 7.4 us
  waiting for transfers between devices: 8.34 us -> 9.31 us
    ppermute x9 -> x13, starting transfers between devices: 9.65 us -> 13.8 us  [along(): return lax.ppermute(value, ('tx', 'ty', 'dose'), pairs)]
    unnamed x4 -> x0, local copies, waits for them, and re-layouts: 1.31 us -> none
    pallas_call x7, Pallas kernels: 6.26 us -> 7.4 us  [call(): pl.pallas_call(body, out_shape=tuple(outs), in_specs=[pl.BlockSpec(memory...]
    ppermute x9 -> x13, waiting for transfers between devices: 8.34 us -> 9.31 us  [along(): return lax.ppermute(value, ('tx', 'ty', 'dose'), pairs)]
  transfers between devices with their start and end apart: 9 -> 13, of which waited for: 4 -> 5; matrix products, arithmetic and copies ran while one was open for 0% -> 0% of each run, Pallas kernels for 13% -> 14%
where the time goes in v5:
time: 30.8 us; the launch traced here: 30.6 us
  starting transfers between devices  13.8 us (45%)
  waiting for transfers between devices  9.31 us (30%)
  Pallas kernels  7.4 us (24%)
    ppermute x13, starting transfers between devices, along(): return lax.ppermute(value, ('tx', 'ty', 'dose'), pairs)  13.8 us
    ppermute x13, waiting for transfers between devices, along(): return lax.ppermute(value, ('tx', 'ty', 'dose'), pairs)  9.31 us
    pallas_call x7, Pallas kernels, call(): pl.pallas_call(body, out_shape=tuple(outs), in_specs=[pl.BlockSpec(memory...  7.4 us
  transfers between devices with their start and end apart: 13, of which 5 were waited for; matrix products, arithmetic and copies ran while one was open for 0% of the time, Pallas kernels for 14%

profile of v5, /device:TPU:0, one launch (start us, length us, event | category | flops | bytes accessed | tf_op | source)
XLA Modules:
  0.0 30.6 jit_solution(9296867347816562066)
XLA Ops:
  0.0 1.1 %shard_map.55 = (f32[192,128]{1,0:T(8,128)S(1)}, f32[192,128]{1,0:T(8,128)S(1)}, f32[2,8,128]{2,1,0:T(8,128)S(1)}, f32[256,128]{1,0:T(8,128)S(1)}, f32[256,128]{1,0:T(8,128)S(1)}, /*index=5*/f32[512,128]{1,0:T(8,128)S(1)}) custom-call(f32[256,128]{1,0:T(8,128)} %bitcast.5, f32[256,128]{1,0:T(8,128)} %bitcast.6, f32[512,128]{1,0:T(8,128)} %bitcast.4, ...), custom_call_target="tpu_custom_call" | custom-call | bytes 1253448 | tf_op jit(solution)/shard_map/pallas_call | solution.py:500
  1.2 0.2 shard_map.56
  1.3 0.6 %collective-permute-start.1 = (f32[30,3,8,128]{3,2,1,0:T(8,128)S(1)}, f32[30,3,8,128]{3,2,1,0:T(8,128)S(1)}, u32[]{:S(2)}, u32[]{:S(2)}) collective-permute-start(f32[30,3,8,128]{3,2,1,0:T(8,128)S(1)} %get-tuple-element.23), channel_id=1, source_target_pairs={{0,2},{1,3},{2,0},{3,1},{4,6},{5,7},{6,4},{7,5},{8,10},{9,11},{10,... | collective-permute-start | bytes 1105928 | tf_op jit(solution)/shard_map/ppermute | solution.py:524
  1.9 2.6 %collective-permute-start.6 = (f32[320,128]{1,0:T(8,128)S(1)}, f32[320,128]{1,0:T(8,128)S(1)}, u32[]{:S(2)}, u32[]{:S(2)}) collective-permute-start(f32[320,128]{1,0:T(8,128)S(1)} %get-tuple-element.26), channel_id=1, source_target_pairs={{0,1},{1,0},{2,3},{3,2},{4,5},{5,4},{6,7},{7,6},{8,9},{9,8},{10,11... | collective-permute-start | bytes 491528 | tf_op jit(solution)/shard_map/ppermute | solution.py:524
  4.4 1.6 %collective-permute-start.2 = (f32[192,128]{1,0:T(8,128)S(1)}, f32[192,128]{1,0:T(8,128)S(1)}, u32[]{:S(2)}, u32[]{:S(2)}) collective-permute-start(f32[192,128]{1,0:T(8,128)S(1)} %get-tuple-element.24), channel_id=1, source_target_pairs={{0,4},{1,5},{2,14},{3,15},{4,8},{5,9},{6,2},{7,3},{8,12},{9,13},{1... | collective-permute-start | bytes 294920 | tf_op jit(solution)/shard_map/ppermute | solution.py:524
  6.0 2.0 %collective-permute-start.3 = (f32[192,128]{1,0:T(8,128)S(1)}, f32[192,128]{1,0:T(8,128)S(1)}, u32[]{:S(2)}, u32[]{:S(2)}) collective-permute-start(f32[192,128]{1,0:T(8,128)S(1)} %get-tuple-element.25), channel_id=1, source_target_pairs={{0,14},{1,15},{2,4},{3,5},{4,2},{5,3},{6,8},{7,9},{8,6},{9,7},{10,... | collective-permute-start | bytes 294920 | tf_op jit(solution)/shard_map/ppermute | solution.py:524
  8.0 1.3 %collective-permute-done.6.refs_6_ = f32[320,128]{1,0:T(8,128)S(1)} collective-permute-done((f32[320,128]{1,0:T(8,128)S(1)}, f32[320,128]{1,0:T(8,128)S(1)}, u32[]{:S(2)}, u32[]{:S(2)}) %collective-permute-start.6) | collective-permute-done | bytes 163872 | tf_op jit(solution)/shard_map/ppermute | solution.py:524
  9.2 0.0 collective-permute-start.7
  9.2 2.8 %collective-permute-done.2.refs_1_ = f32[192,128]{1,0:T(8,128)S(1)} collective-permute-done((f32[192,128]{1,0:T(8,128)S(1)}, f32[192,128]{1,0:T(8,128)S(1)}, u32[]{:S(2)}, u32[]{:S(2)}) %collective-permute-start.2) | collective-permute-done | bytes 98336 | tf_op jit(solution)/shard_map/ppermute | solution.py:524
  12.0 0.0 collective-permute-start.5
  12.0 0.9 %collective-permute-done.3.refs_2_ = f32[192,128]{1,0:T(8,128)S(1)} collective-permute-done((f32[192,128]{1,0:T(8,128)S(1)}, f32[192,128]{1,0:T(8,128)S(1)}, u32[]{:S(2)}, u32[]{:S(2)}) %collective-permute-start.3) | collective-permute-done | bytes 98336 | tf_op jit(solution)/shard_map/ppermute | solution.py:524
  13.0 0.4 %collective-permute-start.4 = (f32[192,128]{1,0:T(8,128)S(1)}, f32[192,128]{1,0:T(8,128)S(1)}, u32[]{:S(2)}, u32[]{:S(2)}) collective-permute-start(f32[192,128]{1,0:T(8,128)S(1)} %collective-permute-done.3.refs_2_), channel_id=1, source_target_pairs={{0,2},{1,3},{2,0},{3,1},{4,6},{5,7},{6,4},{7,5},{8,10},{9,11},{10,... | collective-permute-start | bytes 294920 | tf_op jit(solution)/shard_map/ppermute | solution.py:524
  13.3 0.5 %collective-permute-start = (f32[2,8,128]{2,1,0:T(8,128)S(1)}, f32[2,8,128]{2,1,0:T(8,128)S(1)}, u32[]{:S(2)}, u32[]{:S(2)}) collective-permute-start(f32[2,8,128]{2,1,0:T(8,128)S(1)} %get-tuple-element.19.refs_0_), channel_id=1, source_target_pairs={{0,1},{1,0},{2,3},{3,2},{4,5},{5,4},{6,7},{7,6},{8,9},{9,8},{10,11... | collective-permute-start | bytes 24584 | tf_op jit(solution)/shard_map/ppermute | solution.py:524
  13.9 3.1 %collective-permute-done.refs_1_ = f32[2,8,128]{2,1,0:T(8,128)S(1)} collective-permute-done((f32[2,8,128]{2,1,0:T(8,128)S(1)}, f32[2,8,128]{2,1,0:T(8,128)S(1)}, u32[]{:S(2)}, u32[]{:S(2)}) %collective-permute-start) | collective-permute-done | bytes 8224 | tf_op jit(solution)/shard_map/ppermute | solution.py:524
  17.0 0.7 %collective-permute-start.8 = (f32[128,128]{1,0:T(8,128)S(1)}, f32[128,128]{1,0:T(8,128)S(1)}, u32[]{:S(2)}, u32[]{:S(2)}) collective-permute-start(f32[128,128]{1,0:T(8,128)S(1)} %get-tuple-element.27), channel_id=1, source_target_pairs={{0,4},{1,5},{2,14},{3,15},{4,8},{5,9},{6,2},{7,3},{8,12},{9,13},{1... | collective-permute-start | bytes 196616 | tf_op jit(solution)/shard_map/ppermute | solution.py:524
  17.7 0.0 collective-permute-done.5.refs_3_
  17.7 1.0 %collective-permute-start.9 = (f32[128,128]{1,0:T(8,128)S(1)}, f32[128,128]{1,0:T(8,128)S(1)}, u32[]{:S(2)}, u32[]{:S(2)}) collective-permute-start(f32[128,128]{1,0:T(8,128)S(1)} %get-tuple-element.28), channel_id=1, source_target_pairs={{0,14},{1,15},{2,4},{3,5},{4,2},{5,3},{6,8},{7,9},{8,6},{9,7},{10,... | collective-permute-start | bytes 196616 | tf_op jit(solution)/shard_map/ppermute | solution.py:524
  18.6 0.0 collective-permute-done.4.refs_2_
  18.6 0.9 %collective-permute-start.10 = (f32[128,128]{1,0:T(8,128)S(1)}, f32[128,128]{1,0:T(8,128)S(1)}, u32[]{:S(2)}, u32[]{:S(2)}) collective-permute-start(f32[128,128]{1,0:T(8,128)S(1)} %get-tuple-element.29), channel_id=1, source_target_pairs={{0,5},{1,4},{2,15},{3,14},{4,9},{5,8},{6,3},{7,2},{8,13},{9,12},{1... | collective-permute-start | bytes 196616 | tf_op jit(solution)/shard_map/ppermute | solution.py:524
  19.5 0.0 collective-permute-done.1.refs_4_.refs_5_
  19.5 3.6 %collective-permute-start.11 = (f32[128,128]{1,0:T(8,128)S(1)}, f32[128,128]{1,0:T(8,128)S(1)}, u32[]{:S(2)}, u32[]{:S(2)}) collective-permute-start(f32[128,128]{1,0:T(8,128)S(1)} %get-tuple-element.30), channel_id=1, source_target_pairs={{0,15},{1,14},{2,5},{3,4},{4,3},{5,2},{6,9},{7,8},{8,7},{9,6},{10,... | collective-permute-start | bytes 196616 | tf_op jit(solution)/shard_map/ppermute | solution.py:524
  23.2 1.5 %shard_map.57.refs_0_ = f32[192,6,8,128]{3,2,1,0:T(8,128)S(1)} custom-call(f32[2,8,128]{2,1,0:T(8,128)S(1)} %get-tuple-element.19.refs_0_, f32[2,8,128]{2,1,0:T(8,128)S(1)} %collective-permute-done.refs_1_, f32[256,128]{1,0:T(8,128)S(1)} %get-tuple-element.20.refs_0_.refs_2_, f32[256,128]{1,0:T(8,128)S(1)} %get-tuple-element.21.refs_1_.refs_3_, ...), custom_call_target="tpu_custom_call" | custom-call | flops 10000000 | bytes 5365760 | tf_op jit(solution)/shard_map/pallas_call | solution.py:500
  24.7 1.6 %shard_map.58.refs_1_ = f32[184,6,8,128]{3,2,1,0:T(8,128)S(1)} custom-call(f32[192,6,8,128]{3,2,1,0:T(8,128)S(1)} %shard_map.57.refs_0_, f32[192,128]{1,0:T(8,128)S(1)} %collective-permute-done.2.refs_1_, f32[192,128]{1,0:T(8,128)S(1)} %collective-permute-done.3.refs_2_), custom_call_target="tpu_custom_call" | custom-call | flops 10000000 | bytes 9437184 | tf_op jit(solution)/shard_map/pallas_call | solution.py:500
  26.4 0.0 collective-permute-done.7.refs_7_
  26.4 1.3 %shard_map.59.refs_2_ = f32[124,6,8,128]{3,2,1,0:T(8,128)S(1)} custom-call(f32[192,6,8,128]{3,2,1,0:T(8,128)S(1)} %shard_map.57.refs_0_, f32[184,6,8,128]{3,2,1,0:T(8,128)S(1)} %shard_map.58.refs_1_, f32[192,128]{1,0:T(8,128)S(1)} %collective-permute-done.4.refs_2_, f32[192,128]{1,0:T(8,128)S(1)} %collective-permute-done.5.refs_3_, ...), custom_call_target="tpu_custom_call" | custom-call | flops 10000000 | bytes 13443072 | tf_op jit(solution)/shard_map/pallas_call | solution.py:500
  27.6 0.0 collective-permute-done.8.refs_3_
  27.7 0.0 collective-permute-done.9.refs_4_
  27.7 0.0 collective-permute-done.10.refs_5_
  27.7 0.0 collective-permute-done.11.refs_6_
  27.7 1.0 %shard_map.60 = (f32[4,16,128]{2,1,0:T(8,128)S(1)}, f32[4,16,128]{2,1,0:T(8,128)S(1)}) custom-call(f32[192,6,8,128]{3,2,1,0:T(8,128)S(1)} %shard_map.57.refs_0_, f32[184,6,8,128]{3,2,1,0:T(8,128)S(1)} %shard_map.58.refs_1_, f32[124,6,8,128]{3,2,1,0:T(8,128)S(1)} %shard_map.59.refs_2_, f32[128,128]{1,0:T(8,128)S(1)} %collective-permute-done.8.refs_3_, ...), custom_call_target="tpu_custom_call" | custom-call | flops 10000000 | bytes 12615680 | tf_op jit(solution)/shard_map/pallas_call | solution.py:500
  28.7 0.1 collective-permute-start.12
  28.8 1.2 %collective-permute-done.12.refs_1_ = f32[4,16,128]{2,1,0:T(8,128)S(1)} collective-permute-done((f32[4,16,128]{2,1,0:T(8,128)S(1)}, f32[4,16,128]{2,1,0:T(8,128)S(1)}, u32[]{:S(2)}, u32[]{:S(2)}) %collective-permute-start.12) | collective-permute-done | bytes 32800 | tf_op jit(solution)/shard_map/ppermute | solution.py:524
  30.0 0.6 %shard_map.61 = f32[128,128]{1,0:T(8,128)} custom-call(f32[4,16,128]{2,1,0:T(8,128)S(1)} %get-tuple-element.31.refs_0_, f32[4,16,128]{2,1,0:T(8,128)S(1)} %collective-permute-done.12.refs_1_), custom_call_target="tpu_custom_call" | custom-call | bytes 131072 | tf_op jit(solution)/shard_map/pallas_call | solution.py:500
Async XLA Ops:
  1.3 18.2 %collective-permute-start.1 = (f32[30,3,8,128]{3,2,1,0:T(8,128)S(1)}, f32[30,3,8,128]{3,2,1,0:T(8,128)S(1)}, u32[]{:S(2)}, u32[]{:S(2)}) collective-permute-start(f32[30,3,8,128]{3,2,1,0:T(8,128)S(1)} %get-tuple-element.23), channel_id=1, source_target_pairs={{0,2},{1,3},{2,0},{3,1},{4,6},{5,7},{6,4},{7,5},{8,10},{9,11},{10,... | collective-permute-start | bytes 1105928 | tf_op jit(solution)/shard_map/ppermute | solution.py:524
  1.9 7.3 %collective-permute-start.6 = (f32[320,128]{1,0:T(8,128)S(1)}, f32[320,128]{1,0:T(8,128)S(1)}, u32[]{:S(2)}, u32[]{:S(2)}) collective-permute-start(f32[320,128]{1,0:T(8,128)S(1)} %get-tuple-element.26), channel_id=1, source_target_pairs={{0,1},{1,0},{2,3},{3,2},{4,5},{5,4},{6,7},{7,6},{8,9},{9,8},{10,11... | collective-permute-start | bytes 491528 | tf_op jit(solution)/shard_map/ppermute | solution.py:524
  4.4 7.6 %collective-permute-start.2 = (f32[192,128]{1,0:T(8,128)S(1)}, f32[192,128]{1,0:T(8,128)S(1)}, u32[]{:S(2)}, u32[]{:S(2)}) collective-permute-start(f32[192,128]{1,0:T(8,128)S(1)} %get-tuple-element.24), channel_id=1, source_target_pairs={{0,4},{1,5},{2,14},{3,15},{4,8},{5,9},{6,2},{7,3},{8,12},{9,13},{1... | collective-permute-start | bytes 294920 | tf_op jit(solution)/shard_map/ppermute | solution.py:524
  6.0 6.9 %collective-permute-start.3 = (f32[192,128]{1,0:T(8,128)S(1)}, f32[192,128]{1,0:T(8,128)S(1)}, u32[]{:S(2)}, u32[]{:S(2)}) collective-permute-start(f32[192,128]{1,0:T(8,128)S(1)} %get-tuple-element.25), channel_id=1, source_target_pairs={{0,14},{1,15},{2,4},{3,5},{4,2},{5,3},{6,8},{7,9},{8,6},{9,7},{10,... | collective-permute-start | bytes 294920 | tf_op jit(solution)/shard_map/ppermute | solution.py:524
  9.2 17.1 %collective-permute-start.7 = (f32[320,128]{1,0:T(8,128)S(1)}, f32[320,128]{1,0:T(8,128)S(1)}, u32[]{:S(2)}, u32[]{:S(2)}) collective-permute-start(f32[320,128]{1,0:T(8,128)S(1)} %collective-permute-done.6.refs_6_), channel_id=1, source_target_pairs={{0,2},{1,3},{2,0},{3,1},{4,6},{5,7},{6,4},{7,5},{8,10},{9,11},{10,... | collective-permute-start | bytes 491528 | tf_op jit(solution)/shard_map/ppermute | solution.py:524
  12.0 5.6 %collective-permute-start.5 = (f32[192,128]{1,0:T(8,128)S(1)}, f32[192,128]{1,0:T(8,128)S(1)}, u32[]{:S(2)}, u32[]{:S(2)}) collective-permute-start(f32[192,128]{1,0:T(8,128)S(1)} %collective-permute-done.2.refs_1_), channel_id=1, source_target_pairs={{0,2},{1,3},{2,0},{3,1},{4,6},{5,7},{6,4},{7,5},{8,10},{9,11},{10,... | collective-permute-start | bytes 294920 | tf_op jit(solution)/shard_map/ppermute | solution.py:524
  13.0 5.7 %collective-permute-start.4 = (f32[192,128]{1,0:T(8,128)S(1)}, f32[192,128]{1,0:T(8,128)S(1)}, u32[]{:S(2)}, u32[]{:S(2)}) collective-permute-start(f32[192,128]{1,0:T(8,128)S(1)} %collective-permute-done.3.refs_2_), channel_id=1, source_target_pairs={{0,2},{1,3},{2,0},{3,1},{4,6},{5,7},{6,4},{7,5},{8,10},{9,11},{10,... | collective-permute-start | bytes 294920 | tf_op jit(solution)/shard_map/ppermute | solution.py:524
  13.3 3.7 %collective-permute-start = (f32[2,8,128]{2,1,0:T(8,128)S(1)}, f32[2,8,128]{2,1,0:T(8,128)S(1)}, u32[]{:S(2)}, u32[]{:S(2)}) collective-permute-start(f32[2,8,128]{2,1,0:T(8,128)S(1)} %get-tuple-element.19.refs_0_), channel_id=1, source_target_pairs={{0,1},{1,0},{2,3},{3,2},{4,5},{5,4},{6,7},{7,6},{8,9},{9,8},{10,11... | collective-permute-start | bytes 24584 | tf_op jit(solution)/shard_map/ppermute | solution.py:524
  17.0 10.7 %collective-permute-start.8 = (f32[128,128]{1,0:T(8,128)S(1)}, f32[128,128]{1,0:T(8,128)S(1)}, u32[]{:S(2)}, u32[]{:S(2)}) collective-permute-start(f32[128,128]{1,0:T(8,128)S(1)} %get-tuple-element.27), channel_id=1, source_target_pairs={{0,4},{1,5},{2,14},{3,15},{4,8},{5,9},{6,2},{7,3},{8,12},{9,13},{1... | collective-permute-start | bytes 196616 | tf_op jit(solution)/shard_map/ppermute | solution.py:524
  17.7 10.0 %collective-permute-start.9 = (f32[128,128]{1,0:T(8,128)S(1)}, f32[128,128]{1,0:T(8,128)S(1)}, u32[]{:S(2)}, u32[]{:S(2)}) collective-permute-start(f32[128,128]{1,0:T(8,128)S(1)} %get-tuple-element.28), channel_id=1, source_target_pairs={{0,14},{1,15},{2,4},{3,5},{4,2},{5,3},{6,8},{7,9},{8,6},{9,7},{10,... | collective-permute-start | bytes 196616 | tf_op jit(solution)/shard_map/ppermute | solution.py:524
  18.6 9.1 %collective-permute-start.10 = (f32[128,128]{1,0:T(8,128)S(1)}, f32[128,128]{1,0:T(8,128)S(1)}, u32[]{:S(2)}, u32[]{:S(2)}) collective-permute-start(f32[128,128]{1,0:T(8,128)S(1)} %get-tuple-element.29), channel_id=1, source_target_pairs={{0,5},{1,4},{2,15},{3,14},{4,9},{5,8},{6,3},{7,2},{8,13},{9,12},{1... | collective-permute-start | bytes 196616 | tf_op jit(solution)/shard_map/ppermute | solution.py:524
  19.5 8.1 %collective-permute-start.11 = (f32[128,128]{1,0:T(8,128)S(1)}, f32[128,128]{1,0:T(8,128)S(1)}, u32[]{:S(2)}, u32[]{:S(2)}) collective-permute-start(f32[128,128]{1,0:T(8,128)S(1)} %get-tuple-element.30), channel_id=1, source_target_pairs={{0,15},{1,14},{2,5},{3,4},{4,3},{5,2},{6,9},{7,8},{8,7},{9,6},{10,... | collective-permute-start | bytes 196616 | tf_op jit(solution)/shard_map/ppermute | solution.py:524
  28.7 1.3 %collective-permute-start.12 = (f32[4,16,128]{2,1,0:T(8,128)S(1)}, f32[4,16,128]{2,1,0:T(8,128)S(1)}, u32[]{:S(2)}, u32[]{:S(2)}) collective-permute-start(f32[4,16,128]{2,1,0:T(8,128)S(1)} %get-tuple-element.32), channel_id=1, source_target_pairs={{0,2},{1,3},{2,0},{3,1},{4,6},{5,7},{6,4},{7,5},{8,10},{9,11},{10,... | collective-permute-start | bytes 98312 | tf_op jit(solution)/shard_map/ppermute | solution.py:524

commit v6 on v5

--- a/solution.py
+++ b/solution.py
@@ -108,35 +108,52 @@
         dose[d] = jnp.full(dose.shape[1:], levels[index[d]], jnp.float32)
 
 
-def rest_kernel(rows, window, local, aerial, quench, cot, swap, *dense):
+def swap_layout(rows, window, local):
+    vectors = 2 * rows + local * (rows // 2 + HALO_COT)
+    halo = dense_places(window, cot_parts(local * HALO_COT))[1]
+    return vectors * window.groups * SUB, halo
+
+
+def swapped(swap, groups, place):
+    return [swap[pl.ds((place * groups + k) * SUB, SUB), :] for k in range(groups)]
+
+
+def rest_kernel(rows, window, local, dose, aerial, quench, cot, swap, *dense):
     depth, groups, doses = window.depth, window.groups, window.doses
     area = rows * depth
     inner = rows // 2 + HALO_COT
     owner = lax.axis_index("dose")
     layers = window.layers(HALO_COT)
-    sends = dense[: 2 * doses]
-    wholes = dense[2 * doses :]
+    sends = dense[:doses]
+    wholes = dense[doses:]
+    handed, halo = swap_layout(rows, window, local)
     for ref in dense:
         clear_ends(ref)
     lead = window.size - layers
+    zero = jnp.zeros((SUB, swap.shape[1]), jnp.float32)
     for k in range(doses):
         first = window.sent(lax.rem(owner + k, doses), HALO_COT)
+        block = handed + k * halo
+        swap[pl.ds(block, SUB), :] = zero
+        swap[pl.ds(block + halo - SUB, SUB), :] = zero
         for d in range(local):
             for i in range(HALO_COT):
                 at = lead + (d * HALO_COT + i) * layers
-                put_dense(sends[2 * k], at, cot, d * area, rows, chip_row(rows, rows - HALO_COT + i), first, layers)
-                put_dense(sends[2 * k + 1], at, cot, d * area, rows, chip_row(rows, HALO_COT - 1 - i), first, layers)
+                put_dense(sends[k], at, cot, d * area, rows, chip_row(rows, rows - HALO_COT + i), first, layers)
+                put_dense(swap, block + at, cot, d * area, rows, chip_row(rows, HALO_COT - 1 - i), first, layers)
             if k:
                 for row in range(rows):
                     at = lead + (d * rows + row) * layers
                     put_dense(wholes[k - 1], at, cot, d * area, rows, row, first, layers)
+                wholes[k - 1][pl.ds(wholes[k - 1].shape[0] - (local - d) * SUB, SUB), :] = dose[d]
     place = 0
     parts = [(aerial, 0, rows), (quench, 0, rows)] + [(cot, d * area, inner) for d in range(local)]
     start = window.start(owner)
     for src, base, width in parts:
         for i in range(width):
             for k in range(groups):
-                swap[place, k] = vector(src, rows, groups, start + k, chip_row(rows, rows - 1 - i), base)
+                value = vector(src, rows, groups, start + k, chip_row(rows, rows - 1 - i), base)
+                swap[pl.ds((place * groups + k) * SUB, SUB), :] = value
             place += 1
 
 
@@ -328,12 +345,13 @@
 
     def source(raw, at, row):
         own = [vector(raw, rows, groups, start + k, chip_row(rows, row)) for k in range(groups)]
-        return own + [swap[at + row, k] for k in range(groups)]
+        return own + swapped(swap, groups, at + row)
 
     for row in range(rows):
         fields.put("q0", 0, row, source(quench, rows, row))
     for d in range(total):
-        dose = dose_refs[d // local][d % local]
+        ref, i = dose_refs[d // local], d % local
+        dose = ref[pl.ds(ref.shape[0] - (local - i) * SUB, SUB), :] if d >= local else ref[i]
         fields.put("dose", d, 0, [dose] * (2 * groups))
         rate = -exposure_rate * dose
         for row in range(rows):
@@ -426,7 +444,7 @@
         for row in range(*table["ct"]):
             if k == 0:
                 value = [vector(cot, rows, groups, start + g, chip_row(rows, row), i * area) for g in range(groups)]
-                value += [swap[2 * rows + i * inner + row, g] for g in range(groups)]
+                value += swapped(swap, groups, 2 * rows + i * inner + row)
             else:
                 at = lead + (i * rows + chip_row(rows, row)) * layers
                 sides = (wholes[2 * k - 2], wholes[2 * k - 1])
@@ -437,8 +455,9 @@
 
 def back_far_kernel(rows, window, local, near, far, back_near, *refs):
     doses, groups = window.doses, window.groups
-    sends = refs[: 2 * doses]
-    mine, other, store, full = refs[2 * doses :]
+    sends = refs[:doses]
+    mine, other, store, full = refs[doses:]
+    halo = swap_layout(rows, window, local)[1]
     half = rows // 2
     total = local * doses
     owner = lax.axis_index("dose")
@@ -452,8 +471,8 @@
         k, i = divmod(d, local)
         for row in range(*table["ct"]):
             at = lead + (i * HALO_COT + HALO_COT + row) * layers
-            sides = (sends[2 * k], sends[2 * k + 1])
-            back.put("ct", d, row, [v for src in sides for v in from_dense(src, at, window, owner, HALO_COT)])
+            places = (at, at + halo)
+            back.put("ct", d, row, [v for p in places for v in from_dense(sends[k], p, window, owner, HALO_COT)])
         backward_rows(spread, past, back, d, table)
     for row in range(half):
         value = back.get("g", 0, row)
@@ -527,8 +546,8 @@
         return along(value, cross=1, step=0)
 
     images = array(dense_places(window, image_parts())[1])
-    halos = array(dense_places(window, cot_parts(local * HALO_COT))[1])
-    whole = array(dense_places(window, cot_parts(local * rows))[1])
+    handed, halo = swap_layout(rows, window, local)
+    whole = array(dense_places(window, cot_parts(local * rows))[1] + local * SUB)
     flat = [jax.ShapeDtypeStruct(x.shape, f32) for x in (aerial, quench, cot)]
     image_s, image_c, dose, aerial, quench, cot = call(
         image_kernel,
@@ -544,23 +563,23 @@
     )
     image_s = along(image_s)
     image_c = along(image_c, cross=1)
-    swap_rows = 2 * rows + local * (half + HALO_COT)
     rest = call(
         rest_kernel,
         (rows, window, local),
-        (aerial, quench, cot),
-        [array(swap_rows, groups, SUB)] + [halos] * (2 * doses) + [whole] * (doses - 1),
+        (dose, aerial, quench, cot),
+        [array(handed + doses * halo)] + [array(halo)] * doses + [whole] * (doses - 1),
     )
     swap = across(rest[0])
-    values = [dose] + [along(dose, step=0, k=k) for k in range(1, doses)]
-    wholes = []
+    values, wholes = [dose], []
     for k in range(1, doses):
-        arrived = along(rest[2 * doses + k], step=0, k=k)
+        arrived = along(rest[doses + k], step=0, k=k)
+        values.append(arrived)
         wholes += [arrived, across(arrived)]
     sends = []
     for k in range(doses):
-        sends.append(along(rest[1 + 2 * k], k=k))
-        sends.append(along(rest[2 + 2 * k], cross=1, k=k))
+        other = lax.slice_in_dim(swap, handed + k * halo, handed + (k + 1) * halo)
+        both = jnp.concatenate((rest[1 + k], other), axis=0)
+        sends.append(along(both, k=k))
 
     (near,) = call(
         near_kernel, (rows, window, local), values + [aerial, quench, swap], [array(*store(near_rows))], flops=10_000_000

time: 30.8 us -> 24.5 us (0.80)
  waiting for transfers between devices: 9.31 us -> 4.73 us
  starting transfers between devices: 13.8 us -> 12.1 us
    ppermute x13 -> x10, waiting for transfers between devices: 9.31 us -> 4.73 us  [along(): return lax.ppermute(value, ('tx', 'ty', 'dose'), pairs)]
    ppermute x13 -> x10, starting transfers between devices: 13.8 us -> 12.1 us  [along(): return lax.ppermute(value, ('tx', 'ty', 'dose'), pairs)]
  transfers between devices with their start and end apart: 13 -> 10, of which waited for: 5 -> 3; matrix products, arithmetic and copies ran while one was open for 0% -> 0% of each run, Pallas kernels for 14% -> 18%
where the time goes in v6:
time: 24.5 us; the launch traced here: 24.4 us
  starting transfers between devices  12.1 us (49%)
  Pallas kernels  7.43 us (30%)
  waiting for transfers between devices  4.73 us (19%)
    ppermute x10, starting transfers between devices, along(): return lax.ppermute(value, ('tx', 'ty', 'dose'), pairs)  12.1 us
    pallas_call x7, Pallas kernels, call(): pl.pallas_call(body, out_shape=tuple(outs), in_specs=[pl.BlockSpec(memory...  7.43 us
    ppermute x10, waiting for transfers between devices, along(): return lax.ppermute(value, ('tx', 'ty', 'dose'), pairs)  4.73 us
  transfers between devices with their start and end apart: 10, of which 3 were waited for; matrix products, arithmetic and copies ran while one was open for 0% of the time, Pallas kernels for 18%

profile of v6, /device:TPU:0, one launch (start us, length us, event | category | flops | bytes accessed | tf_op | source)
XLA Modules:
  0.0 24.4 jit_solution(9318810167844221360)
XLA Ops:
  0.0 1.1 %shard_map.55 = (f32[192,128]{1,0:T(8,128)S(1)}, f32[192,128]{1,0:T(8,128)S(1)}, f32[2,8,128]{2,1,0:T(8,128)S(1)}, f32[256,128]{1,0:T(8,128)S(1)}, f32[256,128]{1,0:T(8,128)S(1)}, /*index=5*/f32[512,128]{1,0:T(8,128)S(1)}) custom-call(f32[256,128]{1,0:T(8,128)} %bitcast.5, f32[256,128]{1,0:T(8,128)} %bitcast.6, f32[512,128]{1,0:T(8,128)} %bitcast.4, ...), custom_call_target="tpu_custom_call" | custom-call | bytes 1253448 | tf_op jit(solution)/shard_map/pallas_call | solution.py:519
  1.2 0.2 shard_map.56
  1.3 0.6 %collective-permute-start.1 = (f32[976,128]{1,0:T(8,128)S(1)}, f32[976,128]{1,0:T(8,128)S(1)}, u32[]{:S(2)}, u32[]{:S(2)}) collective-permute-start(f32[976,128]{1,0:T(8,128)S(1)} %get-tuple-element.22), channel_id=1, source_target_pairs={{0,2},{1,3},{2,0},{3,1},{4,6},{5,7},{6,4},{7,5},{8,10},{9,11},{10,... | collective-permute-start | bytes 1499144 | tf_op jit(solution)/shard_map/ppermute | solution.py:543
  1.9 2.6 %collective-permute-start = (f32[336,128]{1,0:T(8,128)S(1)}, f32[336,128]{1,0:T(8,128)S(1)}, u32[]{:S(2)}, u32[]{:S(2)}) collective-permute-start(f32[336,128]{1,0:T(8,128)S(1)} %get-tuple-element.21), channel_id=1, source_target_pairs={{0,1},{1,0},{2,3},{3,2},{4,5},{5,4},{6,7},{7,6},{8,9},{9,8},{10,11... | collective-permute-start | bytes 516104 | tf_op jit(solution)/shard_map/ppermute | solution.py:543
  4.4 1.6 %collective-permute-start.2 = (f32[192,128]{1,0:T(8,128)S(1)}, f32[192,128]{1,0:T(8,128)S(1)}, u32[]{:S(2)}, u32[]{:S(2)}) collective-permute-start(f32[192,128]{1,0:T(8,128)S(1)} %get-tuple-element.23), channel_id=1, source_target_pairs={{0,4},{1,5},{2,14},{3,15},{4,8},{5,9},{6,2},{7,3},{8,12},{9,13},{1... | collective-permute-start | bytes 294920 | tf_op jit(solution)/shard_map/ppermute | solution.py:543
  6.0 2.0 %collective-permute-start.3 = (f32[192,128]{1,0:T(8,128)S(1)}, f32[192,128]{1,0:T(8,128)S(1)}, u32[]{:S(2)}, u32[]{:S(2)}) collective-permute-start(f32[192,128]{1,0:T(8,128)S(1)} %get-tuple-element.24), channel_id=1, source_target_pairs={{0,14},{1,15},{2,4},{3,5},{4,2},{5,3},{6,8},{7,9},{8,6},{9,7},{10,... | collective-permute-start | bytes 294920 | tf_op jit(solution)/shard_map/ppermute | solution.py:543
  8.0 1.4 %collective-permute-done.refs_1_.refs_6_ = f32[336,128]{1,0:T(8,128)S(1)} collective-permute-done((f32[336,128]{1,0:T(8,128)S(1)}, f32[336,128]{1,0:T(8,128)S(1)}, u32[]{:S(2)}, u32[]{:S(2)}) %collective-permute-start) | collective-permute-done | bytes 172064 | tf_op jit(solution)/shard_map/ppermute | solution.py:543
  9.4 0.0 collective-permute-start.6
  9.4 0.0 collective-permute-done.1.refs_4_.refs_5_
  9.4 1.9 %collective-permute-start.7 = (f32[256,128]{1,0:T(8,128)S(1)}, f32[256,128]{1,0:T(8,128)S(1)}, u32[]{:S(2)}, u32[]{:S(2)}) collective-permute-start(f32[256,128]{1,0:T(8,128)S(1)} %pad_maximum_fusion), channel_id=1, source_target_pairs={{0,4},{1,5},{2,14},{3,15},{4,8},{5,9},{6,2},{7,3},{8,12},{9,13},{1... | collective-permute-start | bytes 393224 | tf_op jit(solution)/shard_map/ppermute | solution.py:543
  11.3 2.6 %collective-permute-start.8 = (f32[256,128]{1,0:T(8,128)S(1)}, f32[256,128]{1,0:T(8,128)S(1)}, u32[]{:S(2)}, u32[]{:S(2)}) collective-permute-start(f32[256,128]{1,0:T(8,128)S(1)} %pad_maximum_fusion.1), channel_id=1, source_target_pairs={{0,5},{1,4},{2,15},{3,14},{4,9},{5,8},{6,3},{7,2},{8,13},{9,12},{1... | collective-permute-start | bytes 393224 | tf_op jit(solution)/shard_map/ppermute | solution.py:543
  13.9 0.0 collective-permute-done.3.refs_2_
  13.9 0.8 %collective-permute-start.4 = (f32[192,128]{1,0:T(8,128)S(1)}, f32[192,128]{1,0:T(8,128)S(1)}, u32[]{:S(2)}, u32[]{:S(2)}) collective-permute-start(f32[192,128]{1,0:T(8,128)S(1)} %collective-permute-done.3.refs_2_), channel_id=1, source_target_pairs={{0,2},{1,3},{2,0},{3,1},{4,6},{5,7},{6,4},{7,5},{8,10},{9,11},{10,... | collective-permute-start | bytes 294920 | tf_op jit(solution)/shard_map/ppermute | solution.py:543
  14.7 0.0 collective-permute-done.2.refs_1_
  14.8 0.1 collective-permute-start.5
  14.8 1.5 %shard_map.57.refs_0_ = f32[192,6,8,128]{3,2,1,0:T(8,128)S(1)} custom-call(f32[2,8,128]{2,1,0:T(8,128)S(1)} %get-tuple-element.17.refs_0_, f32[336,128]{1,0:T(8,128)S(1)} %collective-permute-done.refs_1_.refs_6_, f32[256,128]{1,0:T(8,128)S(1)} %get-tuple-element.18.refs_1_.refs_2_, f32[256,128]{1,0:T(8,128)S(1)} %get-tuple-element.19.refs_2_.refs_3_, ...), custom_call_target="tpu_custom_call" | custom-call | flops 10000000 | bytes 5660672 | tf_op jit(solution)/shard_map/pallas_call | solution.py:519
  16.4 1.6 %shard_map.58.refs_1_ = f32[184,6,8,128]{3,2,1,0:T(8,128)S(1)} custom-call(f32[192,6,8,128]{3,2,1,0:T(8,128)S(1)} %shard_map.57.refs_0_, f32[192,128]{1,0:T(8,128)S(1)} %collective-permute-done.2.refs_1_, f32[192,128]{1,0:T(8,128)S(1)} %collective-permute-done.3.refs_2_), custom_call_target="tpu_custom_call" | custom-call | flops 10000000 | bytes 9437184 | tf_op jit(solution)/shard_map/pallas_call | solution.py:519
  18.0 0.0 collective-permute-done.4.refs_2_
  18.0 0.0 collective-permute-done.5.refs_3_
  18.0 0.0 collective-permute-done.6.refs_7_
  18.0 1.3 %shard_map.59.refs_2_ = f32[124,6,8,128]{3,2,1,0:T(8,128)S(1)} custom-call(f32[192,6,8,128]{3,2,1,0:T(8,128)S(1)} %shard_map.57.refs_0_, f32[184,6,8,128]{3,2,1,0:T(8,128)S(1)} %shard_map.58.refs_1_, f32[192,128]{1,0:T(8,128)S(1)} %collective-permute-done.4.refs_2_, f32[192,128]{1,0:T(8,128)S(1)} %collective-permute-done.5.refs_3_, ...), custom_call_target="tpu_custom_call" | custom-call | flops 10000000 | bytes 13590528 | tf_op jit(solution)/shard_map/pallas_call | solution.py:519
  19.3 0.0 collective-permute-done.7.refs_3_
  19.3 2.1 %collective-permute-done.8.refs_4_ = f32[256,128]{1,0:T(8,128)S(1)} collective-permute-done((f32[256,128]{1,0:T(8,128)S(1)}, f32[256,128]{1,0:T(8,128)S(1)}, u32[]{:S(2)}, u32[]{:S(2)}) %collective-permute-start.8) | collective-permute-done | bytes 131104 | tf_op jit(solution)/shard_map/ppermute | solution.py:543
  21.4 1.0 %shard_map.60 = (f32[4,16,128]{2,1,0:T(8,128)S(1)}, f32[4,16,128]{2,1,0:T(8,128)S(1)}) custom-call(f32[192,6,8,128]{3,2,1,0:T(8,128)S(1)} %shard_map.57.refs_0_, f32[184,6,8,128]{3,2,1,0:T(8,128)S(1)} %shard_map.58.refs_1_, f32[124,6,8,128]{3,2,1,0:T(8,128)S(1)} %shard_map.59.refs_2_, f32[256,128]{1,0:T(8,128)S(1)} %collective-permute-done.7.refs_3_, ...), custom_call_target="tpu_custom_call" | custom-call | flops 10000000 | bytes 12615680 | tf_op jit(solution)/shard_map/pallas_call | solution.py:519
  22.4 0.1 collective-permute-start.9
  22.5 1.2 %collective-permute-done.9.refs_1_ = f32[4,16,128]{2,1,0:T(8,128)S(1)} collective-permute-done((f32[4,16,128]{2,1,0:T(8,128)S(1)}, f32[4,16,128]{2,1,0:T(8,128)S(1)}, u32[]{:S(2)}, u32[]{:S(2)}) %collective-permute-start.9) | collective-permute-done | bytes 32800 | tf_op jit(solution)/shard_map/ppermute | solution.py:543
  23.7 0.6 %shard_map.61 = f32[128,128]{1,0:T(8,128)} custom-call(f32[4,16,128]{2,1,0:T(8,128)S(1)} %get-tuple-element.27.refs_0_, f32[4,16,128]{2,1,0:T(8,128)S(1)} %collective-permute-done.9.refs_1_), custom_call_target="tpu_custom_call" | custom-call | bytes 131072 | tf_op jit(solution)/shard_map/pallas_call | solution.py:519
  (3 shorter events, 0.0 us)
Async XLA Ops:
  1.3 8.1 %collective-permute-start.1 = (f32[976,128]{1,0:T(8,128)S(1)}, f32[976,128]{1,0:T(8,128)S(1)}, u32[]{:S(2)}, u32[]{:S(2)}) collective-permute-start(f32[976,128]{1,0:T(8,128)S(1)} %get-tuple-element.22), channel_id=1, source_target_pairs={{0,2},{1,3},{2,0},{3,1},{4,6},{5,7},{6,4},{7,5},{8,10},{9,11},{10,... | collective-permute-start | bytes 1499144 | tf_op jit(solution)/shard_map/ppermute | solution.py:543
  1.9 7.5 %collective-permute-start = (f32[336,128]{1,0:T(8,128)S(1)}, f32[336,128]{1,0:T(8,128)S(1)}, u32[]{:S(2)}, u32[]{:S(2)}) collective-permute-start(f32[336,128]{1,0:T(8,128)S(1)} %get-tuple-element.21), channel_id=1, source_target_pairs={{0,1},{1,0},{2,3},{3,2},{4,5},{5,4},{6,7},{7,6},{8,9},{9,8},{10,11... | collective-permute-start | bytes 516104 | tf_op jit(solution)/shard_map/ppermute | solution.py:543
  4.4 10.3 %collective-permute-start.2 = (f32[192,128]{1,0:T(8,128)S(1)}, f32[192,128]{1,0:T(8,128)S(1)}, u32[]{:S(2)}, u32[]{:S(2)}) collective-permute-start(f32[192,128]{1,0:T(8,128)S(1)} %get-tuple-element.23), channel_id=1, source_target_pairs={{0,4},{1,5},{2,14},{3,15},{4,8},{5,9},{6,2},{7,3},{8,12},{9,13},{1... | collective-permute-start | bytes 294920 | tf_op jit(solution)/shard_map/ppermute | solution.py:543
  6.0 7.9 %collective-permute-start.3 = (f32[192,128]{1,0:T(8,128)S(1)}, f32[192,128]{1,0:T(8,128)S(1)}, u32[]{:S(2)}, u32[]{:S(2)}) collective-permute-start(f32[192,128]{1,0:T(8,128)S(1)} %get-tuple-element.24), channel_id=1, source_target_pairs={{0,14},{1,15},{2,4},{3,5},{4,2},{5,3},{6,8},{7,9},{8,6},{9,7},{10,... | collective-permute-start | bytes 294920 | tf_op jit(solution)/shard_map/ppermute | solution.py:543
  9.4 8.6 %collective-permute-start.6 = (f32[336,128]{1,0:T(8,128)S(1)}, f32[336,128]{1,0:T(8,128)S(1)}, u32[]{:S(2)}, u32[]{:S(2)}) collective-permute-start(f32[336,128]{1,0:T(8,128)S(1)} %collective-permute-done.refs_1_.refs_6_), channel_id=1, source_target_pairs={{0,2},{1,3},{2,0},{3,1},{4,6},{5,7},{6,4},{7,5},{8,10},{9,11},{10,... | collective-permute-start | bytes 516104 | tf_op jit(solution)/shard_map/ppermute | solution.py:543
  9.4 9.9 %collective-permute-start.7 = (f32[256,128]{1,0:T(8,128)S(1)}, f32[256,128]{1,0:T(8,128)S(1)}, u32[]{:S(2)}, u32[]{:S(2)}) collective-permute-start(f32[256,128]{1,0:T(8,128)S(1)} %pad_maximum_fusion), channel_id=1, source_target_pairs={{0,4},{1,5},{2,14},{3,15},{4,8},{5,9},{6,2},{7,3},{8,12},{9,13},{1... | collective-permute-start | bytes 393224 | tf_op jit(solution)/shard_map/ppermute | solution.py:543
  11.3 10.1 %collective-permute-start.8 = (f32[256,128]{1,0:T(8,128)S(1)}, f32[256,128]{1,0:T(8,128)S(1)}, u32[]{:S(2)}, u32[]{:S(2)}) collective-permute-start(f32[256,128]{1,0:T(8,128)S(1)} %pad_maximum_fusion.1), channel_id=1, source_target_pairs={{0,5},{1,4},{2,15},{3,14},{4,9},{5,8},{6,3},{7,2},{8,13},{9,12},{1... | collective-permute-start | bytes 393224 | tf_op jit(solution)/shard_map/ppermute | solution.py:543
  13.9 4.1 %collective-permute-start.4 = (f32[192,128]{1,0:T(8,128)S(1)}, f32[192,128]{1,0:T(8,128)S(1)}, u32[]{:S(2)}, u32[]{:S(2)}) collective-permute-start(f32[192,128]{1,0:T(8,128)S(1)} %collective-permute-done.3.refs_2_), channel_id=1, source_target_pairs={{0,2},{1,3},{2,0},{3,1},{4,6},{5,7},{6,4},{7,5},{8,10},{9,11},{10,... | collective-permute-start | bytes 294920 | tf_op jit(solution)/shard_map/ppermute | solution.py:543
  14.8 3.2 %collective-permute-start.5 = (f32[192,128]{1,0:T(8,128)S(1)}, f32[192,128]{1,0:T(8,128)S(1)}, u32[]{:S(2)}, u32[]{:S(2)}) collective-permute-start(f32[192,128]{1,0:T(8,128)S(1)} %collective-permute-done.2.refs_1_), channel_id=1, source_target_pairs={{0,2},{1,3},{2,0},{3,1},{4,6},{5,7},{6,4},{7,5},{8,10},{9,11},{10,... | collective-permute-start | bytes 294920 | tf_op jit(solution)/shard_map/ppermute | solution.py:543
  22.4 1.3 %collective-permute-start.9 = (f32[4,16,128]{2,1,0:T(8,128)S(1)}, f32[4,16,128]{2,1,0:T(8,128)S(1)}, u32[]{:S(2)}, u32[]{:S(2)}) collective-permute-start(f32[4,16,128]{2,1,0:T(8,128)S(1)} %get-tuple-element.28), channel_id=1, source_target_pairs={{0,2},{1,3},{2,0},{3,1},{4,6},{5,7},{6,4},{7,5},{8,10},{9,11},{10,... | collective-permute-start | bytes 98312 | tf_op jit(solution)/shard_map/ppermute | solution.py:543

commit v7 on v6

--- a/solution.py
+++ b/solution.py
@@ -42,21 +42,53 @@
         return self.clamp(owner, halo, self.layers(halo))
 
 
-def dense_places(window, parts):
-    places, at = [], window.size - window.layers(parts[0][0])
-    for halo, count in parts:
-        places.append(at)
-        at += count * window.layers(halo)
-    at += window.size - window.layers(parts[-1][0])
-    return places, -(-at // SUB) * SUB
-
-
-def image_parts():
-    return ((HALO_AERIAL, HALO_AERIAL), (HALO_QUENCH, HALO_QUENCH))
-
-
-def cot_parts(count):
-    return ((HALO_COT, count),)
+class Dense:
+    def __init__(self, window, reaches, lead=True, tail=True, size=0):
+        self.window = window
+        slack = [window.size - window.layers(reach) for reach in reaches]
+        used = sum(window.layers(reach) for reach in reaches)
+        ends = (slack[0] if lead else 0) + (slack[-1] if tail else 0)
+        self.size = max(size, -(-(used + ends) // SUB) * SUB)
+        at = self.size - used if lead and not tail else slack[0] if lead else 0
+        self.rows = []
+        for reach in reaches:
+            self.rows.append((at, reach))
+            at += window.layers(reach)
+
+    def put(self, dst, i, src, base, rows, row, owner, block=0):
+        at, reach = self.rows[i]
+        first, layers = self.window.sent(owner, reach), self.window.layers(reach)
+        for g in range(0, layers, SUB):
+            n = min(SUB, layers - g)
+            value = src[pl.ds(base + rows * (first + g) + row, n, stride=rows), :]
+            dst[pl.ds(block + at + g, n), :] = value
+
+    def get(self, src, i, owner, block=0):
+        at, reach = self.rows[i]
+        window = self.window
+        start = block + at - (window.sent(owner, reach) - window.start(owner))
+        return [src[pl.ds(start + k, SUB, stride=window.groups), :] for k in range(window.groups)]
+
+
+def clear(dst, at, size):
+    dst[pl.ds(at, size), :] = jnp.zeros((size, dst.shape[1]), jnp.float32)
+
+
+def image_layout(window):
+    aerial = [HALO_AERIAL - i for i in range(1, HALO_AERIAL + 1)]
+    quench = [HALO_QUENCH - i for i in range(HALO_QUENCH, 0, -1)]
+    return Dense(window, aerial + quench)
+
+
+def halo_layouts(window, local):
+    reaches = [HALO_COT - i for _ in range(local) for i in range(1, HALO_COT + 1)]
+    size = Dense(window, reaches, lead=False).size
+    first = Dense(window, reaches, tail=False, size=size)
+    return first, Dense(window, reaches, lead=False, size=first.size)
+
+
+def whole_layout(rows, window, local):
+    return Dense(window, [HALO_COT] * (local * rows))
 
 
 def chip_row(rows, row):
@@ -65,23 +97,6 @@
 
 def vector(ref, rows, groups, first, row, base=0):
     return ref[pl.ds(base + rows * first + row, SUB, stride=rows * groups), :]
-
-
-def put_dense(dst, at, src, base, rows, row, first, layers):
-    for g in range(0, layers, SUB):
-        n = min(SUB, layers - g)
-        dst[pl.ds(at + g, n), :] = src[pl.ds(base + rows * (first + g) + row, n, stride=rows), :]
-
-
-def clear_ends(dst):
-    zero = jnp.zeros((SUB, dst.shape[1]), jnp.float32)
-    dst[pl.ds(0, SUB), :] = zero
-    dst[pl.ds(dst.shape[0] - SUB, SUB), :] = zero
-
-
-def from_dense(src, at, window, owner, halo):
-    start = at - (window.sent(owner, halo) - window.start(owner))
-    return [src[pl.ds(start + k, SUB, stride=window.groups), :] for k in range(window.groups)]
 
 
 def image_kernel(rows, window, local, *refs):
@@ -91,17 +106,18 @@
     copies = [pltpu.make_async_copy(src, dst, sems.at[i]) for i, (src, dst) in enumerate(pairs)]
     for copy in copies:
         copy.start()
-    clear_ends(image_s)
-    clear_ends(image_c)
+    layout = image_layout(window)
+    for ref in (image_s, image_c):
+        clear(ref, 0, SUB)
+        clear(ref, layout.size - 2 * SUB, 2 * SUB)
     owner = lax.axis_index("dose")
-    places, _ = dense_places(window, image_parts())
     copies[0].wait()
     copies[1].wait()
-    for src, at, width in ((aerial, places[0], HALO_AERIAL), (quench, places[1], HALO_QUENCH)):
-        layers, first = window.layers(width), window.sent(owner, width)
-        for i in range(width):
-            for dst, row in ((image_s, rows - width + i), (image_c, width - 1 - i)):
-                put_dense(dst, at + i * layers, src, 0, rows, chip_row(rows, row), first, layers)
+    order = [(aerial, i) for i in range(1, HALO_AERIAL + 1)]
+    order += [(quench, i) for i in range(HALO_QUENCH, 0, -1)]
+    for place, (src, i) in enumerate(order):
+        layout.put(image_s, place, src, 0, rows, chip_row(rows, rows - i), owner)
+        layout.put(image_c, place, src, 0, rows, chip_row(rows, i - 1), owner)
     for copy in copies[2:]:
         copy.wait()
     for d in range(local):
@@ -110,42 +126,45 @@
 
 def swap_layout(rows, window, local):
     vectors = 2 * rows + local * (rows // 2 + HALO_COT)
-    halo = dense_places(window, cot_parts(local * HALO_COT))[1]
-    return vectors * window.groups * SUB, halo
+    return vectors * window.groups * SUB, halo_layouts(window, local)[0].size
 
 
 def swapped(swap, groups, place):
     return [swap[pl.ds((place * groups + k) * SUB, SUB), :] for k in range(groups)]
 
 
-def rest_kernel(rows, window, local, dose, aerial, quench, cot, swap, *dense):
+def rest_kernel(rows, window, local, aerial, quench, cot, swap, *dense):
     depth, groups, doses = window.depth, window.groups, window.doses
     area = rows * depth
     inner = rows // 2 + HALO_COT
     owner = lax.axis_index("dose")
-    layers = window.layers(HALO_COT)
     sends = dense[:doses]
     wholes = dense[doses:]
     handed, halo = swap_layout(rows, window, local)
-    for ref in dense:
-        clear_ends(ref)
-    lead = window.size - layers
-    zero = jnp.zeros((SUB, swap.shape[1]), jnp.float32)
+    layouts = halo_layouts(window, local)
+    whole = whole_layout(rows, window, local)
     for k in range(doses):
-        first = window.sent(lax.rem(owner + k, doses), HALO_COT)
+        target = lax.rem(owner + k, doses)
         block = handed + k * halo
-        swap[pl.ds(block, SUB), :] = zero
-        swap[pl.ds(block + halo - SUB, SUB), :] = zero
+        mine, given = layouts if k % 2 == 0 else layouts[::-1]
+        for ref, at in ((sends[k], 0), (swap, block)):
+            clear(ref, at, 2 * SUB)
+            clear(ref, at + halo - 2 * SUB, 2 * SUB)
         for d in range(local):
-            for i in range(HALO_COT):
-                at = lead + (d * HALO_COT + i) * layers
-                put_dense(sends[k], at, cot, d * area, rows, chip_row(rows, rows - HALO_COT + i), first, layers)
-                put_dense(swap, block + at, cot, d * area, rows, chip_row(rows, HALO_COT - 1 - i), first, layers)
-            if k:
+            for i in range(1, HALO_COT + 1):
+                outer, inward = chip_row(rows, rows - i), chip_row(rows, i - 1)
+                if k % 2:
+                    outer, inward = inward, outer
+                place = d * HALO_COT + i - 1
+                mine.put(sends[k], place, cot, d * area, rows, outer, target)
+                given.put(swap, place, cot, d * area, rows, inward, target, block)
+        if k:
+            ref = wholes[k - 1]
+            clear(ref, 0, SUB)
+            clear(ref, whole.size - 2 * SUB, 2 * SUB)
+            for d in range(local):
                 for row in range(rows):
-                    at = lead + (d * rows + row) * layers
-                    put_dense(wholes[k - 1], at, cot, d * area, rows, row, first, layers)
-                wholes[k - 1][pl.ds(wholes[k - 1].shape[0] - (local - d) * SUB, SUB), :] = dose[d]
+                    whole.put(ref, d * rows + row, cot, d * area, rows, row, target)
     place = 0
     parts = [(aerial, 0, rows), (quench, 0, rows)] + [(cot, d * area, inner) for d in range(local)]
     start = window.start(owner)
@@ -350,8 +369,7 @@
     for row in range(rows):
         fields.put("q0", 0, row, source(quench, rows, row))
     for d in range(total):
-        ref, i = dose_refs[d // local], d % local
-        dose = ref[pl.ds(ref.shape[0] - (local - i) * SUB, SUB), :] if d >= local else ref[i]
+        dose = dose_refs[d // local][d % local]
         fields.put("dose", d, 0, [dose] * (2 * groups))
         rate = -exposure_rate * dose
         for row in range(rows):
@@ -367,18 +385,17 @@
     fields = Fields(rows, total, (near, near_rows), (far, far_rows))
     table = dict(far_rows(rows), e=(0, 0))
     owner = lax.axis_index("dose")
-    places, _ = dense_places(window, image_parts())
-
-    def source(part, halo, row):
-        at = places[part] + (halo + row) * window.layers(halo)
-        return [v for src in (image_s, image_c) for v in from_dense(src, at, window, owner, halo)]
+    layout = image_layout(window)
+
+    def source(place):
+        return [v for src in (image_s, image_c) for v in layout.get(src, place, owner)]
 
     for row in range(-HALO_QUENCH, 0):
-        fields.put("q0", 0, row, source(1, HALO_QUENCH, row))
+        fields.put("q0", 0, row, source(HALO_AERIAL + HALO_QUENCH + row))
     for d in range(total):
         rate = -exposure_rate * fields.get("dose", d, 0)[0]
         for row in range(-HALO_AERIAL, 0):
-            fields.put("a0", d, row, [1.0 - jnp.exp(rate * v) for v in source(0, HALO_AERIAL, row)])
+            fields.put("a0", d, row, [1.0 - jnp.exp(rate * v) for v in source(-1 - row)])
         forward_rows(spread, fields, d, table)
 
 
@@ -423,14 +440,12 @@
     spread = make_spread()
     owner = lax.axis_index("dose")
     start = window.start(owner)
-    layers = window.layers(HALO_COT)
-    lead = window.size - layers
-    places, _ = dense_places(window, image_parts())
-    last = places[0] + (HALO_AERIAL - 1) * window.layers(HALO_AERIAL)
+    image = image_layout(window)
+    whole = whole_layout(rows, window, local)
     for d in range(total):
         past = Fields(rows, total, (near, near_rows), (far, far_rows))
         rate = -exposure_rate * past.get("dose", d, 0)[0]
-        light = [v for src in (extra_own, extra_par) for v in from_dense(src, last, window, owner, HALO_AERIAL)]
+        light = [v for src in (extra_own, extra_par) for v in image.get(src, 0, owner)]
         past.more["a0", d, rows] = [1.0 - jnp.exp(rate * v) for v in light]
         for n in range(3):
             row = rows - 1 - n
@@ -446,9 +461,9 @@
                 value = [vector(cot, rows, groups, start + g, chip_row(rows, row), i * area) for g in range(groups)]
                 value += swapped(swap, groups, 2 * rows + i * inner + row)
             else:
-                at = lead + (i * rows + chip_row(rows, row)) * layers
+                at = chip_row(rows, row) * window.layers(HALO_COT)
                 sides = (wholes[2 * k - 2], wholes[2 * k - 1])
-                value = [v for src in sides for v in from_dense(src, at, window, owner, HALO_COT)]
+                value = [v for src in sides for v in whole.get(src, i * rows, owner, at)]
             back.put("ct", d, row, value)
         backward_rows(spread, past, back, d, table)
 
@@ -457,12 +472,10 @@
     doses, groups = window.doses, window.groups
     sends = refs[:doses]
     mine, other, store, full = refs[doses:]
-    halo = swap_layout(rows, window, local)[1]
+    layouts = halo_layouts(window, local)
     half = rows // 2
     total = local * doses
     owner = lax.axis_index("dose")
-    layers = window.layers(HALO_COT)
-    lead = window.size - layers
     spread = make_spread()
     past = Fields(rows, total, (near, near_rows), (far, far_rows))
     back = Fields(rows, total, (back_near, back_near_rows), (store, back_far_rows))
@@ -470,9 +483,9 @@
     for d in range(total):
         k, i = divmod(d, local)
         for row in range(*table["ct"]):
-            at = lead + (i * HALO_COT + HALO_COT + row) * layers
-            places = (at, at + halo)
-            back.put("ct", d, row, [v for p in places for v in from_dense(sends[k], p, window, owner, HALO_COT)])
+            place = i * HALO_COT - 1 - row
+            value = layouts[0].get(sends[k], place, owner)
+            back.put("ct", d, row, value + layouts[1].get(sends[k], place, owner, layouts[0].size))
         backward_rows(spread, past, back, d, table)
     for row in range(half):
         value = back.get("g", 0, row)
@@ -545,9 +558,9 @@
     def across(value):
         return along(value, cross=1, step=0)
 
-    images = array(dense_places(window, image_parts())[1])
+    images = array(image_layout(window).size)
     handed, halo = swap_layout(rows, window, local)
-    whole = array(dense_places(window, cot_parts(local * rows))[1] + local * SUB)
+    whole = array(whole_layout(rows, window, local).size)
     flat = [jax.ShapeDtypeStruct(x.shape, f32) for x in (aerial, quench, cot)]
     image_s, image_c, dose, aerial, quench, cot = call(
         image_kernel,
@@ -566,20 +579,20 @@
     rest = call(
         rest_kernel,
         (rows, window, local),
-        (dose, aerial, quench, cot),
+        (aerial, quench, cot),
         [array(handed + doses * halo)] + [array(halo)] * doses + [whole] * (doses - 1),
     )
     swap = across(rest[0])
     values, wholes = [dose], []
     for k in range(1, doses):
         arrived = along(rest[doses + k], step=0, k=k)
-        values.append(arrived)
+        values.append(along(dose, step=0, k=k))
         wholes += [arrived, across(arrived)]
     sends = []
     for k in range(doses):
         other = lax.slice_in_dim(swap, handed + k * halo, handed + (k + 1) * halo)
-        both = jnp.concatenate((rest[1 + k], other), axis=0)
-        sends.append(along(both, k=k))
+        both = jnp.concatenate((other, rest[1 + k]) if k % 2 else (rest[1 + k], other), axis=0)
+        sends.append(along(both, cross=k % 2, k=k))
 
     (near,) = call(
         near_kernel, (rows, window, local), values + [aerial, quench, swap], [array(*store(near_rows))], flops=10_000_000

time: 24.5 us -> 23.5 us (0.959)
  waiting for transfers between devices: 4.73 us -> 3.06 us
  starting transfers between devices: 12.1 us -> 12.8 us
    ppermute x10 -> x11, waiting for transfers between devices: 4.73 us -> 3.06 us  [along(): return lax.ppermute(value, ('tx', 'ty', 'dose'), pairs)]
    ppermute x10 -> x11, starting transfers between devices: 12.1 us -> 12.8 us  [along(): return lax.ppermute(value, ('tx', 'ty', 'dose'), pairs)]
  transfers between devices with their start and end apart: 10 -> 11, of which waited for: 3 -> 3; matrix products, arithmetic and copies ran while one was open for 0% -> 0% of each run, Pallas kernels for 18% -> 19%
where the time goes in v7:
time: 23.5 us; the launch traced here: 23.3 us
  starting transfers between devices  12.8 us (54%)
  Pallas kernels  7.37 us (31%)
  waiting for transfers between devices  3.06 us (13%)
    ppermute x11, starting transfers between devices, along(): return lax.ppermute(value, ('tx', 'ty', 'dose'), pairs)  12.8 us
    pallas_call x7, Pallas kernels, call(): pl.pallas_call(body, out_shape=tuple(outs), in_specs=[pl.BlockSpec(memory...  7.37 us
    ppermute x11, waiting for transfers between devices, along(): return lax.ppermute(value, ('tx', 'ty', 'dose'), pairs)  3.06 us
  transfers between devices with their start and end apart: 11, of which 3 were waited for; matrix products, arithmetic and copies ran while one was open for 0% of the time, Pallas kernels for 19%

profile of v7, /device:TPU:0, one launch (start us, length us, event | category | flops | bytes accessed | tf_op | source)
XLA Modules:
  0.0 23.3 jit_solution(10035070776027805222)
XLA Ops:
  0.0 1.1 %shard_map.55 = (f32[176,128]{1,0:T(8,128)S(1)}, f32[176,128]{1,0:T(8,128)S(1)}, f32[2,8,128]{2,1,0:T(8,128)S(1)}, f32[256,128]{1,0:T(8,128)S(1)}, f32[256,128]{1,0:T(8,128)S(1)}, /*index=5*/f32[512,128]{1,0:T(8,128)S(1)}) custom-call(f32[256,128]{1,0:T(8,128)} %bitcast.5, f32[256,128]{1,0:T(8,128)} %bitcast.6, f32[512,128]{1,0:T(8,128)} %bitcast.4, ...), custom_call_target="tpu_custom_call" | custom-call | bytes 1237064 | tf_op jit(solution)/shard_map/pallas_call | solution.py:532
  1.2 0.2 shard_map.56
  1.3 0.6 %collective-permute-start.1 = (f32[944,128]{1,0:T(8,128)S(1)}, f32[944,128]{1,0:T(8,128)S(1)}, u32[]{:S(2)}, u32[]{:S(2)}) collective-permute-start(f32[944,128]{1,0:T(8,128)S(1)} %get-tuple-element.21), channel_id=1, source_target_pairs={{0,2},{1,3},{2,0},{3,1},{4,6},{5,7},{6,4},{7,5},{8,10},{9,11},{10,... | collective-permute-start | bytes 1449992 | tf_op jit(solution)/shard_map/ppermute | solution.py:556
  1.9 2.6 %collective-permute-start.6 = (f32[320,128]{1,0:T(8,128)S(1)}, f32[320,128]{1,0:T(8,128)S(1)}, u32[]{:S(2)}, u32[]{:S(2)}) collective-permute-start(f32[320,128]{1,0:T(8,128)S(1)} %get-tuple-element.24), channel_id=1, source_target_pairs={{0,1},{1,0},{2,3},{3,2},{4,5},{5,4},{6,7},{7,6},{8,9},{9,8},{10,11... | collective-permute-start | bytes 491528 | tf_op jit(solution)/shard_map/ppermute | solution.py:556
  4.4 0.1 collective-permute-start
  4.5 2.0 %collective-permute-start.2 = (f32[176,128]{1,0:T(8,128)S(1)}, f32[176,128]{1,0:T(8,128)S(1)}, u32[]{:S(2)}, u32[]{:S(2)}) collective-permute-start(f32[176,128]{1,0:T(8,128)S(1)} %get-tuple-element.22), channel_id=1, source_target_pairs={{0,4},{1,5},{2,14},{3,15},{4,8},{5,9},{6,2},{7,3},{8,12},{9,13},{1... | collective-permute-start | bytes 270344 | tf_op jit(solution)/shard_map/ppermute | solution.py:556
  6.5 1.7 %collective-permute-start.3 = (f32[176,128]{1,0:T(8,128)S(1)}, f32[176,128]{1,0:T(8,128)S(1)}, u32[]{:S(2)}, u32[]{:S(2)}) collective-permute-start(f32[176,128]{1,0:T(8,128)S(1)} %get-tuple-element.23), channel_id=1, source_target_pairs={{0,14},{1,15},{2,4},{3,5},{4,2},{5,3},{6,8},{7,9},{8,6},{9,7},{10,... | collective-permute-start | bytes 270344 | tf_op jit(solution)/shard_map/ppermute | solution.py:556
  8.2 1.1 %collective-permute-done.6.refs_6_ = f32[320,128]{1,0:T(8,128)S(1)} collective-permute-done((f32[320,128]{1,0:T(8,128)S(1)}, f32[320,128]{1,0:T(8,128)S(1)}, u32[]{:S(2)}, u32[]{:S(2)}) %collective-permute-start.6) | collective-permute-done | bytes 163872 | tf_op jit(solution)/shard_map/ppermute | solution.py:556
  9.3 0.0 collective-permute-start.7
  9.3 0.0 collective-permute-done.1.refs_4_.refs_5_
  9.4 1.9 %collective-permute-start.8 = (f32[224,128]{1,0:T(8,128)S(1)}, f32[224,128]{1,0:T(8,128)S(1)}, u32[]{:S(2)}, u32[]{:S(2)}) collective-permute-start(f32[224,128]{1,0:T(8,128)S(1)} %pad_maximum_fusion), channel_id=1, source_target_pairs={{0,4},{1,5},{2,14},{3,15},{4,8},{5,9},{6,2},{7,3},{8,12},{9,13},{1... | collective-permute-start | bytes 344072 | tf_op jit(solution)/shard_map/ppermute | solution.py:556
  11.2 0.0 collective-permute-done.refs_1_
  11.3 3.3 %collective-permute-start.9 = (f32[224,128]{1,0:T(8,128)S(1)}, f32[224,128]{1,0:T(8,128)S(1)}, u32[]{:S(2)}, u32[]{:S(2)}) collective-permute-start(f32[224,128]{1,0:T(8,128)S(1)} %pad_maximum_fusion.1), channel_id=1, source_target_pairs={{0,15},{1,14},{2,5},{3,4},{4,3},{5,2},{6,9},{7,8},{8,7},{9,6},{10,... | collective-permute-start | bytes 344072 | tf_op jit(solution)/shard_map/ppermute | solution.py:556
  14.6 0.0 collective-permute-done.3.refs_2_
  14.6 0.0 collective-permute-start.4
  14.6 0.0 collective-permute-done.2.refs_1_
  14.6 0.5 %collective-permute-start.5 = (f32[176,128]{1,0:T(8,128)S(1)}, f32[176,128]{1,0:T(8,128)S(1)}, u32[]{:S(2)}, u32[]{:S(2)}) collective-permute-start(f32[176,128]{1,0:T(8,128)S(1)} %collective-permute-done.2.refs_1_), channel_id=1, source_target_pairs={{0,2},{1,3},{2,0},{3,1},{4,6},{5,7},{6,4},{7,5},{8,10},{9,11},{10,... | collective-permute-start | bytes 270344 | tf_op jit(solution)/shard_map/ppermute | solution.py:556
  15.1 1.5 %shard_map.57.refs_0_ = f32[192,6,8,128]{3,2,1,0:T(8,128)S(1)} custom-call(f32[2,8,128]{2,1,0:T(8,128)S(1)} %get-tuple-element.17.refs_0_, f32[2,8,128]{2,1,0:T(8,128)S(1)} %collective-permute-done.refs_1_, f32[256,128]{1,0:T(8,128)S(1)} %get-tuple-element.18.refs_0_.refs_2_, f32[256,128]{1,0:T(8,128)S(1)} %get-tuple-element.19.refs_1_.refs_3_, ...), custom_call_target="tpu_custom_call" | custom-call | flops 10000000 | bytes 5480448 | tf_op jit(solution)/shard_map/pallas_call | solution.py:532
  16.6 1.6 %shard_map.58.refs_1_ = f32[184,6,8,128]{3,2,1,0:T(8,128)S(1)} custom-call(f32[192,6,8,128]{3,2,1,0:T(8,128)S(1)} %shard_map.57.refs_0_, f32[176,128]{1,0:T(8,128)S(1)} %collective-permute-done.2.refs_1_, f32[176,128]{1,0:T(8,128)S(1)} %collective-permute-done.3.refs_2_), custom_call_target="tpu_custom_call" | custom-call | flops 10000000 | bytes 9420800 | tf_op jit(solution)/shard_map/pallas_call | solution.py:532
  18.2 0.0 collective-permute-done.4.refs_2_
  18.2 0.0 collective-permute-done.5.refs_3_
  18.2 0.0 collective-permute-done.7.refs_7_
  18.3 1.3 %shard_map.59.refs_2_ = f32[124,6,8,128]{3,2,1,0:T(8,128)S(1)} custom-call(f32[192,6,8,128]{3,2,1,0:T(8,128)S(1)} %shard_map.57.refs_0_, f32[184,6,8,128]{3,2,1,0:T(8,128)S(1)} %shard_map.58.refs_1_, f32[176,128]{1,0:T(8,128)S(1)} %collective-permute-done.4.refs_2_, f32[176,128]{1,0:T(8,128)S(1)} %collective-permute-done.5.refs_3_, ...), custom_call_target="tpu_custom_call" | custom-call | flops 10000000 | bytes 13541376 | tf_op jit(solution)/shard_map/pallas_call | solution.py:532
  19.5 0.0 collective-permute-done.8.refs_3_
  19.5 0.8 %collective-permute-done.9.refs_4_ = f32[224,128]{1,0:T(8,128)S(1)} collective-permute-done((f32[224,128]{1,0:T(8,128)S(1)}, f32[224,128]{1,0:T(8,128)S(1)}, u32[]{:S(2)}, u32[]{:S(2)}) %collective-permute-start.9) | collective-permute-done | bytes 114720 | tf_op jit(solution)/shard_map/ppermute | solution.py:556
  20.4 1.0 %shard_map.60 = (f32[4,16,128]{2,1,0:T(8,128)S(1)}, f32[4,16,128]{2,1,0:T(8,128)S(1)}) custom-call(f32[192,6,8,128]{3,2,1,0:T(8,128)S(1)} %shard_map.57.refs_0_, f32[184,6,8,128]{3,2,1,0:T(8,128)S(1)} %shard_map.58.refs_1_, f32[124,6,8,128]{3,2,1,0:T(8,128)S(1)} %shard_map.59.refs_2_, f32[224,128]{1,0:T(8,128)S(1)} %collective-permute-done.8.refs_3_, ...), custom_call_target="tpu_custom_call" | custom-call | flops 10000000 | bytes 12582912 | tf_op jit(solution)/shard_map/pallas_call | solution.py:532
  21.4 0.2 collective-permute-start.10
  21.6 1.1 %collective-permute-done.10.refs_1_ = f32[4,16,128]{2,1,0:T(8,128)S(1)} collective-permute-done((f32[4,16,128]{2,1,0:T(8,128)S(1)}, f32[4,16,128]{2,1,0:T(8,128)S(1)}, u32[]{:S(2)}, u32[]{:S(2)}) %collective-permute-start.10) | collective-permute-done | bytes 32800 | tf_op jit(solution)/shard_map/ppermute | solution.py:556
  22.7 0.6 %shard_map.61 = f32[128,128]{1,0:T(8,128)} custom-call(f32[4,16,128]{2,1,0:T(8,128)S(1)} %get-tuple-element.27.refs_0_, f32[4,16,128]{2,1,0:T(8,128)S(1)} %collective-permute-done.10.refs_1_), custom_call_target="tpu_custom_call" | custom-call | bytes 131072 | tf_op jit(solution)/shard_map/pallas_call | solution.py:532
  (3 shorter events, 0.0 us)
Async XLA Ops:
  1.3 8.0 %collective-permute-start.1 = (f32[944,128]{1,0:T(8,128)S(1)}, f32[944,128]{1,0:T(8,128)S(1)}, u32[]{:S(2)}, u32[]{:S(2)}) collective-permute-start(f32[944,128]{1,0:T(8,128)S(1)} %get-tuple-element.21), channel_id=1, source_target_pairs={{0,2},{1,3},{2,0},{3,1},{4,6},{5,7},{6,4},{7,5},{8,10},{9,11},{10,... | collective-permute-start | bytes 1449992 | tf_op jit(solution)/shard_map/ppermute | solution.py:556
  1.9 7.4 %collective-permute-start.6 = (f32[320,128]{1,0:T(8,128)S(1)}, f32[320,128]{1,0:T(8,128)S(1)}, u32[]{:S(2)}, u32[]{:S(2)}) collective-permute-start(f32[320,128]{1,0:T(8,128)S(1)} %get-tuple-element.24), channel_id=1, source_target_pairs={{0,1},{1,0},{2,3},{3,2},{4,5},{5,4},{6,7},{7,6},{8,9},{9,8},{10,11... | collective-permute-start | bytes 491528 | tf_op jit(solution)/shard_map/ppermute | solution.py:556
  4.4 6.8 %collective-permute-start = (f32[2,8,128]{2,1,0:T(8,128)S(1)}, f32[2,8,128]{2,1,0:T(8,128)S(1)}, u32[]{:S(2)}, u32[]{:S(2)}) collective-permute-start(f32[2,8,128]{2,1,0:T(8,128)S(1)} %get-tuple-element.17.refs_0_), channel_id=1, source_target_pairs={{0,1},{1,0},{2,3},{3,2},{4,5},{5,4},{6,7},{7,6},{8,9},{9,8},{10,11... | collective-permute-start | bytes 24584 | tf_op jit(solution)/shard_map/ppermute | solution.py:556
  4.5 10.1 %collective-permute-start.2 = (f32[176,128]{1,0:T(8,128)S(1)}, f32[176,128]{1,0:T(8,128)S(1)}, u32[]{:S(2)}, u32[]{:S(2)}) collective-permute-start(f32[176,128]{1,0:T(8,128)S(1)} %get-tuple-element.22), channel_id=1, source_target_pairs={{0,4},{1,5},{2,14},{3,15},{4,8},{5,9},{6,2},{7,3},{8,12},{9,13},{1... | collective-permute-start | bytes 270344 | tf_op jit(solution)/shard_map/ppermute | solution.py:556
  6.5 8.0 %collective-permute-start.3 = (f32[176,128]{1,0:T(8,128)S(1)}, f32[176,128]{1,0:T(8,128)S(1)}, u32[]{:S(2)}, u32[]{:S(2)}) collective-permute-start(f32[176,128]{1,0:T(8,128)S(1)} %get-tuple-element.23), channel_id=1, source_target_pairs={{0,14},{1,15},{2,4},{3,5},{4,2},{5,3},{6,8},{7,9},{8,6},{9,7},{10,... | collective-permute-start | bytes 270344 | tf_op jit(solution)/shard_map/ppermute | solution.py:556
  9.3 8.9 %collective-permute-start.7 = (f32[320,128]{1,0:T(8,128)S(1)}, f32[320,128]{1,0:T(8,128)S(1)}, u32[]{:S(2)}, u32[]{:S(2)}) collective-permute-start(f32[320,128]{1,0:T(8,128)S(1)} %collective-permute-done.6.refs_6_), channel_id=1, source_target_pairs={{0,2},{1,3},{2,0},{3,1},{4,6},{5,7},{6,4},{7,5},{8,10},{9,11},{10,... | collective-permute-start | bytes 491528 | tf_op jit(solution)/shard_map/ppermute | solution.py:556
  9.4 10.2 %collective-permute-start.8 = (f32[224,128]{1,0:T(8,128)S(1)}, f32[224,128]{1,0:T(8,128)S(1)}, u32[]{:S(2)}, u32[]{:S(2)}) collective-permute-start(f32[224,128]{1,0:T(8,128)S(1)} %pad_maximum_fusion), channel_id=1, source_target_pairs={{0,4},{1,5},{2,14},{3,15},{4,8},{5,9},{6,2},{7,3},{8,12},{9,13},{1... | collective-permute-start | bytes 344072 | tf_op jit(solution)/shard_map/ppermute | solution.py:556
  11.3 9.1 %collective-permute-start.9 = (f32[224,128]{1,0:T(8,128)S(1)}, f32[224,128]{1,0:T(8,128)S(1)}, u32[]{:S(2)}, u32[]{:S(2)}) collective-permute-start(f32[224,128]{1,0:T(8,128)S(1)} %pad_maximum_fusion.1), channel_id=1, source_target_pairs={{0,15},{1,14},{2,5},{3,4},{4,3},{5,2},{6,9},{7,8},{8,7},{9,6},{10,... | collective-permute-start | bytes 344072 | tf_op jit(solution)/shard_map/ppermute | solution.py:556
  14.6 3.7 %collective-permute-start.4 = (f32[176,128]{1,0:T(8,128)S(1)}, f32[176,128]{1,0:T(8,128)S(1)}, u32[]{:S(2)}, u32[]{:S(2)}) collective-permute-start(f32[176,128]{1,0:T(8,128)S(1)} %collective-permute-done.3.refs_2_), channel_id=1, source_target_pairs={{0,2},{1,3},{2,0},{3,1},{4,6},{5,7},{6,4},{7,5},{8,10},{9,11},{10,... | collective-permute-start | bytes 270344 | tf_op jit(solution)/shard_map/ppermute | solution.py:556
  14.6 3.7 %collective-permute-start.5 = (f32[176,128]{1,0:T(8,128)S(1)}, f32[176,128]{1,0:T(8,128)S(1)}, u32[]{:S(2)}, u32[]{:S(2)}) collective-permute-start(f32[176,128]{1,0:T(8,128)S(1)} %collective-permute-done.2.refs_1_), channel_id=1, source_target_pairs={{0,2},{1,3},{2,0},{3,1},{4,6},{5,7},{6,4},{7,5},{8,10},{9,11},{10,... | collective-permute-start | bytes 270344 | tf_op jit(solution)/shard_map/ppermute | solution.py:556
  21.4 1.3 %collective-permute-start.10 = (f32[4,16,128]{2,1,0:T(8,128)S(1)}, f32[4,16,128]{2,1,0:T(8,128)S(1)}, u32[]{:S(2)}, u32[]{:S(2)}) collective-permute-start(f32[4,16,128]{2,1,0:T(8,128)S(1)} %get-tuple-element.28), channel_id=1, source_target_pairs={{0,2},{1,3},{2,0},{3,1},{4,6},{5,7},{6,4},{7,5},{8,10},{9,11},{10,... | collective-permute-start | bytes 98312 | tf_op jit(solution)/shard_map/ppermute | solution.py:556

commit v8 on v7

--- a/solution.py
+++ b/solution.py
@@ -78,6 +78,10 @@
     aerial = [HALO_AERIAL - i for i in range(1, HALO_AERIAL + 1)]
     quench = [HALO_QUENCH - i for i in range(HALO_QUENCH, 0, -1)]
     return Dense(window, aerial + quench)
+
+
+def crosses(k):
+    return k % 2 == 0
 
 
 def halo_layouts(window, local):
@@ -146,14 +150,14 @@
     for k in range(doses):
         target = lax.rem(owner + k, doses)
         block = handed + k * halo
-        mine, given = layouts if k % 2 == 0 else layouts[::-1]
+        mine, given = layouts[::-1] if crosses(k) else layouts
         for ref, at in ((sends[k], 0), (swap, block)):
             clear(ref, at, 2 * SUB)
             clear(ref, at + halo - 2 * SUB, 2 * SUB)
         for d in range(local):
             for i in range(1, HALO_COT + 1):
                 outer, inward = chip_row(rows, rows - i), chip_row(rows, i - 1)
-                if k % 2:
+                if crosses(k):
                     outer, inward = inward, outer
                 place = d * HALO_COT + i - 1
                 mine.put(sends[k], place, cot, d * area, rows, outer, target)
@@ -283,16 +287,16 @@
 
 
 class Fields:
-    def __init__(self, rows, local, *stores):
-        self.stores = [(ref, places_of(table(rows), local)[0]) for ref, table in stores]
+    def __init__(self, rows, *stores):
+        self.stores = [(ref, places_of(table(rows), count)[0], first) for ref, table, first, count in stores]
         self.more = {}
 
     def get(self, name, d, row):
         if (name, d, row) in self.more:
             return self.more[name, d, row]
-        for ref, places in self.stores:
-            if (name, d, row) in places:
-                at = places[name, d, row]
+        for ref, places, first in self.stores:
+            if (name, d - first, row) in places:
+                at = places[name, d - first, row]
                 return [ref[at, i] for i in range(ref.shape[1])]
         raise KeyError((name, row))
 
@@ -300,8 +304,8 @@
         return [self.get(name, d, row + i) for i in (-1, 0, 1)]
 
     def put(self, name, d, row, value):
-        ref, places = self.stores[-1]
-        at = places[name, d, row]
+        ref, places, first = self.stores[-1]
+        at = places[name, d - first, row]
         for i in range(len(value)):
             ref[at, i] = value[i]
 
@@ -359,7 +363,7 @@
     half = rows // 2
     spread = make_spread()
     total = local * doses
-    fields = Fields(rows, total, (near, near_rows))
+    fields = Fields(rows, (near, near_rows, 0, total))
     start = window.start(lax.axis_index("dose"))
 
     def source(raw, at, row):
@@ -382,7 +386,7 @@
 
 def far_kernel(rows, window, total, near, image_s, image_c, far):
     spread = make_spread()
-    fields = Fields(rows, total, (near, near_rows), (far, far_rows))
+    fields = Fields(rows, (near, near_rows, 0, total), (far, far_rows, 0, total))
     table = dict(far_rows(rows), e=(0, 0))
     owner = lax.axis_index("dose")
     layout = image_layout(window)
@@ -430,7 +434,7 @@
                 back.put("m1", d, row, [v - a * (neutral_rate * s) for v, a, s in parts])
 
 
-def back_near_kernel(rows, window, local, near, far, extra_own, extra_par, cot, swap, *refs):
+def back_near_kernel(rows, window, local, group, near, far, extra_own, extra_par, cot, swap, *refs):
     doses, groups = window.doses, window.groups
     wholes, back_near = refs[:-1], refs[-1]
     half = rows // 2
@@ -442,8 +446,8 @@
     start = window.start(owner)
     image = image_layout(window)
     whole = whole_layout(rows, window, local)
-    for d in range(total):
-        past = Fields(rows, total, (near, near_rows), (far, far_rows))
+    for d in range(group * local, (group + 1) * local):
+        past = Fields(rows, (near, near_rows, 0, total), (far, far_rows, 0, total))
         rate = -exposure_rate * past.get("dose", d, 0)[0]
         light = [v for src in (extra_own, extra_par) for v in image.get(src, 0, owner)]
         past.more["a0", d, rows] = [1.0 - jnp.exp(rate * v) for v in light]
@@ -453,23 +457,24 @@
         for n, row in ((3, half + 2), (2, half + 1)):
             left = left_of(past.get("a%d" % (5 - n), d, row))
             past.more["c%d" % n, d, row] = [v * m for v, m in zip(past.get("c%d" % n, d, row), left)]
-        back = Fields(rows, total, (back_near, back_near_rows))
+        back = Fields(rows, (back_near, back_near_rows, group * local, local))
         table = back_near_rows(rows)
-        k, i = divmod(d, local)
+        i = d - group * local
         for row in range(*table["ct"]):
-            if k == 0:
+            if group == 0:
                 value = [vector(cot, rows, groups, start + g, chip_row(rows, row), i * area) for g in range(groups)]
                 value += swapped(swap, groups, 2 * rows + i * inner + row)
             else:
                 at = chip_row(rows, row) * window.layers(HALO_COT)
-                sides = (wholes[2 * k - 2], wholes[2 * k - 1])
+                sides = wholes
                 value = [v for src in sides for v in whole.get(src, i * rows, owner, at)]
             back.put("ct", d, row, value)
         backward_rows(spread, past, back, d, table)
 
 
-def back_far_kernel(rows, window, local, near, far, back_near, *refs):
+def back_far_kernel(rows, window, local, near, far, *refs):
     doses, groups = window.doses, window.groups
+    backs, refs = refs[:doses], refs[doses:]
     sends = refs[:doses]
     mine, other, store, full = refs[doses:]
     layouts = halo_layouts(window, local)
@@ -477,8 +482,9 @@
     total = local * doses
     owner = lax.axis_index("dose")
     spread = make_spread()
-    past = Fields(rows, total, (near, near_rows), (far, far_rows))
-    back = Fields(rows, total, (back_near, back_near_rows), (store, back_far_rows))
+    past = Fields(rows, (near, near_rows, 0, total), (far, far_rows, 0, total))
+    stores = [(ref, back_near_rows, k * local, local) for k, ref in enumerate(backs)]
+    back = Fields(rows, *stores, (store, back_far_rows, 0, total))
     table = back_far_rows(rows)
     for d in range(total):
         k, i = divmod(d, local)
@@ -542,8 +548,8 @@
     def array(*shape):
         return jax.ShapeDtypeStruct(shape + (lanes,), f32)
 
-    def store(table):
-        return (places_of(table(rows), total)[1], 2 * groups, SUB)
+    def store(table, count=total):
+        return (places_of(table(rows), count)[1], 2 * groups, SUB)
 
     def along(value, cross=0, step=1, k=0):
         pairs = []
@@ -587,12 +593,12 @@
     for k in range(1, doses):
         arrived = along(rest[doses + k], step=0, k=k)
         values.append(along(dose, step=0, k=k))
-        wholes += [arrived, across(arrived)]
+        wholes.append([arrived, across(arrived)])
     sends = []
     for k in range(doses):
         other = lax.slice_in_dim(swap, handed + k * halo, handed + (k + 1) * halo)
-        both = jnp.concatenate((other, rest[1 + k]) if k % 2 else (rest[1 + k], other), axis=0)
-        sends.append(along(both, cross=k % 2, k=k))
+        both = jnp.concatenate((other, rest[1 + k]) if crosses(k) else (rest[1 + k], other), axis=0)
+        sends.append(along(both, cross=int(crosses(k)), k=k))
 
     (near,) = call(
         near_kernel, (rows, window, local), values + [aerial, quench, swap], [array(*store(near_rows))], flops=10_000_000
@@ -602,17 +608,19 @@
     (far,) = call(
         far_kernel, (rows, window, total), (near, image_s, image_c), [array(*store(far_rows))], flops=10_000_000
     )
-    (back_near,) = call(
-        back_near_kernel,
-        (rows, window, local),
-        [near, far, extra_own, extra_par, cot, swap] + wholes,
-        [array(*store(back_near_rows))],
-        flops=10_000_000,
-    )
+    backs = []
+    for k in range(doses):
+        backs += call(
+            back_near_kernel,
+            (rows, window, local, k),
+            [near, far, extra_own, extra_par, cot, swap] + (wholes[k - 1] if k else []),
+            [array(*store(back_near_rows, local))],
+            flops=10_000_000,
+        )
     mine, other = call(
         back_far_kernel,
         (rows, window, local),
-        [near, far, back_near] + sends,
+        [near, far] + backs + sends,
         [array(half, piece)] * 2,
         [
             pltpu.VMEM(store(back_far_rows) + (lanes,), f32),

time: 23.5 us -> 24 us (1.021)
  waiting for transfers between devices: 3.06 us -> 4.24 us
  starting transfers between devices: 12.8 us -> 12.2 us
    ppermute x11, waiting for transfers between devices: 3.06 us -> 4.24 us  [along(): return lax.ppermute(value, ('tx', 'ty', 'dose'), pairs)]
    ppermute x11, starting transfers between devices: 12.8 us -> 12.2 us  [along(): return lax.ppermute(value, ('tx', 'ty', 'dose'), pairs)]
    pallas_call x7 -> x8, Pallas kernels: 7.37 us -> 7.31 us  [call(): pl.pallas_call(body, out_shape=tuple(outs), in_specs=[pl.BlockSpec(memory...]
  transfers between devices with their start and end apart: 11 -> 11, of which waited for: 3 -> 3; matrix products, arithmetic and copies ran while one was open for 0% -> 0% of each run, Pallas kernels for 19% -> 18%
where the time goes in v8:
time: 24 us; the launch traced here: 23.9 us
  starting transfers between devices  12.2 us (51%)
  Pallas kernels  7.31 us (30%)
  waiting for transfers between devices  4.24 us (18%)
    ppermute x11, starting transfers between devices, along(): return lax.ppermute(value, ('tx', 'ty', 'dose'), pairs)  12.2 us
    pallas_call x8, Pallas kernels, call(): pl.pallas_call(body, out_shape=tuple(outs), in_specs=[pl.BlockSpec(memory...  7.31 us
    ppermute x11, waiting for transfers between devices, along(): return lax.ppermute(value, ('tx', 'ty', 'dose'), pairs)  4.24 us
  transfers between devices with their start and end apart: 11, of which 3 were waited for; matrix products, arithmetic and copies ran while one was open for 0% of the time, Pallas kernels for 18%

profile of v8, /device:TPU:0, one launch (start us, length us, event | category | flops | bytes accessed | tf_op | source)
XLA Modules:
  0.0 23.9 jit_solution(5017884123327370746)
XLA Ops:
  0.0 1.1 %shard_map.55 = (f32[176,128]{1,0:T(8,128)S(1)}, f32[176,128]{1,0:T(8,128)S(1)}, f32[2,8,128]{2,1,0:T(8,128)S(1)}, f32[256,128]{1,0:T(8,128)S(1)}, f32[256,128]{1,0:T(8,128)S(1)}, /*index=5*/f32[512,128]{1,0:T(8,128)S(1)}) custom-call(f32[256,128]{1,0:T(8,128)} %bitcast.5, f32[256,128]{1,0:T(8,128)} %bitcast.6, f32[512,128]{1,0:T(8,128)} %bitcast.4, ...), custom_call_target="tpu_custom_call" | custom-call | bytes 1237064 | tf_op jit(solution)/shard_map/pallas_call | solution.py:538
  1.2 0.2 shard_map.56
  1.3 0.6 %collective-permute-start.1 = (f32[944,128]{1,0:T(8,128)S(1)}, f32[944,128]{1,0:T(8,128)S(1)}, u32[]{:S(2)}, u32[]{:S(2)}) collective-permute-start(f32[944,128]{1,0:T(8,128)S(1)} %get-tuple-element.21), channel_id=1, source_target_pairs={{0,2},{1,3},{2,0},{3,1},{4,6},{5,7},{6,4},{7,5},{8,10},{9,11},{10,... | collective-permute-start | bytes 1449992 | tf_op jit(solution)/shard_map/ppermute | solution.py:562
  1.9 2.6 %collective-permute-start.6 = (f32[320,128]{1,0:T(8,128)S(1)}, f32[320,128]{1,0:T(8,128)S(1)}, u32[]{:S(2)}, u32[]{:S(2)}) collective-permute-start(f32[320,128]{1,0:T(8,128)S(1)} %get-tuple-element.24), channel_id=1, source_target_pairs={{0,1},{1,0},{2,3},{3,2},{4,5},{5,4},{6,7},{7,6},{8,9},{9,8},{10,11... | collective-permute-start | bytes 491528 | tf_op jit(solution)/shard_map/ppermute | solution.py:562
  4.4 0.1 collective-permute-start
  4.5 2.0 %collective-permute-start.2 = (f32[176,128]{1,0:T(8,128)S(1)}, f32[176,128]{1,0:T(8,128)S(1)}, u32[]{:S(2)}, u32[]{:S(2)}) collective-permute-start(f32[176,128]{1,0:T(8,128)S(1)} %get-tuple-element.22), channel_id=1, source_target_pairs={{0,4},{1,5},{2,14},{3,15},{4,8},{5,9},{6,2},{7,3},{8,12},{9,13},{1... | collective-permute-start | bytes 270344 | tf_op jit(solution)/shard_map/ppermute | solution.py:562
  6.5 1.7 %collective-permute-start.3 = (f32[176,128]{1,0:T(8,128)S(1)}, f32[176,128]{1,0:T(8,128)S(1)}, u32[]{:S(2)}, u32[]{:S(2)}) collective-permute-start(f32[176,128]{1,0:T(8,128)S(1)} %get-tuple-element.23), channel_id=1, source_target_pairs={{0,14},{1,15},{2,4},{3,5},{4,2},{5,3},{6,8},{7,9},{8,6},{9,7},{10,... | collective-permute-start | bytes 270344 | tf_op jit(solution)/shard_map/ppermute | solution.py:562
  8.2 1.1 %collective-permute-done.6.refs_6_ = f32[320,128]{1,0:T(8,128)S(1)} collective-permute-done((f32[320,128]{1,0:T(8,128)S(1)}, f32[320,128]{1,0:T(8,128)S(1)}, u32[]{:S(2)}, u32[]{:S(2)}) %collective-permute-start.6) | collective-permute-done | bytes 163872 | tf_op jit(solution)/shard_map/ppermute | solution.py:562
  9.3 0.0 collective-permute-start.7
  9.3 0.0 collective-permute-done.1.refs_4_.refs_5_
  9.4 4.0 %collective-permute-start.8 = (f32[224,128]{1,0:T(8,128)S(1)}, f32[224,128]{1,0:T(8,128)S(1)}, u32[]{:S(2)}, u32[]{:S(2)}) collective-permute-start(f32[224,128]{1,0:T(8,128)S(1)} %pad_maximum_fusion), channel_id=1, source_target_pairs={{0,14},{1,15},{2,4},{3,5},{4,2},{5,3},{6,8},{7,9},{8,6},{9,7},{10,... | collective-permute-start | bytes 344072 | tf_op jit(solution)/shard_map/ppermute | solution.py:562
  13.4 0.0 collective-permute-done.refs_1_
  13.4 0.1 collective-permute-start.9
  13.5 0.0 collective-permute-done.3.refs_2_
  13.5 1.0 %collective-permute-start.4 = (f32[176,128]{1,0:T(8,128)S(1)}, f32[176,128]{1,0:T(8,128)S(1)}, u32[]{:S(2)}, u32[]{:S(2)}) collective-permute-start(f32[176,128]{1,0:T(8,128)S(1)} %collective-permute-done.3.refs_2_), channel_id=1, source_target_pairs={{0,2},{1,3},{2,0},{3,1},{4,6},{5,7},{6,4},{7,5},{8,10},{9,11},{10,... | collective-permute-start | bytes 270344 | tf_op jit(solution)/shard_map/ppermute | solution.py:562
  14.5 0.0 collective-permute-done.2.refs_1_
  14.5 0.1 collective-permute-start.5
  14.6 1.5 %shard_map.57.refs_0_ = f32[192,6,8,128]{3,2,1,0:T(8,128)S(1)} custom-call(f32[2,8,128]{2,1,0:T(8,128)S(1)} %get-tuple-element.17.refs_0_, f32[2,8,128]{2,1,0:T(8,128)S(1)} %collective-permute-done.refs_1_, f32[256,128]{1,0:T(8,128)S(1)} %get-tuple-element.18.refs_0_.refs_2_, f32[256,128]{1,0:T(8,128)S(1)} %get-tuple-element.19.refs_1_.refs_3_, ...), custom_call_target="tpu_custom_call" | custom-call | flops 10000000 | bytes 5480448 | tf_op jit(solution)/shard_map/pallas_call | solution.py:538
  16.1 1.5 %shard_map.58.refs_1_ = f32[184,6,8,128]{3,2,1,0:T(8,128)S(1)} custom-call(f32[192,6,8,128]{3,2,1,0:T(8,128)S(1)} %shard_map.57.refs_0_, f32[176,128]{1,0:T(8,128)S(1)} %collective-permute-done.2.refs_1_, f32[176,128]{1,0:T(8,128)S(1)} %collective-permute-done.3.refs_2_), custom_call_target="tpu_custom_call" | custom-call | flops 10000000 | bytes 9420800 | tf_op jit(solution)/shard_map/pallas_call | solution.py:538
  17.6 0.0 collective-permute-done.4.refs_2_
  17.7 0.0 collective-permute-done.5.refs_3_
  17.7 0.7 %shard_map.59.refs_2_ = f32[62,6,8,128]{3,2,1,0:T(8,128)S(1)} custom-call(f32[192,6,8,128]{3,2,1,0:T(8,128)S(1)} %shard_map.57.refs_0_, f32[184,6,8,128]{3,2,1,0:T(8,128)S(1)} %shard_map.58.refs_1_, f32[176,128]{1,0:T(8,128)S(1)} %collective-permute-done.4.refs_2_, f32[176,128]{1,0:T(8,128)S(1)} %collective-permute-done.5.refs_3_, ...), custom_call_target="tpu_custom_call" | custom-call | flops 10000000 | bytes 11689984 | tf_op jit(solution)/shard_map/pallas_call | solution.py:538
  18.3 0.0 collective-permute-done.7.refs_7_
  18.3 0.7 %shard_map.60.refs_3_ = f32[62,6,8,128]{3,2,1,0:T(8,128)S(1)} custom-call(f32[192,6,8,128]{3,2,1,0:T(8,128)S(1)} %shard_map.57.refs_0_, f32[184,6,8,128]{3,2,1,0:T(8,128)S(1)} %shard_map.58.refs_1_, f32[176,128]{1,0:T(8,128)S(1)} %collective-permute-done.4.refs_2_, f32[176,128]{1,0:T(8,128)S(1)} %collective-permute-done.5.refs_3_, ...), custom_call_target="tpu_custom_call" | custom-call | flops 10000000 | bytes 12017664 | tf_op jit(solution)/shard_map/pallas_call | solution.py:538
  19.0 0.0 collective-permute-done.8.refs_4_
  19.0 1.9 %collective-permute-done.9.refs_5_ = f32[224,128]{1,0:T(8,128)S(1)} collective-permute-done((f32[224,128]{1,0:T(8,128)S(1)}, f32[224,128]{1,0:T(8,128)S(1)}, u32[]{:S(2)}, u32[]{:S(2)}) %collective-permute-start.9) | collective-permute-done | bytes 114720 | tf_op jit(solution)/shard_map/ppermute | solution.py:562
  20.9 1.0 %shard_map.61 = (f32[4,16,128]{2,1,0:T(8,128)S(1)}, f32[4,16,128]{2,1,0:T(8,128)S(1)}) custom-call(f32[192,6,8,128]{3,2,1,0:T(8,128)S(1)} %shard_map.57.refs_0_, f32[184,6,8,128]{3,2,1,0:T(8,128)S(1)} %shard_map.58.refs_1_, f32[62,6,8,128]{3,2,1,0:T(8,128)S(1)} %shard_map.59.refs_2_, f32[62,6,8,128]{3,2,1,0:T(8,128)S(1)} %shard_map.60.refs_3_, ...), custom_call_target="tpu_custom_call" | custom-call | flops 10000000 | bytes 12582912 | tf_op jit(solution)/shard_map/pallas_call | solution.py:538
  22.0 0.1 collective-permute-start.10
  22.0 1.2 %collective-permute-done.10.refs_1_ = f32[4,16,128]{2,1,0:T(8,128)S(1)} collective-permute-done((f32[4,16,128]{2,1,0:T(8,128)S(1)}, f32[4,16,128]{2,1,0:T(8,128)S(1)}, u32[]{:S(2)}, u32[]{:S(2)}) %collective-permute-start.10) | collective-permute-done | bytes 32800 | tf_op jit(solution)/shard_map/ppermute | solution.py:562
  23.2 0.6 %shard_map.62 = f32[128,128]{1,0:T(8,128)} custom-call(f32[4,16,128]{2,1,0:T(8,128)S(1)} %get-tuple-element.27.refs_0_, f32[4,16,128]{2,1,0:T(8,128)S(1)} %collective-permute-done.10.refs_1_), custom_call_target="tpu_custom_call" | custom-call | bytes 131072 | tf_op jit(solution)/shard_map/pallas_call | solution.py:538
  (3 shorter events, 0.0 us)
Async XLA Ops:
  1.3 8.0 %collective-permute-start.1 = (f32[944,128]{1,0:T(8,128)S(1)}, f32[944,128]{1,0:T(8,128)S(1)}, u32[]{:S(2)}, u32[]{:S(2)}) collective-permute-start(f32[944,128]{1,0:T(8,128)S(1)} %get-tuple-element.21), channel_id=1, source_target_pairs={{0,2},{1,3},{2,0},{3,1},{4,6},{5,7},{6,4},{7,5},{8,10},{9,11},{10,... | collective-permute-start | bytes 1449992 | tf_op jit(solution)/shard_map/ppermute | solution.py:562
  1.9 7.4 %collective-permute-start.6 = (f32[320,128]{1,0:T(8,128)S(1)}, f32[320,128]{1,0:T(8,128)S(1)}, u32[]{:S(2)}, u32[]{:S(2)}) collective-permute-start(f32[320,128]{1,0:T(8,128)S(1)} %get-tuple-element.24), channel_id=1, source_target_pairs={{0,1},{1,0},{2,3},{3,2},{4,5},{5,4},{6,7},{7,6},{8,9},{9,8},{10,11... | collective-permute-start | bytes 491528 | tf_op jit(solution)/shard_map/ppermute | solution.py:562
  4.4 9.0 %collective-permute-start = (f32[2,8,128]{2,1,0:T(8,128)S(1)}, f32[2,8,128]{2,1,0:T(8,128)S(1)}, u32[]{:S(2)}, u32[]{:S(2)}) collective-permute-start(f32[2,8,128]{2,1,0:T(8,128)S(1)} %get-tuple-element.17.refs_0_), channel_id=1, source_target_pairs={{0,1},{1,0},{2,3},{3,2},{4,5},{5,4},{6,7},{7,6},{8,9},{9,8},{10,11... | collective-permute-start | bytes 24584 | tf_op jit(solution)/shard_map/ppermute | solution.py:562
  4.5 10.0 %collective-permute-start.2 = (f32[176,128]{1,0:T(8,128)S(1)}, f32[176,128]{1,0:T(8,128)S(1)}, u32[]{:S(2)}, u32[]{:S(2)}) collective-permute-start(f32[176,128]{1,0:T(8,128)S(1)} %get-tuple-element.22), channel_id=1, source_target_pairs={{0,4},{1,5},{2,14},{3,15},{4,8},{5,9},{6,2},{7,3},{8,12},{9,13},{1... | collective-permute-start | bytes 270344 | tf_op jit(solution)/shard_map/ppermute | solution.py:562
  6.5 6.9 %collective-permute-start.3 = (f32[176,128]{1,0:T(8,128)S(1)}, f32[176,128]{1,0:T(8,128)S(1)}, u32[]{:S(2)}, u32[]{:S(2)}) collective-permute-start(f32[176,128]{1,0:T(8,128)S(1)} %get-tuple-element.23), channel_id=1, source_target_pairs={{0,14},{1,15},{2,4},{3,5},{4,2},{5,3},{6,8},{7,9},{8,6},{9,7},{10,... | collective-permute-start | bytes 270344 | tf_op jit(solution)/shard_map/ppermute | solution.py:562
  9.3 9.0 %collective-permute-start.7 = (f32[320,128]{1,0:T(8,128)S(1)}, f32[320,128]{1,0:T(8,128)S(1)}, u32[]{:S(2)}, u32[]{:S(2)}) collective-permute-start(f32[320,128]{1,0:T(8,128)S(1)} %collective-permute-done.6.refs_6_), channel_id=1, source_target_pairs={{0,2},{1,3},{2,0},{3,1},{4,6},{5,7},{6,4},{7,5},{8,10},{9,11},{10,... | collective-permute-start | bytes 491528 | tf_op jit(solution)/shard_map/ppermute | solution.py:562
  9.4 9.7 %collective-permute-start.8 = (f32[224,128]{1,0:T(8,128)S(1)}, f32[224,128]{1,0:T(8,128)S(1)}, u32[]{:S(2)}, u32[]{:S(2)}) collective-permute-start(f32[224,128]{1,0:T(8,128)S(1)} %pad_maximum_fusion), channel_id=1, source_target_pairs={{0,14},{1,15},{2,4},{3,5},{4,2},{5,3},{6,8},{7,9},{8,6},{9,7},{10,... | collective-permute-start | bytes 344072 | tf_op jit(solution)/shard_map/ppermute | solution.py:562
  13.4 7.5 %collective-permute-start.9 = (f32[224,128]{1,0:T(8,128)S(1)}, f32[224,128]{1,0:T(8,128)S(1)}, u32[]{:S(2)}, u32[]{:S(2)}) collective-permute-start(f32[224,128]{1,0:T(8,128)S(1)} %pad_maximum_fusion.1), channel_id=1, source_target_pairs={{0,5},{1,4},{2,15},{3,14},{4,9},{5,8},{6,3},{7,2},{8,13},{9,12},{1... | collective-permute-start | bytes 344072 | tf_op jit(solution)/shard_map/ppermute | solution.py:562
  13.5 4.2 %collective-permute-start.4 = (f32[176,128]{1,0:T(8,128)S(1)}, f32[176,128]{1,0:T(8,128)S(1)}, u32[]{:S(2)}, u32[]{:S(2)}) collective-permute-start(f32[176,128]{1,0:T(8,128)S(1)} %collective-permute-done.3.refs_2_), channel_id=1, source_target_pairs={{0,2},{1,3},{2,0},{3,1},{4,6},{5,7},{6,4},{7,5},{8,10},{9,11},{10,... | collective-permute-start | bytes 270344 | tf_op jit(solution)/shard_map/ppermute | solution.py:562
  14.5 3.1 %collective-permute-start.5 = (f32[176,128]{1,0:T(8,128)S(1)}, f32[176,128]{1,0:T(8,128)S(1)}, u32[]{:S(2)}, u32[]{:S(2)}) collective-permute-start(f32[176,128]{1,0:T(8,128)S(1)} %collective-permute-done.2.refs_1_), channel_id=1, source_target_pairs={{0,2},{1,3},{2,0},{3,1},{4,6},{5,7},{6,4},{7,5},{8,10},{9,11},{10,... | collective-permute-start | bytes 270344 | tf_op jit(solution)/shard_map/ppermute | solution.py:562
  22.0 1.3 %collective-permute-start.10 = (f32[4,16,128]{2,1,0:T(8,128)S(1)}, f32[4,16,128]{2,1,0:T(8,128)S(1)}, u32[]{:S(2)}, u32[]{:S(2)}) collective-permute-start(f32[4,16,128]{2,1,0:T(8,128)S(1)} %get-tuple-element.28), channel_id=1, source_target_pairs={{0,2},{1,3},{2,0},{3,1},{4,6},{5,7},{6,4},{7,5},{8,10},{9,11},{10,... | collective-permute-start | bytes 98312 | tf_op jit(solution)/shard_map/ppermute | solution.py:562
